TPU v7x, 32 devices: a whole 2x2x4 slice. The times are simulated.
32 devices in a mesh: dp: 8 (over z, x), tensor: 4 (over y, core).
Axes of the slice: x: 2, y: 2, z: 4, core: 2. Of those that a mesh axis runs over, the one named last changes fastest.
Arguments:
- block_input: bfloat16 [16384, 768], P(('dp', 'tensor')), may hold values from -6 to 6
- output_grad: bfloat16 [16384, 768], P(('dp', 'tensor')), may hold values from -6 to 6
- lengths: int32 [8], P('dp'), may hold values from 1024 to 2048, as said below
- in_proj: float32 [768, 2, 1536], P('dp', None, 'tensor'), may hold values from -0.21875 to 0.21875
- step_proj: float32 [768, 24], P('dp', 'tensor'), may hold values from -0.21875 to 0.21875
- out_proj: float32 [768, 1536], P('dp', 'tensor'), may hold values from -0.15625 to 0.15625
- channel_params: float32 [6, 1536], P(None, 'tensor'), may hold values from -0.6 to 1.5
- head_params: float32 [3, 24], P(None, 'tensor'), may hold values from -6 to 2.31
- state_proj: float32 [768, 256], P(('dp', 'tensor')), may hold values from -0.21875 to 0.21875
- state_conv: float32 [256, 5], P(('dp', 'tensor')), may hold values from -0.5 to 0.5
- norm_gain: float32 [768], P(('dp', 'tensor')), may hold values from 0.5 to 1.5
- first_in_proj: float32 [768, 2, 1536], P('dp', None, 'tensor'), may hold values from -1200 to 1200
- first_step_proj: float32 [768, 24], P('dp', 'tensor'), may hold values from -1200 to 1200
- first_out_proj: float32 [768, 1536], P('dp', 'tensor'), may hold values from -1200 to 1200
- first_channel_params: float32 [6, 1536], P(None, 'tensor'), may hold values from -1200 to 1200
- first_head_params: float32 [3, 24], P(None, 'tensor'), may hold values from -1200 to 1200
- first_state_proj: float32 [768, 256], P(('dp', 'tensor')), may hold values from -1200 to 1200
- first_state_conv: float32 [256, 5], P(('dp', 'tensor')), may hold values from -1200 to 1200
- first_norm_gain: float32 [768], P(('dp', 'tensor')), may hold values from -1200 to 1200
- second_in_proj: float32 [768, 2, 1536], P('dp', None, 'tensor'), may hold values from 1000 to 100000
- second_step_proj: float32 [768, 24], P('dp', 'tensor'), may hold values from 1000 to 100000
- second_out_proj: float32 [768, 1536], P('dp', 'tensor'), may hold values from 1000 to 100000
- second_channel_params: float32 [6, 1536], P(None, 'tensor'), may hold values from 1000 to 100000
- second_head_params: float32 [3, 24], P(None, 'tensor'), may hold values from 1000 to 100000
- second_state_proj: float32 [768, 256], P(('dp', 'tensor')), may hold values from 1000 to 100000
- second_state_conv: float32 [256, 5], P(('dp', 'tensor')), may hold values from 1000 to 100000
- second_norm_gain: float32 [768], P(('dp', 'tensor')), may hold values from 1000 to 100000
Outputs:
- output: bfloat16 [16384, 768], P(('dp', 'tensor'))
- input_grad: float32 [16384, 768], P(('dp', 'tensor'))
- grad_in_proj: float32 [768, 2, 1536], P('dp', None, 'tensor')
- grad_step_proj: float32 [768, 24], P('dp', 'tensor')
- grad_out_proj: float32 [768, 1536], P('dp', 'tensor')
- grad_channel_params: float32 [6, 1536], P(None, 'tensor')
- grad_head_params: float32 [3, 24], P(None, 'tensor')
- grad_state_proj: float32 [768, 256], P(('dp', 'tensor'))
- grad_state_conv: float32 [256, 5], P(('dp', 'tensor'))
- grad_norm_gain: float32 [768], P(('dp', 'tensor'))
- new_first_in_proj: float32 [768, 2, 1536], P('dp', None, 'tensor')
- new_first_step_proj: float32 [768, 24], P('dp', 'tensor')
- new_first_out_proj: float32 [768, 1536], P('dp', 'tensor')
- new_first_channel_params: float32 [6, 1536], P(None, 'tensor')
- new_first_head_params: float32 [3, 24], P(None, 'tensor')
- new_first_state_proj: float32 [768, 256], P(('dp', 'tensor'))
- new_first_state_conv: float32 [256, 5], P(('dp', 'tensor'))
- new_first_norm_gain: float32 [768], P(('dp', 'tensor'))
- new_second_in_proj: float32 [768, 2, 1536], P('dp', None, 'tensor')
- new_second_step_proj: float32 [768, 24], P('dp', 'tensor')
- new_second_out_proj: float32 [768, 1536], P('dp', 'tensor')
- new_second_channel_params: float32 [6, 1536], P(None, 'tensor')
- new_second_head_params: float32 [3, 24], P(None, 'tensor')
- new_second_state_proj: float32 [768, 256], P(('dp', 'tensor'))
- new_second_state_conv: float32 [256, 5], P(('dp', 'tensor'))
- new_second_norm_gain: float32 [768], P(('dp', 'tensor'))
- update_in_proj: float32 [768, 2, 1536], P('dp', None, 'tensor')
- update_step_proj: float32 [768, 24], P('dp', 'tensor')
- update_out_proj: float32 [768, 1536], P('dp', 'tensor')
- update_channel_params: float32 [6, 1536], P(None, 'tensor')
- update_head_params: float32 [3, 24], P(None, 'tensor')
- update_state_proj: float32 [768, 256], P(('dp', 'tensor'))
- update_state_conv: float32 [256, 5], P(('dp', 'tensor'))
- update_norm_gain: float32 [768], P(('dp', 'tensor'))
- lamb_norms: float32 [2, 8], replicated
Inputs may be any that keep to these rules, and one draw needn't show every extreme that they name: `lengths`: some sequence has exactly 2048 live positions.
All inputs are finite; a program needn't handle non-finite values.
Results may differ from a plain program's by a relative error of at most 0.012.
The roundings to bfloat16 on the way count: a program that leaves them out, or rounds other values in their place, can miss the bound.
Values may be sent and summed in bfloat16 or wider, within the bound.
No kernel may reach another device: no remote copies, remote signals or barrier semaphores. Data moves between devices by JAX's collectives and lax.ppermute only.
A program may use at most 192 MiB of HBM per device.

v0:
```python
import jax
import jax.numpy as jnp
from jax import lax
from jax.sharding import PartitionSpec as P

STATE = 128
CONV = 4
SPAN = 256
LMAX = 2048
INNER = 1536


EPSILON = 1e-05
ADAM_EPSILON = 1e-06
DECAY = 0.5
BIAS_FIRST = 0.875
BIAS_SECOND = 0.875
RATE = 0.3
WEIGHT_DECAY = 0.01
HIGHEST = lax.Precision.HIGHEST


def rounded(values):
    return lax.optimization_barrier(values.astype(jnp.bfloat16)).astype(jnp.float32)


def contract(left, right, left_dim, right_dim):
    return lax.dot_general(
        left, right, (((left_dim,), (right_dim,)), ((), ())), preferred_element_type=jnp.float32
    )


def causal_conv(values, kernel, offsets):
    padded = jnp.pad(values, ((kernel.shape[0] - 1, 0), (0, 0)))
    summed = offsets[None, :] + jnp.zeros_like(values)
    for offset in range(kernel.shape[0]):
        summed = summed + kernel[offset][None, :] * padded[offset : offset + values.shape[0]]
    return jax.nn.silu(summed)


def ssd_scan(signal, b_rows, c_rows, step_size, log_rate):
    length, head_count, head_width = signal.shape
    blocks = length // SPAN
    decay_log = -jnp.exp(log_rate)[None, :] * step_size
    x_blocks = signal.reshape(blocks, SPAN, head_count, head_width)
    dt_blocks = step_size.reshape(blocks, SPAN, head_count)
    b_blocks = b_rows.reshape(blocks, SPAN, -1)
    c_blocks = c_rows.reshape(blocks, SPAN, -1)
    cumulative = jnp.cumsum(decay_log.reshape(blocks, SPAN, head_count), axis=1)
    intersection = jnp.einsum("cqn,ckn->cqk", c_blocks, b_blocks, precision=HIGHEST)
    causal = jnp.arange(SPAN)[:, None] >= jnp.arange(SPAN)[None, :]
    spread = cumulative[:, :, None, :] - cumulative[:, None, :, :]
    damping = jnp.exp(jnp.where(causal[None, :, :, None], spread, -jnp.inf))
    mixing = intersection[:, :, :, None] * damping * dt_blocks[:, None, :, :]
    within = jnp.einsum("cqkh,ckhp->cqhp", mixing, x_blocks, precision=HIGHEST)
    closing = cumulative[:, -1, :]
    weights_end = jnp.exp(closing[:, None, :] - cumulative) * dt_blocks
    states = jnp.einsum("ckh,ckhp,ckn->chpn", weights_end, x_blocks, b_blocks, precision=HIGHEST)

    def carry_step(carried, element):
        state_new, closing_new = element
        return (jnp.exp(closing_new)[:, None, None] * carried + state_new, carried)

    initial = jnp.zeros(states.shape[1:], jnp.float32)
    unused, entering = lax.scan(carry_step, initial, (states, closing))
    across = (
        jnp.einsum("cqn,chpn->cqhp", c_blocks, entering, precision=HIGHEST)
        * jnp.exp(cumulative)[..., None]
    )
    return (within + across).reshape(length, head_count, head_width)


def gate_mix(signal, b_rows, c_rows, step_raw, gate_raw, head_local):
    length = signal.shape[0]
    head_count = head_local.shape[1]
    step_size = jax.nn.softplus(step_raw + head_local[1][None, :])
    shaped = signal.reshape(length, head_count, -1)
    mixed = (
        ssd_scan(shaped, b_rows, c_rows, step_size, head_local[0])
        + head_local[2][None, :, None] * shaped
    )
    return mixed.reshape(length, -1) * jax.nn.silu(gate_raw)


def gate_blocks(signal, b_rows, c_rows, step_raw, gate_raw, head_local):

    def one_sequence(element):
        return gate_mix(element[0], element[1], element[2], element[3], element[4], head_local)

    return lax.map(one_sequence, (signal, b_rows, c_rows, step_raw, gate_raw))


def conv_signal(values, params):
    return jax.vmap(causal_conv, (0, None, None))(values, params[:CONV], params[CONV])


def conv_state(values, params):
    return jax.vmap(causal_conv, (0, None, None))(values, params[:, :CONV].T, params[:, CONV])


def lamb_parts(weight, gradient, first_old, second_old):
    first_new = DECAY * first_old + (1.0 - DECAY) * gradient
    second_new = DECAY * second_old + (1.0 - DECAY) * gradient * gradient
    direction = (
        first_new / BIAS_FIRST / (jnp.sqrt(second_new / BIAS_SECOND) + ADAM_EPSILON)
        + WEIGHT_DECAY * weight
    )
    return (first_new, second_new, direction)


def local(
    block_input,
    output_grad,
    lengths,
    in_proj,
    step_proj,
    out_proj,
    channel_params,
    head_params,
    state_proj,
    state_conv,
    norm_gain,
    first_in_proj,
    first_step_proj,
    first_out_proj,
    first_channel_params,
    first_head_params,
    first_state_proj,
    first_state_conv,
    first_norm_gain,
    second_in_proj,
    second_step_proj,
    second_out_proj,
    second_channel_params,
    second_head_params,
    second_state_proj,
    second_state_conv,
    second_norm_gain,
):
    tensor_count = lax.axis_size("tensor")
    own_count = block_input.shape[0]
    group_count = own_count * tensor_count
    sequence_count = lengths.shape[0]
    by_sequence = (sequence_count, LMAX, -1)
    inputs = block_input.astype(jnp.float32)
    shared = (
        lax.all_gather(state_proj, ("dp", "tensor"), axis=0, tiled=True),
        lax.all_gather(state_conv, ("dp", "tensor"), axis=0, tiled=True),
        lax.all_gather(norm_gain, ("dp", "tensor"), axis=0, tiled=True),
    )
    state_weight = shared[0].astype(jnp.bfloat16)
    conv_whole = shared[1]
    gain_whole = shared[2]
    in_weight, step_weight, out_weight = (
        lax.all_gather(in_proj.astype(jnp.bfloat16), "dp", axis=0, tiled=True),
        lax.all_gather(step_proj.astype(jnp.bfloat16), "dp", axis=0, tiled=True),
        lax.all_gather(out_proj.astype(jnp.bfloat16), "dp", axis=0, tiled=True),
    )
    scale = lax.rsqrt(jnp.mean(inputs * inputs, axis=-1, keepdims=True) + EPSILON)
    normed_own = (inputs * scale * gain_whole[None, :]).astype(jnp.bfloat16)
    normed = lax.all_gather(normed_own, "tensor", axis=0, tiled=True)
    gate_raw = contract(normed, in_weight[:, 0, :], 1, 0)
    signal_raw = contract(normed, in_weight[:, 1, :], 1, 0)
    state_raw = contract(normed, state_weight, 1, 0)
    step_raw = contract(normed, step_weight, 1, 0)
    signal_act, signal_back = jax.vjp(
        conv_signal, signal_raw.reshape(by_sequence), channel_params[: CONV + 1]
    )
    state_act, state_back = jax.vjp(conv_state, state_raw.reshape(by_sequence), conv_whole)
    signal = rounded(signal_act)
    b_rows = rounded(state_act[:, :, :STATE])
    c_rows = rounded(state_act[:, :, STATE:])
    mixer_inputs = (
        signal,
        b_rows,
        c_rows,
        step_raw.reshape(by_sequence),
        gate_raw.reshape(by_sequence),
        head_params,
    )
    gated, mixer_back = jax.vjp(gate_blocks, *mixer_inputs)
    squares = lax.psum(jnp.sum(gated * gated, axis=-1), "tensor")
    gate_scale = lax.rsqrt(squares / INNER + EPSILON)[:, :, None]
    gate_gain = channel_params[CONV + 1]
    normalized = gated * gate_scale
    merged = (normalized * gate_gain).astype(jnp.bfloat16).reshape(group_count, -1)
    branch = lax.psum_scatter(
        contract(merged, out_weight, 1, 1), "tensor", scatter_dimension=0, tiled=True
    )
    position_all = lax.axis_index("tensor") * own_count + jnp.arange(own_count, dtype=jnp.int32)
    sequence_of = position_all // LMAX
    length_of = jnp.sum(
        jnp.where(
            sequence_of[:, None] == jnp.arange(sequence_count, dtype=jnp.int32)[None, :],
            lengths[None, :],
            0,
        ),
        axis=1,
    )
    live_own = (position_all % LMAX < length_of).astype(jnp.float32)[:, None]
    output = (inputs + branch * live_own).astype(jnp.bfloat16)
    masked_grad = jnp.where(live_own > 0.5, output_grad, jnp.zeros_like(output_grad))
    grad_rows = lax.all_gather(masked_grad, "tensor", axis=0, tiled=True)
    in_back, step_back, out_back = (
        lax.all_gather(in_proj.astype(jnp.bfloat16), "dp", axis=0, tiled=True),
        lax.all_gather(step_proj.astype(jnp.bfloat16), "dp", axis=0, tiled=True),
        lax.all_gather(out_proj.astype(jnp.bfloat16), "dp", axis=0, tiled=True),
    )
    merged_grad = contract(grad_rows, out_back, 1, 0).reshape(by_sequence)
    out_grad = contract(grad_rows, merged, 0, 0)
    weighted = merged_grad * gate_gain
    gain_grad = jnp.sum(merged_grad * normalized, axis=(0, 1))
    products = lax.psum(jnp.sum(weighted * gated, axis=-1), "tensor")
    gated_grad = gate_scale * weighted - gated * gate_scale**3 * (products / INNER)[:, :, None]
    signal_grad, b_grad, c_grad, step_grad, gate_grad, head_grad = mixer_back(gated_grad)
    signal_raw_grad, kernel_grad = signal_back(signal_grad)
    state_raw_grad, conv_grad = state_back(jnp.concatenate([b_grad, c_grad], axis=-1))
    gate_low = gate_grad.reshape(group_count, -1).astype(jnp.bfloat16)
    signal_low = signal_raw_grad.reshape(group_count, -1).astype(jnp.bfloat16)
    step_low = step_grad.reshape(group_count, -1).astype(jnp.bfloat16)
    in_grad = jnp.stack(
        [contract(normed, gate_low, 0, 0), contract(normed, signal_low, 0, 0)], axis=1
    )
    step_weight_grad = contract(normed, step_low, 0, 0)
    normed_part = (
        contract(gate_low, in_back[:, 0, :], 1, 1)
        + contract(signal_low, in_back[:, 1, :], 1, 1)
        + contract(step_low, step_back, 1, 1)
    )
    normed_sum, state_sum = (
        lax.psum_scatter(normed_part, "tensor", scatter_dimension=0, tiled=True),
        lax.psum_scatter(
            state_raw_grad.reshape(group_count, -1), "tensor", scatter_dimension=0, tiled=True
        ),
    )
    state_low = state_sum.astype(jnp.bfloat16)
    normed_grad = normed_sum + contract(state_low, state_weight, 1, 1)
    state_weight_grad = contract(normed_own, state_low, 0, 0)
    gain_in_grad = jnp.sum(normed_grad * inputs * scale, axis=0)
    scaled_grad = normed_grad * gain_whole[None, :]
    input_grad = (
        output_grad.astype(jnp.float32)
        + scale * scaled_grad
        - inputs * scale**3 * jnp.mean(scaled_grad * inputs, axis=-1, keepdims=True)
    )
    channel_grad = jnp.concatenate([kernel_grad, gain_grad[None, :]], axis=0)
    in_sum, step_sum, out_sum = (
        lax.psum_scatter(in_grad, "dp", scatter_dimension=0, tiled=True),
        lax.psum_scatter(step_weight_grad, "dp", scatter_dimension=0, tiled=True),
        lax.psum_scatter(out_grad, "dp", scatter_dimension=0, tiled=True),
    )
    channel_sum, head_sum = lax.psum((channel_grad, head_grad), "dp")
    state_proj_sum, state_conv_sum, gain_sum = (
        lax.psum_scatter(state_weight_grad, ("dp", "tensor"), scatter_dimension=0, tiled=True),
        lax.psum_scatter(conv_grad, ("dp", "tensor"), scatter_dimension=0, tiled=True),
        lax.psum_scatter(gain_in_grad, ("dp", "tensor"), scatter_dimension=0, tiled=True),
    )
    masters = (
        in_proj,
        step_proj,
        out_proj,
        channel_params,
        head_params,
        state_proj,
        state_conv,
        norm_gain,
    )
    gradients = (
        in_sum,
        step_sum,
        out_sum,
        channel_sum,
        head_sum,
        state_proj_sum,
        state_conv_sum,
        gain_sum,
    )
    firsts = (
        first_in_proj,
        first_step_proj,
        first_out_proj,
        first_channel_params,
        first_head_params,
        first_state_proj,
        first_state_conv,
        first_norm_gain,
    )
    seconds = (
        second_in_proj,
        second_step_proj,
        second_out_proj,
        second_channel_params,
        second_head_params,
        second_state_proj,
        second_state_conv,
        second_norm_gain,
    )
    dp_copies = float(lax.axis_size("dp"))
    copies = (1.0, 1.0, 1.0, dp_copies, dp_copies, 1.0, 1.0, 1.0)
    first_list = []
    second_list = []
    directions = []
    partials = []
    for weight, gradient, first_old, second_old, copy_count in zip(
        masters, gradients, firsts, seconds, copies
    ):
        first_new, second_new, direction = lamb_parts(weight, gradient, first_old, second_old)
        first_list.append(first_new)
        second_list.append(second_new)
        directions.append(direction)
        partials.append(
            jnp.stack(
                [jnp.sum(weight * weight) / copy_count, jnp.sum(direction * direction) / copy_count]
            )
        )
    norm_totals = lax.psum(jnp.stack(partials, axis=1), ("dp", "tensor"))
    lamb_norms = jnp.sqrt(norm_totals)
    update_list = [
        -RATE * lamb_norms[0, position] / lamb_norms[1, position] * directions[position]
        for position in range(8)
    ]
    return (
        output,
        input_grad,
        in_sum,
        step_sum,
        out_sum,
        channel_sum,
        head_sum,
        state_proj_sum,
        state_conv_sum,
        gain_sum,
        first_list[0],
        first_list[1],
        first_list[2],
        first_list[3],
        first_list[4],
        first_list[5],
        first_list[6],
        first_list[7],
        second_list[0],
        second_list[1],
        second_list[2],
        second_list[3],
        second_list[4],
        second_list[5],
        second_list[6],
        second_list[7],
        update_list[0],
        update_list[1],
        update_list[2],
        update_list[3],
        update_list[4],
        update_list[5],
        update_list[6],
        update_list[7],
        lamb_norms,
    )


def solution(mesh):
    placed = (
        P(("dp", "tensor"), None),
        P(("dp", "tensor"), None),
        P("dp"),
        P("dp", None, "tensor"),
        P("dp", "tensor"),
        P("dp", "tensor"),
        P(None, "tensor"),
        P(None, "tensor"),
        P(("dp", "tensor"), None),
        P(("dp", "tensor"), None),
        P(("dp", "tensor")),
        P("dp", None, "tensor"),
        P("dp", "tensor"),
        P("dp", "tensor"),
        P(None, "tensor"),
        P(None, "tensor"),
        P(("dp", "tensor"), None),
        P(("dp", "tensor"), None),
        P(("dp", "tensor")),
        P("dp", None, "tensor"),
        P("dp", "tensor"),
        P("dp", "tensor"),
        P(None, "tensor"),
        P(None, "tensor"),
        P(("dp", "tensor"), None),
        P(("dp", "tensor"), None),
        P(("dp", "tensor")),
    )
    return jax.shard_map(
        local,
        mesh=mesh,
        in_specs=placed,
        out_specs=(
            P(("dp", "tensor"), None),
            P(("dp", "tensor"), None),
            P("dp", None, "tensor"),
            P("dp", "tensor"),
            P("dp", "tensor"),
            P(None, "tensor"),
            P(None, "tensor"),
            P(("dp", "tensor"), None),
            P(("dp", "tensor"), None),
            P(("dp", "tensor")),
            P("dp", None, "tensor"),
            P("dp", "tensor"),
            P("dp", "tensor"),
            P(None, "tensor"),
            P(None, "tensor"),
            P(("dp", "tensor"), None),
            P(("dp", "tensor"), None),
            P(("dp", "tensor")),
            P("dp", None, "tensor"),
            P("dp", "tensor"),
            P("dp", "tensor"),
            P(None, "tensor"),
            P(None, "tensor"),
            P(("dp", "tensor"), None),
            P(("dp", "tensor"), None),
            P(("dp", "tensor")),
            P("dp", None, "tensor"),
            P("dp", "tensor"),
            P("dp", "tensor"),
            P(None, "tensor"),
            P(None, "tensor"),
            P(("dp", "tensor"), None),
            P(("dp", "tensor"), None),
            P(("dp", "tensor")),
            P(),
        ),
        check_vma=False,
    )
```

profile of v0, /device:TPU:0, one launch (start us, length us, event | category | flops | bytes accessed | tf_op | source)
XLA Modules:
  0.0 971.0 jit_solution(7439061539372715546)
XLA Ops:
  8.2 42.0 %all-reduce.26 = f32[768]{0:T(1024)S(1)} all-reduce(f32[768]{0:T(1024)S(1)} %dynamic-update-slice), channel_id=1, replica_groups=mesh['dp'=8,'tensor'=4] {'dp','tensor'}, use_global_device_ids=true, to_apply=%add.26 | all-reduce | flops 768 | bytes 6144
  57.8 40.9 %all_gather.27 = f32[256,5]{1,0:T(8,128)S(1)} all-gather(f32[8,5]{1,0:T(8,128)S(1)} %copy-done.72), channel_id=1, replica_groups=mesh['dp'=8,'tensor'=4] {'dp','tensor'}, dimensions={0}, use_global_device_ids=true | all-gather | bytes 5280 | tf_op jit(solution)/shard_map/all_gather | solution.py:148
  100.7 26.1 %all-gather = bf16[8,96,6]{1,2,0:T(8,128)(2,1)S(1)} all-gather(bf16[1,96,6]{1,2,0:T(8,128)(2,1)S(1)} %get-tuple-element.954), channel_id=1, replica_groups=mesh['dp'=8,'tensor'=4] {'dp'}, dimensions={0}, use_global_device_ids=true | all-gather | bytes 10368 | tf_op jit(solution)/shard_map/all_gather | solution.py:156
  128.2 40.5 %all_gather.30 = bf16[768,256]{1,0:T(8,128)(2,1)} all-gather(bf16[24,256]{1,0:T(8,128)(2,1)S(1)} %get-tuple-element.951), channel_id=1, replica_groups=mesh['dp'=8,'tensor'=4] {'dp','tensor'}, dimensions={0}, use_global_device_ids=true | all-gather | bytes 405504 | tf_op jit(solution)/shard_map/all_gather | solution.py:147
  206.3 18.3 %while.62 = (s32[]{:T(128)}, f32[6,64,128]{2,1,0:T(8,128)S(1)}, f32[8,6,64,128]{3,2,1,0:T(8,128)}, f32[8,6]{1,0:T(8,128)S(1)}, f32[8,6,1,1]{1,3,2,0:T(1,128)}, /...) while((s32[]{:T(128)}, f32[6,64,128]{2,1,0:T(8,128)S(1)}, ...), condition=%wide.region_4.5_spmd.clone, body=%wide.region_3.4_spmd.clone.sunk | while | flops 196611 | bytes 984808 | solution.py:65
  231.6 9.4 bitcast_add_fusion.3
  253.0 7.6 multiply_reduce_fusion.8
  260.6 7.8 psum.35
  274.3 60.4 %reduce-scatter.19.cloned.1.call-done = f32[96,384]{1,0:T(8,128)} async-done(((f32[768,384]{1,0:T(8,128)}), f32[96,384]{1,0:T(8,128)}) %reduce-scatter.19.cloned.1.call-update) | async-done | bytes 147472 | tf_op jit(solution)/shard_map/reduce_scatter | solution.py:250
  337.4 31.6 %all_gather.33 = bf16[768,384]{1,0:T(8,128)(2,1)S(1)} all-gather(bf16[96,384]{1,0:T(8,128)(2,1)S(1)} %get-tuple-element.940), channel_id=1, replica_groups=mesh['dp'=8,'tensor'=4] {'dp'}, dimensions={0}, use_global_device_ids=true | all-gather | bytes 663552 | tf_op jit(solution)/shard_map/all_gather | solution.py:157
  369.0 7.5 fusion.31
  376.5 6.6 psum.36
  409.9 16.4 %fusion.12 = (f32[8,256,6]{1,2,0:T(8,128)}, f32[8,256,6]{1,2,0:T(8,128)}, f32[8,256,6]{1,2,0:T(8,128)}, f32[8,256,256]{2,1,0:T(8,128)}) fusion(f32[8,256,6]{1,2,0:T(8,128)S(1)} %get-tuple-element.920, f32[8,256,6]{1,2,0:T(8,128)S(1)} %bitcast.370, f32[8,256,256]{2,1,0:T(8,128)S(1)} %copy-done.42, pred[256,256]{1,0:T(8,128)(4,1)S(1)} %copy-done.67, ...), kind=kOutput, calls=%fused_computation.24 | convolution fusion | flops 2456252416 | bytes 9224192 | tf_op jit(solution)/shard_map/transpose(jvp())/while/body/eval_jaxpr/cqkh,ckhp->cqhp/dot_general | solution.py:55
  436.9 26.4 %while.63 = (s32[]{:T(128)}, f32[6,64,128]{2,1,0:T(8,128)S(1)}, f32[8,6,64,128]{3,2,1,0:T(8,128)}, f32[8,6]{1,0:T(8,128)S(1)}, f32[8,6,64,128]{3,2,1,0:T(8,128)}...) while((s32[]{:T(128)}, f32[6,64,128]{2,1,0:T(8,128)S(1)}, ...), condition=%wide.region_12.13_spmd.clone, body=%wide.region_10.12_spmd.clone.sunk | while | flops 294916 | bytes 1180016 | solution.py:65
  463.3 8.4 fusion.69
  491.0 15.0 %reduce-window.28 = f32[8,6,2,128]{3,0,1,2:T(8,128)S(1)} reduce-window(f32[8,6,2,128]{3,0,1,2:T(8,128)S(1)} %copy.271, f32[]{:T(128)} %constant.337.clone.1), window={size=1x1x1x128 pad=0_0x0_0x0_0x0_127}, to_apply=%region_18.19 | reduce-window | flops 1560576 | bytes 98308 | tf_op jit(solution)/shard_map/reduce-window
  506.4 13.3 %bitcast_add_fusion.2 = f32[8,256,6,64]{1,3,2,0:T(8,128)S(1)} fusion(f32[8,256,6,64]{1,3,2,0:T(8,128)} %fusion.132, f32[8,256,6]{1,2,0:T(8,128)S(1)} %get-tuple-element.920, f32[8,256,6]{1,2,0:T(8,128)} %bitcast.368, f32[8,256,256]{2,1,0:T(8,128)} %copy-done.41, pred[256,256]{1,0:T(8,128)(4,1)} %iota_compare_fusion, f32[8,256,6,64]{1,3,2,0:T(8,128)} %copy-done.7, ...), kind=kOutput, calls=%fused_computation.57 | convolution fusion | flops 2430074880 | bytes 11747328 | tf_op jit(solution)/shard_map/transpose(jvp())/while/body/eval_jaxpr/cqkh,ckhp->cqhp/dot_general | solution.py:55
  534.6 11.2 %multiply_reduce_fusion.5 = (f32[384]{0:T(512)}, f32[384]{0:T(512)}, f32[384]{0:T(512)}, f32[384]{0:T(512)}, f32[384]{0:T(512)}, /*index=5*/f32[1,2048,384]{2,1,0:T(8,128)S(1)}) fusion(f32[1,2048,384]{2,1,0:T(8,128)} %bitcast.333, f32[2048,384]{1,0:T(8,128)} %copy-done.4, f32[1,2048,384]{2,1,0:T(8,128)} %get-tuple-element.918, f32[1,2048,384]{2,1,0:T(8,128)} %copy.264, ...), kind=kLoop, calls=%fused_computation.76 | loop fusion | flops 19658880 | bytes 22029312 | tf_op jit(solution)/shard_map/transpose(jvp(vmap()))/reduce_sum | solution.py:37
  591.3 35.5 %all-reduce.30 = (f32[6,384]{1,0:T(8,128)S(1)}, f32[3,6]{1,0:T(4,128)S(1)}) all-reduce(f32[6,384]{1,0:T(8,128)S(1)} %pad_maximum_fusion.2, f32[3,6]{1,0:T(4,128)S(1)} %pad_add_fusion.9), channel_id=1, replica_groups=mesh['dp'=8,'tensor'=4] {'dp'}, use_global_device_ids=true, to_apply=%region_33.34 | all-reduce | flops 2322 | bytes 18576 | tf_op jit(solution)/shard_map/psum | solution.py:252
  640.1 43.3 %reduce-scatter.17.cloned.1.call-done = f32[96,2,384]{2,0,1:T(8,128)} async-done(((f32[768,2,384]{2,0,1:T(8,128)}), f32[96,2,384]{2,0,1:T(8,128)}) %reduce-scatter.17.cloned.1.call-update) | async-done | bytes 294928 | tf_op jit(solution)/shard_map/reduce_scatter | solution.py:248
  689.9 94.7 %reduce-scatter.21.cloned.1.call-done = f32[24,256]{1,0:T(8,128)} async-done(((f32[768,256]{1,0:T(8,128)}), f32[24,256]{1,0:T(8,128)}) %reduce-scatter.21.cloned.1.call-update) | async-done | bytes 24592 | tf_op jit(solution)/shard_map/reduce_scatter | solution.py:254
  788.5 56.2 %reduce-scatter.13.cloned.1.call-done = f32[512,768]{1,0:T(8,128)} async-done(((f32[2048,768]{1,0:T(8,128)}), f32[512,768]{1,0:T(8,128)}) %reduce-scatter.13.cloned.1.call-update) | async-done | bytes 1572880 | tf_op jit(solution)/shard_map/reduce_scatter | solution.py:231
  847.6 39.9 %all-reduce.29 = (f32[256,5]{0,1:T(8,128)S(1)}, f32[768]{0:T(1024)S(1)}) all-reduce(f32[256,5]{0,1:T(8,128)} %pad_add_fusion.7, f32[768]{0:T(1024)} %get-tuple-element.823), channel_id=9, replica_groups=mesh['dp'=8,'tensor'=4] {'dp','tensor'}, use_global_device_ids=true, to_apply=%region_45.46.clone | all-reduce | flops 2048 | bytes 16384
  896.3 41.0 %psum.39 = f32[2,8]{1,0:T(2,128)S(1)} all-reduce(f32[2,8]{1,0:T(2,128)S(1)} %stack.143), channel_id=1, replica_groups=mesh['dp'=8,'tensor'=4] {'dp','tensor'}, use_global_device_ids=true, to_apply=%region_64.65 | all-reduce | flops 16 | bytes 128 | tf_op jit(solution)/shard_map/psum | solution.py:316
  (536 shorter events, 285.1 us)
Async XLA Ops:
  7.2 162.6 %all-gather.5.cloned.1.call-start = ((), (), s32[]{:S(2)}) async-start(), calls=%async_computation.7 | async-start | bytes 3932160 | tf_op jit(solution)/shard_map/all_gather | solution.py:161
  51.6 75.3 %copy-start.70 = (f32[6,384]{1,0:T(8,128)S(1)}, f32[6,384]{1,0:T(8,128)}, u32[]{:S(2)}) copy-start(f32[6,384]{1,0:T(8,128)} %param.37) | copy-start | bytes 27652
  51.6 76.0 %copy-start.63 = (f32[24,256]{1,0:T(8,128)S(1)}, f32[24,256]{1,0:T(8,128)}, u32[]{:S(2)}) copy-start(f32[24,256]{1,0:T(8,128)} %param.39) | copy-start | bytes 73732
  55.1 128.0 %all-gather.7.cloned.1.call-start = ((), (), s32[]{:S(2)}) async-start(), calls=%async_computation.8 | async-start | bytes 1327104 | tf_op jit(solution)/shard_map/all_gather | solution.py:155
  55.9 212.5 %all-gather.9.cloned.1.call-start = ((), (), s32[]{:S(2)}) async-start(), calls=%async_computation.10 | async-start | bytes 3932160 | tf_op jit(solution)/shard_map/all_gather | solution.py:203
  57.7 277.1 %reduce-scatter.19.cloned.1.call-start = ((), (), s32[]{:S(2)}) async-start(), calls=%async_computation.14 | async-start | bytes 1327104 | tf_op jit(solution)/shard_map/reduce_scatter | solution.py:250
  127.6 256.2 %copy-start.74 = (f32[384]{0:T(512)}, f32[384]{0:T(512)S(1)}, u32[]{:S(2)}) copy-start(f32[384]{0:T(512)S(1)} %get-tuple-element.831) | copy-start | bytes 4612
  169.8 83.2 %copy-start.79 = (f32[384]{0:T(512)}, f32[384]{0:T(512)S(1)}, u32[]{:S(2)}) copy-start(f32[384]{0:T(512)S(1)} %mul.1038) | copy-start | bytes 4612
  274.3 293.3 %reduce-scatter.15.cloned.1.call-start = ((), (), s32[]{:S(2)}) async-start(), calls=%async_computation.12 | async-start | bytes 2621440 | tf_op jit(solution)/shard_map/reduce_scatter | solution.py:232
  484.1 151.9 %reduce-scatter.23.cloned.1.call-start = ((), (), s32[]{:S(2)}) async-start(), calls=%async_computation.16 | async-start | bytes 442368
  550.6 132.9 %reduce-scatter.17.cloned.1.call-start = ((), (), s32[]{:S(2)}) async-start(), calls=%async_computation.13 | async-start | bytes 2654208 | tf_op jit(solution)/shard_map/reduce_scatter | solution.py:248
  561.7 222.9 %reduce-scatter.21.cloned.1.call-start = ((), (), s32[]{:S(2)}) async-start(), calls=%async_computation.15 | async-start | bytes 811008 | tf_op jit(solution)/shard_map/reduce_scatter | solution.py:254
  570.1 274.6 %reduce-scatter.13.cloned.1.call-start = ((), (), s32[]{:S(2)}) async-start(), calls=%async_computation.11 | async-start | bytes 7864320 | tf_op jit(solution)/shard_map/reduce_scatter | solution.py:231
  578.5 382.0 %reduce-scatter.11.cloned.1.call-start = ((), (), s32[]{:S(2)}) async-start(), calls=%async_computation.9 | async-start | bytes 7864320 | tf_op jit(solution)/shard_map/reduce_scatter | solution.py:187
  586.3 97.2 %copy-start.51 = (f32[96,2,384]{2,1,0:T(2,128)S(1)}, f32[96,2,384]{2,1,0:T(2,128)}, u32[]{:S(2)}) copy-start(f32[96,2,384]{2,1,0:T(2,128)} %param.50) | copy-start | bytes 884740
  586.3 97.2 %copy-start.52 = (f32[96,2,384]{2,1,0:T(2,128)S(1)}, f32[96,2,384]{2,1,0:T(2,128)}, u32[]{:S(2)}) copy-start(f32[96,2,384]{2,1,0:T(2,128)} %param.42) | copy-start | bytes 884740
  586.3 198.2 %copy-start.64 = (f32[24,256]{1,0:T(8,128)S(1)}, f32[24,256]{1,0:T(8,128)}, u32[]{:S(2)}) copy-start(f32[24,256]{1,0:T(8,128)} %param.39) | copy-start | bytes 73732
  586.3 198.2 %copy-start.77 = (f32[24,256]{1,0:T(8,128)S(1)}, f32[24,256]{1,0:T(8,128)}, u32[]{:S(2)}) copy-start(f32[24,256]{1,0:T(8,128)} %param.55) | copy-start | bytes 73732
  586.3 198.2 %copy-start.78 = (f32[24,256]{1,0:T(8,128)S(1)}, f32[24,256]{1,0:T(8,128)}, u32[]{:S(2)}) copy-start(f32[24,256]{1,0:T(8,128)} %param.47) | copy-start | bytes 73732
  586.3 258.3 %copy-start.27 = (bf16[512,768]{1,0:T(8,128)(2,1)S(1)}, bf16[512,768]{1,0:T(8,128)(2,1)}, u32[]{:S(2)}) copy-start(bf16[512,768]{1,0:T(8,128)(2,1)} %param.31) | copy-start | bytes 2359300
  586.4 258.3 %copy-start.35 = (bf16[768,256]{1,0:T(8,128)(2,1)S(1)}, bf16[768,256]{1,0:T(8,128)(2,1)}, u32[]{:S(2)}) copy-start(bf16[768,256]{1,0:T(8,128)(2,1)} %all_gather.30) | copy-start | bytes 1179652
  586.4 258.3 %copy-start.69 = (f32[768]{0:T(1024)S(1)}, f32[768]{0:T(1024)}, u32[]{:S(2)}) copy-start(f32[768]{0:T(1024)} %copy-done.68) | copy-start | bytes 9220
  636.9 151.7 %copy-start.91 = (f32[96,6]{0,1:T(8,128)}, f32[96,6]{0,1:T(8,128)S(1)}, u32[]{:S(2)}) copy-start(f32[96,6]{0,1:T(8,128)S(1)} %copy.311) | copy-start | bytes 6916
  788.5 172.0 %copy-start.37 = (bf16[512,768]{1,0:T(8,128)(2,1)S(1)}, bf16[512,768]{1,0:T(8,128)(2,1)}, u32[]{:S(2)}) copy-start(bf16[512,768]{1,0:T(8,128)(2,1)} %param.32) | copy-start | bytes 2359300
  (118 other events, 1623.9 us)
Sparse Core Ops, SparseCore 0:
  55.2 29.0 all-gather.4
  87.1 41.1 all-gather.6
  129.8 29.2 all-gather.8
  274.4 60.3 reduce-scatter.18
  484.2 30.5 reduce-scatter.14
  550.7 60.5 reduce-scatter.22
  615.2 68.1 reduce-scatter.16
  689.9 94.5 reduce-scatter.20
  787.2 57.4 reduce-scatter.12
  847.1 59.2 reduce-scatter.10
where the time goes:
time: 977 us; the launch traced here: 971 us
  blocking collectives  312 us (32%)
  waiting for transfers between devices  255 us (26%)
  other arithmetic  155 us (16%)
  matrix products  125 us (13%)
  local copies, waits for them, and re-layouts  92.9 us (10%)
  between operations  29.8 us (3%)
    reduce_scatter x1, waiting for transfers between devices, local(): lax.psum_scatter(state_weight_grad, ('dp', 'tensor'), scatter_dimension=0...  94.7 us
    unnamed x2, blocking collectives  81.9 us
    reduce_scatter x1, waiting for transfers between devices, local(): lax.psum_scatter(out_grad, 'dp', scatter_dimension=0, tiled=True)  60.4 us
    reduce_scatter x1, waiting for transfers between devices, local(): lax.psum_scatter(normed_part, 'tensor', scatter_dimension=0, tiled=True)  56.2 us
    dot_general x14, matrix products, contract(): lax.dot_general(left, right, (((left_dim,), (right_dim,)), ((), ())), pre...  55 us
    reduce_scatter x1, waiting for transfers between devices, local(): lax.psum_scatter(in_grad, 'dp', scatter_dimension=0, tiled=True)  43.3 us
    psum x1, blocking collectives, local(): norm_totals = lax.psum(jnp.stack(partials, axis=1), ('dp', 'tensor'))  41 us
    all_gather x1, blocking collectives, local(): lax.all_gather(state_conv, ('dp', 'tensor'), axis=0, tiled=True)  40.9 us
  transfers between devices with their start and end apart: 10, of which 4 were waited for; matrix products, arithmetic and copies ran while one was open for 25% of the time, Pallas kernels for 0%

commit v1 on v0

v1 whole, which is shorter than its diff:
```python
import functools

import jax
import jax.numpy as jnp
from jax import lax
from jax.experimental import pallas as pl
from jax.experimental.pallas import tpu as pltpu
from jax.sharding import PartitionSpec as P

STATE = 128
CONV = 4
SPAN = 256
LMAX = 2048
INNER = 1536
HEAD = 64
MAPS = 2 * STATE
LANES = 128
SMALL = 16

EPSILON = 1e-05
ADAM_EPSILON = 1e-06
DECAY = 0.5
BIAS_FIRST = 0.875
BIAS_SECOND = 0.875
RATE = 0.3
WEIGHT_DECAY = 0.01
HIGHEST = lax.Precision.HIGHEST
BF = jnp.bfloat16
F32 = jnp.float32


def dot(left, right, left_dim=1, right_dim=0, precision=None):
    return lax.dot_general(
        left,
        right,
        (((left_dim,), (right_dim,)), ((), ())),
        precision=precision,
        preferred_element_type=F32,
    )


def exchange(values, axis, mask):
    count = lax.axis_size(axis)
    return lax.ppermute(values, axis, [(at, at ^ mask) for at in range(count)])


def low_count(count):
    low = 1
    while low * low * 4 <= count:
        low *= 2
    return low


def gather_pieces(own, axis, low):
    count = lax.axis_size(axis)
    pieces = {0: own}
    for high in range(low, count, low):
        pieces[high] = exchange(own, axis, high)
    for high in range(0, count, low):
        for near in range(1, low):
            pieces[high + near] = exchange(pieces[high], axis, near)
    return [pieces[mask] for mask in range(count)]


def slot_masks(count, low):
    return [high + near for near in range(low) for high in range(0, count, low)]


def scatter_parts(slots, axis, low, small=0):
    count = lax.axis_size(axis)
    highs = count // low
    total = slots[:highs].astype(F32)
    for near in range(1, low):
        sent = slots[near * highs : (near + 1) * highs]
        total = total + exchange(sent, axis, near).astype(F32)
    if small > 0:
        joined = total[:, :small] + total[:, small : 2 * small]
        high = lax.reduce_precision(joined, 8, 7)
        total = jnp.concatenate([high, joined - high, total[:, 2 * small :]], axis=1)
    received = [
        exchange(total[position].astype(slots.dtype), axis, position * low)
        for position in range(1, highs)
    ]
    return total[0], received


def scatter_sum(slots, axis, low):
    kept, received = scatter_parts(slots, axis, low)
    for values in received:
        kept = kept + values.astype(F32)
    return kept


def lane_ids(shape):
    return lax.broadcasted_iota(jnp.int32, shape, len(shape) - 1)


def spread_heads(columns, heads):
    rows = columns.shape[0]
    left = lane_ids((rows, LANES)) < HEAD
    return jnp.concatenate(
        [
            jnp.where(left, columns[:, head : head + 1], columns[:, head + 1 : head + 2])
            for head in range(0, heads, 2)
        ],
        axis=1,
    )


def causal_mask():
    rows = lax.broadcasted_iota(jnp.int32, (SPAN, SPAN), 0)
    columns = lax.broadcasted_iota(jnp.int32, (SPAN, SPAN), 1)
    return rows >= columns


def step_terms(step_in, heads_ref):
    step = jnp.maximum(step_in, 0.0) + jnp.log1p(jnp.exp(-jnp.abs(step_in)))
    rate = jnp.exp(heads_ref[0:1, :])
    decay = -rate * step
    lower = causal_mask().astype(F32).astype(BF)
    cumulative = sum(dot(lower, part) for part in thirds(decay))
    return step, rate, decay, cumulative


def halves(values):
    high = values.astype(BF)
    return high, (values - high.astype(F32)).astype(BF)


def thirds(values):
    high = values.astype(BF)
    rest = values - high.astype(F32)
    middle = rest.astype(BF)
    return high, middle, (rest - middle.astype(F32)).astype(BF)


def sigmoid(values):
    return 1.0 / (1.0 + jnp.exp(-values))


def forward_kernel(
    channels, pieces, blocks_per, ids, u_ref, *refs
):
    width = channels
    heads = width // HEAD
    mixed_width = width + MAPS
    piece_refs = refs[:pieces]
    (
        state_w_ref,
        gain_ref,
        taps_ref,
        heads_ref,
        skip_ref,
        normed_ref,
        gate_ref,
        raw_ref,
        pre_ref,
        act_ref,
        step_ref,
        state_ref,
        mixed_ref,
        weight_ref,
        tail,
        carried,
    ) = refs[pieces:]
    at = pl.program_id(0)

    @pl.when(at == 0)
    def _():
        rows = weight_ref.shape[0] // pieces
        for mask in range(pieces):
            block = ids[0] ^ mask if pieces > 1 else 0
            where_ = pl.ds(pl.multiple_of(block * rows, 8), rows) if pieces > 1 else slice(None)
            weight_ref[where_, : 2 * width] = piece_refs[mask][:, : 2 * width]
            weight_ref[where_, 2 * width + MAPS :] = piece_refs[mask][:, 2 * width :]
        weight_ref[:, 2 * width : 2 * width + MAPS] = state_w_ref[...]

    @pl.when(at % (LMAX // SPAN) == 0)
    def _():
        tail[0:8, :] = jnp.zeros((8, mixed_width), F32)
        carried[...] = jnp.zeros_like(carried)

    inputs = u_ref[0].astype(F32)
    scale = lax.rsqrt(jnp.mean(inputs * inputs, axis=-1, keepdims=True) + EPSILON)
    normed = (inputs * scale * gain_ref[0:1, :]).astype(BF)
    normed_ref[...] = normed
    gate_ref[...] = dot(normed, weight_ref[:, :width])
    raw = dot(normed, weight_ref[:, width : 2 * width + MAPS])
    raw_ref[...] = raw
    tail[8:, :] = raw
    step_in = dot(normed, weight_ref[:, 2 * width + MAPS :]) + heads_ref[1:2, :]
    step_ref[...] = step_in
    pre = taps_ref[CONV : CONV + 1, :] + taps_ref[0:1, :] * tail[5 : 5 + SPAN, :]
    for tap in range(1, CONV):
        pre = pre + taps_ref[tap : tap + 1, :] * tail[5 + tap : 5 + tap + SPAN, :]
    tail[0:8, :] = tail[SPAN : SPAN + 8, :]
    pre_ref[...] = pre
    act = (pre * sigmoid(pre)).astype(BF)
    act_ref[...] = act
    signal = act[:, :width].astype(F32)
    b_rows = act[:, width : width + STATE]
    c_rows = act[:, width + STATE :]
    step, rate, decay, cumulative = step_terms(step_in, heads_ref)
    across_rows = jnp.transpose(cumulative)
    closing = cumulative[SPAN - 1 : SPAN, :]
    held = jnp.where(causal_mask(), dot(c_rows, b_rows, 1, 1), 0.0)
    weighted = (spread_heads(step, heads) * signal).astype(BF)
    left = lane_ids((SPAN, LANES)) < HEAD
    state = carried[...]
    state_ref[0] = state
    across = dot(
        jnp.concatenate([c_rows, c_rows], axis=1),
        jnp.concatenate(halves(state), axis=1),
        1,
        1,
    ) * spread_heads(jnp.exp(cumulative), heads)
    within = []
    for head in range(0, heads, 2):
        lanes = slice(head * HEAD, head * HEAD + LANES)
        pair = weighted[:, lanes]
        total = None
        for side in range(2):
            spread = (
                cumulative[:, head + side : head + side + 1]
                - across_rows[head + side : head + side + 1, :]
            )
            mixing = (held * jnp.exp(jnp.minimum(spread, 0.0))).astype(BF)
            kept = jnp.where(left if side == 0 else ~left, pair, jnp.zeros_like(pair))
            part = dot(mixing, kept)
            total = part if total is None else total + part
        within.append(total)
    mixed_ref[...] = jnp.concatenate(within, axis=1) + across + skip_ref[0:1, :] * signal
    ended = weighted.astype(F32) * spread_heads(jnp.exp(closing - cumulative), heads)
    fresh = sum(dot(part, b_rows, 0, 0) for part in halves(ended))
    kept_rate = jnp.exp(closing)
    for head in range(heads):
        rows = slice(head * HEAD, (head + 1) * HEAD)
        carried[rows, :] = kept_rate[:, head : head + 1] * state[rows, :] + fresh[rows, :]


def rows_live(ids, at, lengths):
    sequence = at // (LMAX // SPAN)
    position = (at % (LMAX // SPAN)) * SPAN + lax.broadcasted_iota(jnp.int32, (SPAN, 1), 0)
    return position < lengths[sequence]


def middle_kernel(ids, lengths, grad_ref, gate_ref, mixed_ref, *refs):
    weight, gain_ref, merged_grad_ref, branch_ref, sums_ref = refs
    at = pl.program_id(0)

    upstream = grad_ref[0]
    upstream = jnp.where(rows_live(ids, at, lengths), upstream, jnp.zeros_like(upstream))
    merged_grad = dot(upstream, weight[...])
    merged_grad_ref[...] = merged_grad
    gate = gate_ref[...]
    gated = mixed_ref[...] * (gate * sigmoid(gate))
    gained = gated * gain_ref[0:1, :]
    squares = jnp.sum(gated * gated, axis=1, keepdims=True)
    products = jnp.sum(merged_grad * gained, axis=1, keepdims=True)
    branch_ref[0] = dot(gained.astype(BF), weight[...], 1, 1).astype(BF)
    lanes = lane_ids((SPAN, LANES))
    both = jnp.where(lanes == 0, squares, jnp.where(lanes == 1, products, 0.0))
    sums_ref[...] = jnp.transpose(both)[0:2, :]


def backward_kernel(
    channels,
    masks,
    ids,
    lengths,
    sums_ref,
    u_ref,
    grad_ref,
    normed_ref,
    gate_ref,
    mixed_ref,
    merged_grad_ref,
    raw_ref,
    pre_ref,
    act_ref,
    step_ref,
    state_ref,
    state_next_ref,
    weight_ref,
    taps_ref,
    heads_ref,
    skip_ref,
    gain_ref,
    part_ref,
    slots_ref,
    carried,
    ahead,
    weight_sum,
    out_sum,
    tap_sum,
    head_sum,
    gain_sum,
):
    width = channels
    heads = width // HEAD
    mixed_width = width + MAPS
    step_at = pl.program_id(0)
    at = pl.num_programs(0) - 1 - step_at

    @pl.when(step_at == 0)
    def _():
        weight_sum[...] = jnp.zeros_like(weight_sum)
        out_sum[...] = jnp.zeros_like(out_sum)
        tap_sum[...] = jnp.zeros_like(tap_sum)
        head_sum[...] = jnp.zeros_like(head_sum)
        gain_sum[...] = jnp.zeros_like(gain_sum)

    @pl.when(step_at % (LMAX // SPAN) == 0)
    def _():
        carried[...] = jnp.zeros_like(carried)
        ahead[SPAN:, :] = jnp.zeros((8, mixed_width), F32)

    sums = sums_ref[...]
    scale_row = lax.rsqrt(sums[0:1, :] / INNER + EPSILON)
    cross_row = scale_row * scale_row * scale_row * (sums[1:2, :] / INNER)
    row_ids = lax.broadcasted_iota(jnp.int32, (LANES, SPAN), 0)
    columns = jnp.transpose(jnp.where(row_ids == 0, scale_row, cross_row))
    gate_scale = columns[:, 0:1]
    cross = columns[:, 1:2]

    gate = gate_ref[...]
    gate_s = sigmoid(gate)
    gate_act = gate * gate_s
    mixed = mixed_ref[...]
    gated = mixed * gate_act
    merged_grad = merged_grad_ref[...]
    gain = skip_ref[1:2, :]
    scaled = gated * gate_scale
    tap_sum[5:6, :width] += jnp.sum(merged_grad * scaled, axis=0, keepdims=True)
    merged = (scaled * gain).astype(BF)
    upstream = grad_ref[0]
    upstream = jnp.where(rows_live(ids, at, lengths), upstream, jnp.zeros_like(upstream))
    out_sum[...] += dot(upstream, merged, 0, 0)
    gated_grad = gate_scale * (merged_grad * gain) - gated * cross
    mixed_grad = gated_grad * gate_act
    gate_grad = gated_grad * mixed * (gate_s * (1.0 + gate * (1.0 - gate_s)))

    act = act_ref[...]
    signal = act[:, :width].astype(F32)
    b_rows = act[:, width : width + STATE]
    c_rows = act[:, width + STATE :]
    skip = skip_ref[0:1, :]
    tap_sum[6:7, :width] += jnp.sum(mixed_grad * signal, axis=0, keepdims=True)
    grad_high, grad_rest = halves(mixed_grad)
    grad_rows = grad_high.astype(F32) + grad_rest.astype(F32)

    step_in = step_ref[...]
    step, rate, decay, cumulative = step_terms(step_in, heads_ref)
    across_rows = jnp.transpose(cumulative)
    closing = cumulative[SPAN - 1 : SPAN, :]
    causal = causal_mask()
    held = jnp.where(causal, dot(c_rows, b_rows, 1, 1), 0.0)
    step_wide = spread_heads(step, heads)
    weighted = (step_wide * signal).astype(BF)
    weighted_rows = weighted.astype(F32)
    end_wide = spread_heads(jnp.exp(closing - cumulative), heads)
    state_grad = carried[...]
    state_parts = halves(state_grad)
    grown = halves(grad_rows * spread_heads(jnp.exp(cumulative), heads))
    before = halves(state_ref[0])
    c_grad = dot(grown[0], before[0]) + dot(grown[0], before[1]) + dot(grown[1], before[0])
    ended = halves(weighted_rows * end_wide)
    b_grad = (
        dot(ended[0], state_parts[0])
        + dot(ended[0], state_parts[1])
        + dot(ended[1], state_parts[0])
    )
    from_state = end_wide * dot(
        jnp.concatenate([b_rows, b_rows], axis=1), jnp.concatenate(state_parts, axis=1), 1, 1
    )
    left = lane_ids((SPAN, LANES)) < HEAD
    held_grad = None
    within = []
    for head in range(0, heads, 2):
        lanes = slice(head * HEAD, head * HEAD + LANES)
        pair = weighted[:, lanes]
        pair_twice = jnp.concatenate([pair, pair], axis=1)
        total = None
        for side in range(2):
            spread = (
                cumulative[:, head + side : head + side + 1]
                - across_rows[head + side : head + side + 1, :]
            )
            damping = jnp.exp(jnp.minimum(spread, 0.0))
            mixing = (held * damping).astype(BF)
            side_lanes = left if side == 0 else ~left
            kept = jnp.concatenate(
                [
                    jnp.where(side_lanes, part[:, lanes], jnp.zeros_like(pair))
                    for part in (grad_high, grad_rest)
                ],
                axis=1,
            )
            term = dot(kept, pair_twice, 1, 1) * damping
            held_grad = term if held_grad is None else held_grad + term
            part = dot(mixing, kept, 0, 0)
            total = part if total is None else total + part
        within.append(total[:, :LANES] + total[:, LANES:])
    held_low = jnp.where(causal, held_grad, 0.0).astype(BF)
    c_grad = c_grad + dot(held_low, b_rows)
    b_grad = b_grad + dot(held_low, c_rows, 0, 0)
    weighted_grad = jnp.concatenate(within, axis=1) + from_state
    fresh = sum(dot(part, c_rows, 0, 0) for part in grown)
    kept_rate = jnp.exp(closing)
    overlap = jnp.sum(state_grad * state_next_ref[0], axis=1, keepdims=True)
    lane_row = lane_ids((1, LANES))
    closing_grad = jnp.zeros((1, LANES), F32)
    for head in range(heads):
        rows = slice(head * HEAD, (head + 1) * HEAD)
        carried[rows, :] = kept_rate[:, head : head + 1] * state_grad[rows, :] + fresh[rows, :]
        closing_grad = closing_grad + jnp.where(
            lane_row == head, jnp.sum(overlap[rows, :], axis=0, keepdims=True), 0.0
        )
    picker = (
        lax.broadcasted_iota(jnp.int32, (width, LANES), 0) // HEAD
        == lax.broadcasted_iota(jnp.int32, (width, LANES), 1)
    ).astype(F32).astype(BF)
    shaped = mixed - skip * signal
    cumulative_grad = sum(
        dot(part, picker)
        for part in halves(grad_rows * shaped - weighted_rows * weighted_grad)
    )
    lower = causal.astype(F32).astype(BF)
    decay_grad = sum(dot(lower, part, 0, 0) for part in halves(cumulative_grad)) + closing_grad
    step_grad = (
        sum(dot(part, picker) for part in halves(signal * weighted_grad)) - rate * decay_grad
    )
    step_in_grad = step_grad * sigmoid(step_in)
    head_sum[0:1, :] += jnp.sum(decay * decay_grad, axis=0, keepdims=True)
    head_sum[1:2, :] += jnp.sum(step_in_grad, axis=0, keepdims=True)
    signal_grad = step_wide * weighted_grad + skip * mixed_grad

    pre = pre_ref[...]
    pre_s = sigmoid(pre)
    slope = pre_s * (1.0 + pre * (1.0 - pre_s))
    ahead[:SPAN, :] = jnp.concatenate([signal_grad, b_grad, c_grad], axis=1) * slope
    raw = raw_ref[...]
    raw_grad = None
    for shift in range(CONV):
        moved = ahead[shift : shift + SPAN, :]
        tap = CONV - 1 - shift
        term = taps_ref[tap : tap + 1, :] * moved
        raw_grad = term if raw_grad is None else raw_grad + term
        tap_sum[tap : tap + 1, :] += jnp.sum(raw * moved, axis=0, keepdims=True)
        if shift == 0:
            tap_sum[CONV : CONV + 1, :] += jnp.sum(moved, axis=0, keepdims=True)
    ahead[SPAN:, :] = ahead[0:8, :]

    low = jnp.concatenate(
        [gate_grad.astype(BF), raw_grad.astype(BF), step_in_grad.astype(BF)], axis=1
    )
    normed = normed_ref[...]
    weight_sum[...] += dot(normed, low, 0, 0)
    part = dot(low, weight_ref[...], 1, 1)
    part_ref[0] = part.astype(BF)
    inputs = u_ref[0].astype(F32)
    scale = lax.rsqrt(jnp.mean(inputs * inputs, axis=-1, keepdims=True) + EPSILON)
    gain_sum[0:1, :] += jnp.sum(part * (inputs * scale), axis=0, keepdims=True)

    @pl.when(step_at == pl.num_programs(0) - 1)
    def _():
        columns_in = weight_sum.shape[1]
        rows = weight_sum.shape[0] // len(masks)
        channel_count = rows * len(masks)
        for position, mask in enumerate(masks):
            block = ids[0] ^ mask
            small = jnp.concatenate(
                [
                    tap_sum[:, :width],
                    head_sum[...],
                    pltpu.roll(
                        tap_sum[:, width:], (MAPS - block * (MAPS // len(masks))) % MAPS, 1
                    )[:, :LANES],
                    pltpu.roll(gain_sum[...], (channel_count - block * rows) % channel_count, 1)[
                        :, :LANES
                    ],
                ],
                axis=1,
            )
            both = jnp.concatenate(halves(small), axis=0)
            picked = pl.ds(pl.multiple_of(block * rows, 8), rows)
            slots_ref[position, 0:SMALL, : both.shape[1]] = both
            slots_ref[position, 0:SMALL, both.shape[1] :] = jnp.zeros(
                (SMALL, slots_ref.shape[2] - both.shape[1]), BF
            )
            slots_ref[position, SMALL:, :columns_in] = weight_sum[picked, :].astype(BF)
            slots_ref[position, SMALL:, columns_in:] = out_sum[picked, :].astype(BF)


def pad_to(values, axis, size):
    if values.shape[axis] == size:
        return values
    pads = [(0, 0)] * values.ndim
    pads[axis] = (0, size - values.shape[axis])
    return jnp.pad(values, pads)


def whole_spec(shape):
    return pl.BlockSpec(shape, lambda *_: (0,) * len(shape))


def lamb_parts(weight, gradient, first_old, second_old):
    first_new = DECAY * first_old + (1.0 - DECAY) * gradient
    second_new = DECAY * second_old + (1.0 - DECAY) * gradient * gradient
    direction = (
        first_new / BIAS_FIRST / (jnp.sqrt(second_new / BIAS_SECOND) + ADAM_EPSILON)
        + WEIGHT_DECAY * weight
    )
    return (first_new, second_new, direction)


def total_of(values):
    while len(values.shape) > 2:
        values = jnp.sum(values, axis=0)
    return jnp.sum(jnp.sum(values, axis=1, keepdims=True), axis=0, keepdims=True)


def lamb_one(position, copies, gradient, olds, outs, norms):
    weight = olds[0][...]
    first_new, second_new, direction = lamb_parts(weight, gradient, olds[1][...], olds[2][...])
    outs[0][...] = gradient
    outs[1][...] = first_new
    outs[2][...] = second_new
    outs[3][...] = direction
    lanes = lane_ids((1, LANES))
    share = 1.0 / copies
    return (
        norms
        + jnp.where(lanes == position, total_of(weight * weight) * share, 0.0)
        + jnp.where(lanes == 8 + position, total_of(direction * direction) * share, 0.0)
    )


def pack_kernel(width, tensor_count, kept_ref, *refs):
    received = refs[:-1]
    packed_ref = refs[-1]
    maps_rows = packed_ref.shape[1] - 8
    lanes = slice(2 * width, 2 * width + MAPS)
    state = kept_ref[SMALL:, lanes]
    small = kept_ref[0:SMALL, width + LANES : width + LANES + MAPS]
    for ref in received:
        state = state + ref[SMALL:, lanes].astype(F32)
        small = small + ref[0:SMALL, width + LANES : width + LANES + MAPS].astype(F32)
    small = small[:8] + small[8:]
    for at in range(tensor_count):
        packed_ref[at, 0:8, :] = small
        packed_ref[at, 8:, :] = state[at * maps_rows : (at + 1) * maps_rows, :]


def lamb_wide_kernel(width, channels, heads, copies, count, kept_ref, *refs):
    received = refs[:count]
    olds = refs[count : count + 15]
    outs = refs[count + 15 : count + 35]
    norms_ref = refs[count + 35]
    whole = kept_ref[...]
    for ref in received:
        whole = whole + ref[...].astype(F32)
    columns = 2 * width + MAPS + LANES
    block = whole[SMALL:]
    small = whole[:8] + whole[8:SMALL]
    norms = jnp.zeros((1, LANES), F32)
    in_grad = jnp.stack([block[:, :channels], block[:, width : width + channels]], axis=1)
    step_grad = block[:, 2 * width + MAPS : 2 * width + MAPS + heads]
    out_grad = block[:, columns : columns + channels]
    channel_grad = small[: CONV + 2, :channels]
    picker = (
        lax.broadcasted_iota(jnp.int32, (width, LANES), 0) // HEAD
        == lax.broadcasted_iota(jnp.int32, (width, LANES), 1)
    ).astype(F32)
    skips = dot(small[:, :width], picker, precision=HIGHEST)
    head_grad = jnp.concatenate(
        [small[0:2, width : width + LANES], skips[6:7, :]], axis=0
    )[:, :heads]
    gradients = (in_grad, step_grad, out_grad, channel_grad, head_grad)
    for position, gradient in enumerate(gradients):
        norms = lamb_one(
            position,
            copies if position > 2 else 1.0,
            gradient,
            olds[position::5],
            outs[position::5],
            norms,
        )
    norms_ref[...] = norms


def lamb_maps_kernel(ids, packed_ref, *refs):
    olds = refs[:9]
    norms_in_ref = refs[9]
    outs = refs[10:22]
    norms_ref = refs[22]
    whole = jnp.sum(packed_ref[...], axis=0)
    small = whole[:8]
    conv_rows = olds[1].shape[0]
    gain_size = olds[2].shape[1]
    picker = (
        lax.broadcasted_iota(jnp.int32, (conv_rows, LANES), 0) + ids[1] * conv_rows
        == lax.broadcasted_iota(jnp.int32, (conv_rows, LANES), 1)
    ).astype(F32)
    conv_grad = dot(picker, small[:, :LANES], 1, 1, precision=HIGHEST)[:, : CONV + 1]
    gain_grad = pltpu.roll(small[:, LANES:], (LANES - ids[1] * gain_size) % LANES, 1)[
        0:1, :gain_size
    ]
    norms = norms_in_ref[...]
    for position, gradient in enumerate((whole[8:], conv_grad, gain_grad)):
        norms = lamb_one(
            5 + position, 1.0, gradient, olds[position::3], outs[position::3], norms
        )
    norms_ref[...] = jnp.broadcast_to(norms[None], norms_ref.shape)


def update_kernel(norms_ref, *refs):
    norms = jnp.sqrt(jnp.sum(norms_ref[...], axis=0))
    refs[-1][...] = jnp.concatenate([norms[:, :8], norms[:, 8:16]], axis=0)
    for position in range(8):
        ratio = -RATE * norms[:, position : position + 1] / norms[:, 8 + position : 9 + position]
        direction = refs[position][...]
        if direction.ndim == 3:
            ratio = ratio[None]
        refs[8 + position][...] = ratio * direction


def split_three(values):
    high = lax.reduce_precision(values, 8, 7)
    rest = values - high
    middle = lax.reduce_precision(rest, 8, 7)
    return [high.astype(BF), middle.astype(BF), (rest - middle).astype(BF)]


def local(*arguments):
    block_input, output_grad, lengths = arguments[:3]
    masters = arguments[3:11]
    firsts = arguments[11:19]
    seconds = arguments[19:27]
    (
        in_proj,
        step_proj,
        out_proj,
        channel_params,
        head_params,
        state_proj,
        state_conv,
        norm_gain,
    ) = masters
    dp_count = lax.axis_size("dp")
    tensor_count = lax.axis_size("tensor")
    dp_at = lax.axis_index("dp")
    tensor_at = lax.axis_index("tensor")
    everywhere = dp_count * tensor_count
    own_count, model = block_input.shape
    tokens = own_count * tensor_count
    chunks = tokens // SPAN
    own_chunks = own_count // SPAN
    rows = in_proj.shape[0]
    channels = in_proj.shape[2]
    heads = head_params.shape[1]
    width = -(-channels // LANES) * LANES
    mixed_width = width + MAPS
    columns = 2 * width + MAPS + LANES
    dp_low = low_count(dp_count)
    ids = jnp.stack([dp_at, tensor_at]).astype(jnp.int32)

    in_low = jnp.concatenate(
        [
            pad_to(in_proj[:, 0, :].astype(BF), 1, width),
            pad_to(in_proj[:, 1, :].astype(BF), 1, width),
            pad_to(step_proj.astype(BF), 1, LANES),
        ],
        axis=1,
    )
    out_low = pad_to(out_proj.astype(BF), 1, width)
    u_pieces = jnp.stack(gather_pieces(block_input, "tensor", 2))
    in_pieces = gather_pieces(in_low, "dp", dp_low)
    maps_rows = state_proj.shape[0]
    conv_rows = state_conv.shape[0]
    small_own = jnp.concatenate(
        split_three(state_conv.reshape(-1)) + split_three(norm_gain), axis=0
    )
    shared_own = jnp.concatenate(
        [state_proj.astype(BF), pad_to(small_own, 0, MAPS)[None, :]], axis=0
    )
    shared = lax.all_to_all(
        jnp.broadcast_to(shared_own[None], (everywhere,) + shared_own.shape),
        ("dp", "tensor"),
        0,
        0,
    )
    state_weight = shared[:, :maps_rows].reshape(-1, MAPS)
    small_all = shared[:, maps_rows].astype(F32)
    conv_size = conv_rows * (CONV + 1)
    conv_whole = sum(
        small_all[:, part * conv_size : (part + 1) * conv_size] for part in range(3)
    ).reshape(-1, CONV + 1)
    gain_base = 3 * conv_size
    gain_size = norm_gain.shape[0]
    gain_whole = sum(
        small_all[:, gain_base + part * gain_size : gain_base + (part + 1) * gain_size]
        for part in range(3)
    ).reshape(-1)
    grad_far = {
        high: exchange(output_grad, "tensor", high) for high in range(2, tensor_count, 2)
    }
    out_spread = lax.all_to_all(
        jnp.broadcast_to(out_low[None], (dp_count,) + out_low.shape), "dp", 0, 0
    ).reshape(model, width)
    if rows % 16 != 0:
        order = dp_at ^ jnp.arange(dp_count)
        in_pieces = [jnp.stack(in_pieces)[order].reshape(model, -1)]
    pieces = len(in_pieces)

    channel_wide = pad_to(channel_params, 1, width)
    taps = pad_to(
        jnp.concatenate([channel_wide[: CONV + 1], conv_whole.T], axis=1), 0, 8
    )
    heads_wide = pad_to(pad_to(head_params, 1, LANES), 0, 8)
    skip_wide = jnp.repeat(pad_to(head_params[2], 0, width // HEAD), HEAD)
    skip_gain = pad_to(jnp.stack([skip_wide, channel_wide[CONV + 1]]), 0, 8)
    gain_rows = pad_to(gain_whole[None, :], 0, 8)

    def token_spec(size, reverse=False):
        if reverse:
            return pl.BlockSpec((SPAN, size), lambda at, *_: (chunks - 1 - at, 0))
        return pl.BlockSpec((SPAN, size), lambda at, *_: (at, 0))

    def piece_spec(reverse=False):
        def index(at, ids_ref, *_):
            block = chunks - 1 - at if reverse else at
            return ((block // own_chunks) ^ ids_ref[1], block % own_chunks, 0)

        return pl.BlockSpec((1, SPAN, model), index)

    def struct(shape, dtype=F32):
        return jax.ShapeDtypeStruct(shape, dtype)

    arbitrary = pltpu.CompilerParams(
        dimension_semantics=("arbitrary",), vmem_limit_bytes=56 * 1024 * 1024
    )
    normed, gate_raw, raw, pre, act, step_in, states, mixed, weight = pl.pallas_call(
        functools.partial(forward_kernel, width, pieces, own_chunks),
        grid_spec=pltpu.PrefetchScalarGridSpec(
            num_scalar_prefetch=1,
            grid=(chunks,),
            in_specs=[piece_spec()]
            + [whole_spec(piece.shape) for piece in in_pieces]
            + [
                whole_spec(state_weight.shape),
                whole_spec(gain_rows.shape),
                whole_spec(taps.shape),
                whole_spec(heads_wide.shape),
                whole_spec(skip_gain.shape),
            ],
            out_specs=[
                token_spec(model),
                token_spec(width),
                token_spec(mixed_width),
                token_spec(mixed_width),
                token_spec(mixed_width),
                token_spec(LANES),
                pl.BlockSpec((1, width, STATE), lambda at, *_: (at, 0, 0)),
                token_spec(width),
                whole_spec((model, columns)),
            ],
            scratch_shapes=[
                pltpu.VMEM((SPAN + 8, mixed_width), F32),
                pltpu.VMEM((width, STATE), F32),
            ],
        ),
        out_shape=[
            struct((tokens, model), BF),
            struct((tokens, width)),
            struct((tokens, mixed_width)),
            struct((tokens, mixed_width)),
            struct((tokens, mixed_width), BF),
            struct((tokens, LANES)),
            struct((chunks, width, STATE)),
            struct((tokens, width)),
            struct((model, columns), BF),
        ],
        compiler_params=arbitrary,
        name="ssd_forward",
    )(ids, u_pieces, *in_pieces, state_weight, gain_rows, taps, heads_wide, skip_gain)

    masks_far = list(grad_far)
    *far, gate_raw = lax.optimization_barrier([grad_far[mask] for mask in masks_far] + [gate_raw])
    grad_far = dict(zip(masks_far, far))
    grad_far[0] = output_grad
    grad_pieces = jnp.stack(
        [
            exchange(grad_far[mask & ~1], "tensor", 1) if mask & 1 else grad_far[mask]
            for mask in range(tensor_count)
        ]
    )
    gate_gain_rows = pad_to(channel_wide[CONV + 1][None, :], 0, 8)
    merged_grad, branch_part, sums_part = pl.pallas_call(
        middle_kernel,
        grid_spec=pltpu.PrefetchScalarGridSpec(
            num_scalar_prefetch=2,
            grid=(chunks,),
            in_specs=[
                piece_spec(),
                token_spec(width),
                token_spec(width),
                whole_spec(out_spread.shape),
                whole_spec(gate_gain_rows.shape),
            ],
            out_specs=[
                token_spec(width),
                piece_spec(),
                pl.BlockSpec((2, SPAN), lambda at, *_: (0, at)),
            ],
        ),
        out_shape=[
            struct((tokens, width)),
            struct((tensor_count, own_count, model), BF),
            struct((2, tokens)),
        ],
        compiler_params=arbitrary,
        name="gate_middle",
    )(ids, lengths, grad_pieces, gate_raw, mixed, out_spread, gate_gain_rows)

    sums = sums_part
    bit = 1
    while bit < tensor_count:
        sums = sums + exchange(sums, "tensor", bit)
        bit *= 2

    masks = slot_masks(dp_count, dp_low)
    slot_columns = columns + width
    token_back = functools.partial(token_spec, reverse=True)
    normed_part, slots = pl.pallas_call(
        functools.partial(backward_kernel, width, masks),
        grid_spec=pltpu.PrefetchScalarGridSpec(
            num_scalar_prefetch=2,
            grid=(chunks,),
            in_specs=[
                pl.BlockSpec((2, SPAN), lambda at, *_: (0, chunks - 1 - at)),
                piece_spec(True),
                piece_spec(True),
                token_back(model),
                token_back(width),
                token_back(width),
                token_back(width),
                token_back(mixed_width),
                token_back(mixed_width),
                token_back(mixed_width),
                token_back(LANES),
                pl.BlockSpec((1, width, STATE), lambda at, *_: (chunks - 1 - at, 0, 0)),
                pl.BlockSpec(
                    (1, width, STATE), lambda at, *_: (jnp.minimum(chunks - at, chunks - 1), 0, 0)
                ),
                whole_spec((model, columns)),
                whole_spec(taps.shape),
                whole_spec(heads_wide.shape),
                whole_spec(skip_gain.shape),
                whole_spec(gain_rows.shape),
            ],
            out_specs=[
                piece_spec(True),
                whole_spec((dp_count, SMALL + rows, slot_columns)),
            ],
            scratch_shapes=[
                pltpu.VMEM((width, STATE), F32),
                pltpu.VMEM((SPAN + 8, mixed_width), F32),
                pltpu.VMEM((model, columns), F32),
                pltpu.VMEM((model, width), F32),
                pltpu.VMEM((8, mixed_width), F32),
                pltpu.VMEM((8, LANES), F32),
                pltpu.VMEM((8, model), F32),
            ],
        ),
        out_shape=[
            struct((tensor_count, own_count, model), BF),
            struct((dp_count, SMALL + rows, slot_columns), BF),
        ],
        compiler_params=arbitrary,
        name="ssd_backward",
    )(
        ids,
        lengths,
        sums,
        u_pieces,
        grad_pieces,
        normed,
        gate_raw,
        mixed,
        merged_grad,
        raw,
        pre,
        act,
        step_in,
        states,
        states,
        weight,
        taps,
        heads_wide,
        skip_gain,
        gain_rows,
    )

    def owner_sum(parts):
        ordered = jnp.stack([parts[mask] for mask in slot_masks(tensor_count, 2)])
        return scatter_sum(ordered, "tensor", 2)

    inputs = block_input.astype(F32)
    branch = owner_sum(branch_part)
    position_all = tensor_at * own_count + jnp.arange(own_count, dtype=jnp.int32)
    length_of = jnp.sum(
        jnp.where(
            (position_all // LMAX)[:, None]
            == jnp.arange(lengths.shape[0], dtype=jnp.int32)[None, :],
            lengths[None, :],
            0,
        ),
        axis=1,
    )
    live_own = (position_all % LMAX < length_of)[:, None]
    own_squares = lax.dynamic_slice(sums[0], (tensor_at * own_count,), (own_count,))
    own_scale = lax.rsqrt(own_squares / INNER + EPSILON)[:, None]
    output = (inputs + jnp.where(live_own, branch * own_scale, 0.0)).astype(BF)

    normed_grad = owner_sum(normed_part)
    scale = lax.rsqrt(jnp.mean(inputs * inputs, axis=-1, keepdims=True) + EPSILON)
    scaled_grad = normed_grad * gain_whole[None, :]
    input_grad = (
        output_grad.astype(F32)
        + scale * scaled_grad
        - inputs * scale**3 * jnp.mean(scaled_grad * inputs, axis=-1, keepdims=True)
    )

    kept, received = scatter_parts(slots, "dp", dp_low, SMALL // 2)
    whole_vmem = pl.BlockSpec(memory_space=pltpu.VMEM)
    plain = pltpu.CompilerParams(vmem_limit_bytes=48 * 1024 * 1024)
    packed = pl.pallas_call(
        functools.partial(pack_kernel, width, tensor_count),
        in_specs=[whole_vmem] * (1 + len(received)),
        out_specs=whole_vmem,
        out_shape=struct((tensor_count, maps_rows + 8, MAPS)),
        compiler_params=plain,
        name="pack_maps",
    )(kept, *received)
    maps_parts = lax.all_to_all(packed, "tensor", 0, 0)
    wide_shapes = [struct(weight_.shape) for weight_ in masters[:5]]
    wide = pl.pallas_call(
        functools.partial(
            lamb_wide_kernel, width, channels, heads, float(dp_count), len(received)
        ),
        in_specs=[whole_vmem] * (1 + len(received) + 15),
        out_specs=[whole_vmem] * 21,
        out_shape=wide_shapes * 4 + [struct((1, LANES))],
        compiler_params=plain,
        name="lamb_wide",
    )(kept, *received, *masters[:5], *firsts[:5], *seconds[:5])

    def flat(values):
        return [values[5], values[6], values[7][None, :]]

    maps_shapes = [struct(values.shape) for values in flat(masters)]
    maps = pl.pallas_call(
        lamb_maps_kernel,
        in_specs=[pl.BlockSpec(memory_space=pltpu.SMEM)] + [whole_vmem] * 11,
        out_specs=[whole_vmem] * 13,
        out_shape=maps_shapes * 4 + [struct((everywhere, 1, LANES))],
        compiler_params=plain,
        name="lamb_maps",
    )(ids, maps_parts, *flat(masters), *flat(firsts), *flat(seconds), wide[20])
    spread = lax.all_to_all(maps[12], ("dp", "tensor"), 0, 0)
    updates = pl.pallas_call(
        update_kernel,
        in_specs=[whole_vmem] * 9,
        out_specs=[whole_vmem] * 9,
        out_shape=wide_shapes + maps_shapes + [struct((2, 8))],
        compiler_params=plain,
        name="lamb_update",
    )(spread, *wide[15:20], *maps[9:12])

    def joined(kind):
        values = list(wide[5 * kind : 5 * kind + 5]) + list(maps[3 * kind : 3 * kind + 3])
        return tuple(values[:7]) + (values[7][0],)

    return (
        (output, input_grad)
        + joined(0)
        + joined(1)
        + joined(2)
        + tuple(updates[:7])
        + (updates[7][0], updates[8])
    )


WEIGHT_SPECS = (
    P("dp", None, "tensor"),
    P("dp", "tensor"),
    P("dp", "tensor"),
    P(None, "tensor"),
    P(None, "tensor"),
    P(("dp", "tensor"), None),
    P(("dp", "tensor"), None),
    P(("dp", "tensor")),
)


def solution(mesh):
    tokens = P(("dp", "tensor"), None)
    return jax.shard_map(
        local,
        mesh=mesh,
        in_specs=(tokens, tokens, P("dp")) + WEIGHT_SPECS * 3,
        out_specs=(tokens, tokens) + WEIGHT_SPECS * 4 + (P(),),
        check_vma=False,
    )
```

time: 977 us -> 295 us (0.30)
  blocking collectives: 312 us -> 0 us
  waiting for transfers between devices: 255 us -> 91.4 us
  other arithmetic: 155 us -> 23.2 us
  matrix products: 125 us -> 0 us
  Pallas kernels: 0 us -> 93.1 us
  local copies, waits for them, and re-layouts: 92.9 us -> 38.6 us
  starting transfers between devices: 0.42 us -> 44.9 us
  between operations: 29.8 us -> 1.99 us
    reduce_scatter x6 -> x0, waiting for transfers between devices: 255 us -> none  [the longest x1 94.7 us: local(): lax.psum_scatter(state_weight_grad, ('dp', 'tensor'), scatter_dimension=0...]
    all_gather x4 -> x0, blocking collectives: 139 us -> none  [the longest x1 40.9 us: local(): lax.all_gather(state_conv, ('dp', 'tensor'), axis=0, tiled=True)]
    dot_general x26 -> x0, matrix products: 123 us -> none  [the longest x14 55 us: contract(): lax.dot_general(left, right, (((left_dim,), (right_dim,)), ((), ())), pre...]
    pallas_call x0 -> x7, Pallas kernels: none -> 93.1 us  [the longest x1 48.2 us: local(): pl.pallas_call(functools.partial(backward_kernel, width, masks), grid_spe...]
    psum x4 -> x0, blocking collectives: 90.9 us -> none  [the longest x1 41 us: local(): norm_totals = lax.psum(jnp.stack(partials, axis=1), ('dp', 'tensor'))]
    unnamed x2 -> x0, blocking collectives: 81.9 us -> none
    ppermute x0 -> x23, waiting for transfers between devices: none -> 76.6 us  [exchange(): return lax.ppermute(values, axis, [(at, at ^ mask) for at in range(count)])]
    reduce_sum x28 -> x0, other arithmetic: 50.1 us -> none  [the longest x2 13.6 us: causal_conv(): kernel[offset][None, :] * padded[offset:offset + values.shape[0]]]
  transfers between devices with their start and end apart: 10 -> 27, of which waited for: 4 -> 12; matrix products, arithmetic and copies ran while one was open for 25% -> 11% of each run, Pallas kernels for 0% -> 12%
where the time goes in v1:
time: 295 us; the launch traced here: 293 us
  Pallas kernels  93.1 us (32%)
  waiting for transfers between devices  91.4 us (31%)
  starting transfers between devices  44.9 us (15%)
  local copies, waits for them, and re-layouts  38.6 us (13%)
  other arithmetic  23.2 us (8%)
    ppermute x23, waiting for transfers between devices, exchange(): return lax.ppermute(values, axis, [(at, at ^ mask) for at in range(count)])  76.6 us
    pallas_call x1, Pallas kernels, local(): pl.pallas_call(functools.partial(backward_kernel, width, masks), grid_spe...  48.2 us
    pallas_call x1, Pallas kernels, local(): pl.pallas_call(functools.partial(forward_kernel, width, pieces, own_chunk...  28.4 us
    unnamed x129, local copies, waits for them, and re-layouts  25.9 us
    ppermute x23, starting transfers between devices, exchange(): return lax.ppermute(values, axis, [(at, at ^ mask) for at in range(count)])  21.5 us
    all_to_all x1, waiting for transfers between devices, local(): lax.all_to_all(jnp.broadcast_to(out_low[None], (dp_count,) + out_low.shap...  12.8 us
    pallas_call x1, Pallas kernels, local(): pl.pallas_call(middle_kernel, grid_spec=pltpu.PrefetchScalarGridSpec(num_...  10.6 us
    all_to_all x1, starting transfers between devices, local(): lax.all_to_all(jnp.broadcast_to(shared_own[None], (everywhere,) + shared_...  7.3 us
  transfers between devices with their start and end apart: 27, of which 12 were waited for; matrix products, arithmetic and copies ran while one was open for 11% of the time, Pallas kernels for 12%

profile of v1, /device:TPU:0, one launch (start us, length us, event | category | flops | bytes accessed | tf_op | source)
XLA Modules:
  0.0 293.2 jit_solution(12528239403480200120)
XLA Ops:
  4.0 7.3 %all-to-all-start = ((bf16[32,25,256]{2,1,0:T(8,128)(2,1)}), bf16[32,25,256]{2,1,0:T(8,128)(2,1)S(1)}, u32[]{:S(2)}, u32[]{:S(2)}) async-start(bf16[32,25,256]{2,1,0:T(8,128)(2,1)} %broadcast_in_dim.61), calls=%async_computation | async-start | bytes 1048576 | tf_op jit(solution)/shard_map/all_to_all | solution.py:687
  15.0 3.4 %collective-permute-start.10 = (bf16[96,896]{1,0:T(8,128)(2,1)S(1)}, bf16[96,896]{1,0:T(8,128)(2,1)S(1)}, u32[]{:S(2)}, u32[]{:S(2)}) collective-permute-start(bf16[96,896]{1,0:T(8,128)(2,1)S(1)} %fusion.13.refs_0_), channel_id=1, source_target_pairs={{0,24},{4,28},{8,16},{12,20},{16,8},{20,12},{24,0},{28,4},{1,25},{... | collective-permute-start | bytes 516104 | tf_op jit(solution)/shard_map/ppermute | solution.py:44
  21.0 16.2 %collective-permute-done.3 = bf16[512,768]{1,0:T(8,128)(2,1)} collective-permute-done((bf16[512,768]{1,0:T(8,128)(2,1)}, bf16[512,768]{1,0:T(8,128)(2,1)}, u32[]{:S(2)}, u32[]{:S(2)}) %collective-permute-start.3) | collective-permute-done | bytes 786464 | tf_op jit(solution)/shard_map/ppermute | solution.py:44
  44.8 4.1 %collective-permute-done.8.refs_4_ = bf16[96,896]{1,0:T(8,128)(2,1)} collective-permute-done((bf16[96,896]{1,0:T(8,128)(2,1)S(1)}, bf16[96,896]{1,0:T(8,128)(2,1)}, u32[]{:S(2)}, u32[]{:S(2)}) %collective-permute-start.8) | collective-permute-done | bytes 172064 | tf_op jit(solution)/shard_map/ppermute | solution.py:44
  52.1 3.1 %pad_maximum_fusion.u_ref = bf16[4,512,768]{2,1,0:T(8,128)(2,1)} fusion(bf16[1,512,768]{2,1,0:T(8,128)(2,1)} %bitcast.8, bf16[1,512,768]{2,1,0:T(8,128)(2,1)} %bitcast.7, bf16[1,512,768]{2,1,0:T(8,128)(2,1)} %bitcast.6, bf16[1,512,768]{2,1,0:T(8,128)(2,1)S(1)} %bitcast.69), kind=kLoop, calls=%fused_computation | loop fusion | flops 4718592 | bytes 6291456 | tf_op jit(solution)/shard_map/stack | solution.py:677
  56.2 3.7 %collective-permute-done.7.refs_3_ = bf16[96,896]{1,0:T(8,128)(2,1)S(1)} collective-permute-done((bf16[96,896]{1,0:T(8,128)(2,1)S(1)}, bf16[96,896]{1,0:T(8,128)(2,1)S(1)}, u32[]{:S(2)}, u32[]{:S(2)}) %collective-permute-start.7) | collective-permute-done | bytes 172064 | tf_op jit(solution)/shard_map/ppermute | solution.py:44
  59.9 2.4 collective-permute-done.9.refs_5_
  63.0 28.4 %ssd_forward.1 = (bf16[2048,768]{1,0:T(8,128)(2,1)}, f32[2048,384]{1,0:T(8,128)}, f32[2048,640]{1,0:T(8,128)}, f32[2048,640]{1,0:T(8,128)}, bf16[2048,640]{1,0:T...) custom-call(s32[2]{0:T(128)} %pad_add_fusion.ids, ...), custom_call_target="tpu_custom_call" | custom-call | tf_op jit(solution)/shard_map/ssd_forward/pallas_call | solution.py:743
  92.4 5.5 %all-to-all-start.1 = ((bf16[8,96,384]{2,1,0:T(8,128)(2,1)}), bf16[8,96,384]{2,1,0:T(8,128)(2,1)S(1)}, u32[]{:S(2)}, u32[]{:S(2)}) async-start(bf16[8,96,384]{2,1,0:T(8,128)(2,1)} %broadcast_in_dim.63), calls=%async_computation.1 | async-start | bytes 1179648 | tf_op jit(solution)/shard_map/all_to_all | solution.py:708
  98.5 3.1 %pad_maximum_fusion.1.grad_ref = bf16[4,512,768]{2,1,0:T(8,128)(2,1)} fusion(bf16[1,512,768]{2,1,0:T(8,128)(2,1)} %bitcast.15, bf16[1,512,768]{2,1,0:T(8,128)(2,1)S(1)} %bitcast.73, bf16[1,512,768]{2,1,0:T(8,128)(2,1)} %bitcast.4, bf16[1,512,768]{2,1,0:T(8,128)(2,1)S(1)} %bitcast.70), kind=kLoop, calls=%fused_computation.1 | loop fusion | flops 4718592 | bytes 6291456 | tf_op jit(solution)/shard_map/stack | solution.py:792
  101.6 12.8 %all-to-all-done.1 = bf16[8,96,384]{2,1,0:T(8,128)(2,1)S(1)} async-done(((bf16[8,96,384]{2,1,0:T(8,128)(2,1)}), bf16[8,96,384]{2,1,0:T(8,128)(2,1)S(1)}, u32[]{:S(2)}, u32[]{:S(2)}) %all-to-all-start.1) | async-done | bytes 589856 | tf_op jit(solution)/shard_map/all_to_all | solution.py:708
  115.2 10.6 %gate_middle.1 = (f32[2048,384]{1,0:T(8,128)}, bf16[4,512,768]{2,1,0:T(8,128)(2,1)}, f32[2,2048]{1,0:T(2,128)}) custom-call(s32[2]{0:T(128)} %pad_add_fusion.ids, s32[1]{0:T(128)} %copy.108.lengths, bf16[4,512,768]{2,1,0:T(8,128)(2,1)} %pad_maximum_fusion.1.grad_ref, f32[2048,384]{1,0:T(8,128)} %get-tuple-element.96.gate_ref, ...), custom_call_target="tpu_custom_call" | custom-call | tf_op jit(solution)/shard_map/gate_middle/pallas_call | solution.py:799
  128.4 3.4 %collective-permute-done.16 = f32[2,2048]{1,0:T(2,128)S(1)} collective-permute-done((f32[2,2048]{1,0:T(2,128)S(1)}, f32[2,2048]{1,0:T(2,128)S(1)}, u32[]{:S(2)}, u32[]{:S(2)}) %collective-permute-start.16) | collective-permute-done | bytes 16416 | tf_op jit(solution)/shard_map/ppermute | solution.py:44
  132.3 48.2 %ssd_backward.1 = (bf16[4,512,768]{2,1,0:T(8,128)(2,1)}, bf16[8,112,1536]{2,1,0:T(8,128)(2,1)}) custom-call(s32[2]{0:T(128)} %pad_add_fusion.ids, s32[1]{0:T(128)} %copy.108.lengths, f32[2,2048]{1,0:T(2,128)} %add.126.sums_ref, bf16[4,512,768]{2,1,0:T(8,128)(2,1)} %pad_maximum_fusion.u_ref, bf16[4,512,768]{2,1,0:T(8,128)(2,1)} %pad_maximum_fusion.1.grad_ref, ...), custom_call_target="tpu_custom_call" | custom-call | tf_op jit(solution)/shard_map/ssd_backward/pallas_call | solution.py:835
  180.6 2.5 slice.148
  187.5 27.1 %collective-permute-done.19 = bf16[4,112,1536]{2,1,0:T(8,128)(2,1)} collective-permute-done((bf16[4,112,1536]{2,1,0:T(8,128)(2,1)}, bf16[4,112,1536]{2,1,0:T(8,128)(2,1)}, u32[]{:S(2)}, u32[]{:S(2)}) %collective-permute-start.19) | collective-permute-done | bytes 1376288 | tf_op jit(solution)/shard_map/ppermute | solution.py:44
  218.9 2.4 collective-permute-start.22
  226.7 3.9 %collective-permute-done.20.refs_0_ = bf16[112,1536]{1,0:T(8,128)(2,1)S(1)} collective-permute-done((bf16[112,1536]{1,0:T(8,128)(2,1)S(1)}, bf16[112,1536]{1,0:T(8,128)(2,1)S(1)}, u32[]{:S(2)}, u32[]{:S(2)}) %collective-permute-start.20) | collective-permute-done | bytes 344096 | tf_op jit(solution)/shard_map/ppermute | solution.py:44
  230.6 13.6 %collective-permute-done.21.refs_1_ = bf16[112,1536]{1,0:T(8,128)(2,1)S(1)} collective-permute-done((bf16[112,1536]{1,0:T(8,128)(2,1)S(1)}, bf16[112,1536]{1,0:T(8,128)(2,1)S(1)}, u32[]{:S(2)}, u32[]{:S(2)}) %collective-permute-start.21) | collective-permute-done | bytes 344096 | tf_op jit(solution)/shard_map/ppermute | solution.py:44
  244.9 3.5 %all-to-all-start.2 = ((f32[4,32,256]{2,1,0:T(8,128)}), f32[4,32,256]{2,1,0:T(8,128)S(1)}, u32[]{:S(2)}, u32[]{:S(2)}) async-start(f32[4,32,256]{2,1,0:T(8,128)} %pack_maps.1), calls=%async_computation.2 | async-start | bytes 262144 | tf_op jit(solution)/shard_map/all_to_all | solution.py:946
  253.9 2.8 lamb_wide.1
  267.8 7.0 %all-to-all-start.3 = ((f32[32,1,128]{2,1,0:T(1,128)}), f32[32,1,128]{2,1,0:T(1,128)S(1)}, u32[]{:S(2)}, u32[]{:S(2)}) async-start(f32[32,1,128]{2,1,0:T(1,128)} %get-tuple-element.135), calls=%async_computation.3 | async-start | bytes 32768 | tf_op jit(solution)/shard_map/all_to_all | solution.py:971
  286.6 2.7 fusion.1
  289.3 3.9 %fusion.3 = (f32[512,768]{1,0:T(8,128)}, bf16[512,768]{1,0:T(8,128)(2,1)}) fusion(bf16[512,768]{1,0:T(8,128)(2,1)} %param.27, bf16[512,768]{1,0:T(8,128)(2,1)} %param.28, bf16[512,768]{1,0:T(8,128)(2,1)} %collective-permute-done.18, f32[2,512,768]{2,1,0:T(8,128)S(1)} %copy-done.37, f32[512]{0:T(512)S(1)} %get-tuple-element.322, ...), kind=kLoop, calls=%fused_computation.13 | loop fusion | flops 6291456 | bytes 8662528 | tf_op jit(solution)/shard_map/sub | solution.py:930
  (224 shorter events, 69.6 us)
Async XLA Ops:
  4.0 33.2 %all-to-all-start = ((bf16[32,25,256]{2,1,0:T(8,128)(2,1)}), bf16[32,25,256]{2,1,0:T(8,128)(2,1)S(1)}, u32[]{:S(2)}, u32[]{:S(2)}) async-start(bf16[32,25,256]{2,1,0:T(8,128)(2,1)} %broadcast_in_dim.61), calls=%async_computation | async-start | bytes 1048576 | tf_op jit(solution)/shard_map/all_to_all | solution.py:687
  11.3 25.9 %collective-permute-start.3 = (bf16[512,768]{1,0:T(8,128)(2,1)}, bf16[512,768]{1,0:T(8,128)(2,1)}, u32[]{:S(2)}, u32[]{:S(2)}) collective-permute-start(bf16[512,768]{1,0:T(8,128)(2,1)} %param.27), channel_id=1, source_target_pairs={{0,2},{1,3},{2,0},{3,1},{4,6},{5,7},{6,4},{7,5},{8,10},{9,11},{10,... | collective-permute-start | bytes 2359304 | tf_op jit(solution)/shard_map/ppermute | solution.py:44
  15.0 22.3 %collective-permute-start.10 = (bf16[96,896]{1,0:T(8,128)(2,1)S(1)}, bf16[96,896]{1,0:T(8,128)(2,1)S(1)}, u32[]{:S(2)}, u32[]{:S(2)}) collective-permute-start(bf16[96,896]{1,0:T(8,128)(2,1)S(1)} %fusion.13.refs_0_), channel_id=1, source_target_pairs={{0,24},{4,28},{8,16},{12,20},{16,8},{20,12},{24,0},{28,4},{1,25},{... | collective-permute-start | bytes 516104 | tf_op jit(solution)/shard_map/ppermute | solution.py:44
  18.4 24.9 %collective-permute-start.6 = (bf16[96,896]{1,0:T(8,128)(2,1)S(1)}, bf16[96,896]{1,0:T(8,128)(2,1)S(1)}, u32[]{:S(2)}, u32[]{:S(2)}) collective-permute-start(bf16[96,896]{1,0:T(8,128)(2,1)S(1)} %fusion.13.refs_0_), channel_id=1, source_target_pairs={{0,8},{4,12},{8,0},{12,4},{16,24},{20,28},{24,16},{28,20},{1,9},{5... | collective-permute-start | bytes 516104 | tf_op jit(solution)/shard_map/ppermute | solution.py:44
  18.4 31.7 %collective-permute-start.2 = (bf16[512,768]{1,0:T(8,128)(2,1)S(1)}, bf16[512,768]{1,0:T(8,128)(2,1)}, u32[]{:S(2)}, u32[]{:S(2)}) collective-permute-start(bf16[512,768]{1,0:T(8,128)(2,1)S(1)} %copy-done.39), channel_id=1, source_target_pairs={{0,1},{1,0},{2,3},{3,2},{4,5},{5,4},{6,7},{7,6},{8,9},{9,8},{10,11... | collective-permute-start | bytes 2359304 | tf_op jit(solution)/shard_map/ppermute | solution.py:44
  18.4 73.0 %collective-permute-start.1 = (bf16[512,768]{1,0:T(8,128)(2,1)S(1)}, bf16[512,768]{1,0:T(8,128)(2,1)S(1)}, u32[]{:S(2)}, u32[]{:S(2)}) collective-permute-start(bf16[512,768]{1,0:T(8,128)(2,1)S(1)} %copy-done.40), channel_id=1, source_target_pairs={{0,2},{1,3},{2,0},{3,1},{4,6},{5,7},{6,4},{7,5},{8,10},{9,11},{10,... | collective-permute-start | bytes 2359304 | tf_op jit(solution)/shard_map/ppermute | solution.py:44
  37.2 13.7 %collective-permute-start.4 = (bf16[512,768]{1,0:T(8,128)(2,1)}, bf16[512,768]{1,0:T(8,128)(2,1)}, u32[]{:S(2)}, u32[]{:S(2)}) collective-permute-start(bf16[512,768]{1,0:T(8,128)(2,1)} %collective-permute-done.3), channel_id=1, source_target_pairs={{0,1},{1,0},{2,3},{3,2},{4,5},{5,4},{6,7},{7,6},{8,9},{9,8},{10,11... | collective-permute-start | bytes 2359304 | tf_op jit(solution)/shard_map/ppermute | solution.py:44
  37.4 11.5 %collective-permute-start.8 = (bf16[96,896]{1,0:T(8,128)(2,1)S(1)}, bf16[96,896]{1,0:T(8,128)(2,1)}, u32[]{:S(2)}, u32[]{:S(2)}) collective-permute-start(bf16[96,896]{1,0:T(8,128)(2,1)S(1)} %fusion.13.refs_0_), channel_id=1, source_target_pairs={{0,16},{4,20},{8,24},{12,28},{16,0},{20,4},{24,8},{28,12},{1,17},{... | collective-permute-start | bytes 516104 | tf_op jit(solution)/shard_map/ppermute | solution.py:44
  43.3 11.9 %collective-permute-start.5 = (bf16[96,896]{1,0:T(8,128)(2,1)S(1)}, bf16[96,896]{1,0:T(8,128)(2,1)S(1)}, u32[]{:S(2)}, u32[]{:S(2)}) collective-permute-start(bf16[96,896]{1,0:T(8,128)(2,1)S(1)} %fusion.13.refs_0_), channel_id=1, source_target_pairs={{0,4},{4,0},{8,12},{12,8},{16,20},{20,16},{24,28},{28,24},{1,5},{5... | collective-permute-start | bytes 516104 | tf_op jit(solution)/shard_map/ppermute | solution.py:44
  48.9 7.3 %collective-permute-start.11 = (bf16[96,896]{1,0:T(8,128)(2,1)S(1)}, bf16[96,896]{1,0:T(8,128)(2,1)S(1)}, u32[]{:S(2)}, u32[]{:S(2)}) collective-permute-start(bf16[96,896]{1,0:T(8,128)(2,1)S(1)} %collective-permute-done.10.refs_6_), channel_id=1, source_target_pairs={{0,4},{4,0},{8,12},{12,8},{16,20},{20,16},{24,28},{28,24},{1,5},{5... | collective-permute-start | bytes 516104 | tf_op jit(solution)/shard_map/ppermute | solution.py:44
  50.1 9.8 %collective-permute-start.7 = (bf16[96,896]{1,0:T(8,128)(2,1)S(1)}, bf16[96,896]{1,0:T(8,128)(2,1)S(1)}, u32[]{:S(2)}, u32[]{:S(2)}) collective-permute-start(bf16[96,896]{1,0:T(8,128)(2,1)S(1)} %collective-permute-done.6.refs_2_), channel_id=1, source_target_pairs={{0,4},{4,0},{8,12},{12,8},{16,20},{20,16},{24,28},{28,24},{1,5},{5... | collective-permute-start | bytes 516104 | tf_op jit(solution)/shard_map/ppermute | solution.py:44
  50.9 11.3 %collective-permute-start.9 = (bf16[96,896]{1,0:T(8,128)(2,1)}, bf16[96,896]{1,0:T(8,128)(2,1)S(1)}, u32[]{:S(2)}, u32[]{:S(2)}) collective-permute-start(bf16[96,896]{1,0:T(8,128)(2,1)} %collective-permute-done.8.refs_4_), channel_id=1, source_target_pairs={{0,4},{4,0},{8,12},{12,8},{16,20},{20,16},{24,28},{28,24},{1,5},{5... | collective-permute-start | bytes 516104 | tf_op jit(solution)/shard_map/ppermute | solution.py:44
  55.3 43.2 %collective-permute-start = (bf16[512,768]{1,0:T(8,128)(2,1)S(1)}, bf16[512,768]{1,0:T(8,128)(2,1)}, u32[]{:S(2)}, u32[]{:S(2)}) collective-permute-start(bf16[512,768]{1,0:T(8,128)(2,1)S(1)} %copy-done.40), channel_id=1, source_target_pairs={{0,1},{1,0},{2,3},{3,2},{4,5},{5,4},{6,7},{7,6},{8,9},{9,8},{10,11... | collective-permute-start | bytes 2359304 | tf_op jit(solution)/shard_map/ppermute | solution.py:44
  92.4 22.0 %all-to-all-start.1 = ((bf16[8,96,384]{2,1,0:T(8,128)(2,1)}), bf16[8,96,384]{2,1,0:T(8,128)(2,1)S(1)}, u32[]{:S(2)}, u32[]{:S(2)}) async-start(bf16[8,96,384]{2,1,0:T(8,128)(2,1)} %broadcast_in_dim.63), calls=%async_computation.1 | async-start | bytes 1179648 | tf_op jit(solution)/shard_map/all_to_all | solution.py:708
  183.1 31.5 %collective-permute-start.19 = (bf16[4,112,1536]{2,1,0:T(8,128)(2,1)}, bf16[4,112,1536]{2,1,0:T(8,128)(2,1)}, u32[]{:S(2)}, u32[]{:S(2)}) collective-permute-start(bf16[4,112,1536]{2,1,0:T(8,128)(2,1)} %slice.148), channel_id=1, source_target_pairs={{0,4},{4,0},{8,12},{12,8},{16,20},{20,16},{24,28},{28,24},{1,5},{5... | collective-permute-start | bytes 4128776 | tf_op jit(solution)/shard_map/ppermute | solution.py:44
  185.3 36.2 %collective-permute-start.13 = (bf16[2,512,768]{2,1,0:T(8,128)(2,1)S(1)}, bf16[2,512,768]{2,1,0:T(8,128)(2,1)S(1)}, u32[]{:S(2)}, u32[]{:S(2)}) collective-permute-start(bf16[2,512,768]{2,1,0:T(8,128)(2,1)S(1)} %pad_maximum_fusion.3), channel_id=1, source_target_pairs={{0,1},{1,0},{2,3},{3,2},{4,5},{5,4},{6,7},{7,6},{8,9},{9,8},{10,11... | collective-permute-start | bytes 4718600 | tf_op jit(solution)/shard_map/ppermute | solution.py:44
  187.4 34.5 %collective-permute-start.17 = (bf16[2,512,768]{2,1,0:T(8,128)(2,1)S(1)}, bf16[2,512,768]{2,1,0:T(8,128)(2,1)S(1)}, u32[]{:S(2)}, u32[]{:S(2)}) collective-permute-start(bf16[2,512,768]{2,1,0:T(8,128)(2,1)S(1)} %pad_maximum_fusion.4), channel_id=1, source_target_pairs={{0,1},{1,0},{2,3},{3,2},{4,5},{5,4},{6,7},{7,6},{8,9},{9,8},{10,11... | collective-permute-start | bytes 4718600 | tf_op jit(solution)/shard_map/ppermute | solution.py:44
  216.9 13.8 %collective-permute-start.20 = (bf16[112,1536]{1,0:T(8,128)(2,1)S(1)}, bf16[112,1536]{1,0:T(8,128)(2,1)S(1)}, u32[]{:S(2)}, u32[]{:S(2)}) collective-permute-start(bf16[112,1536]{1,0:T(8,128)(2,1)S(1)} %get-tuple-element.307), channel_id=1, source_target_pairs={{0,8},{4,12},{8,0},{12,4},{16,24},{20,28},{24,16},{28,20},{1,9},{5... | collective-permute-start | bytes 1032200 | tf_op jit(solution)/shard_map/ppermute | solution.py:44
  217.5 26.6 %collective-permute-start.21 = (bf16[112,1536]{1,0:T(8,128)(2,1)S(1)}, bf16[112,1536]{1,0:T(8,128)(2,1)S(1)}, u32[]{:S(2)}, u32[]{:S(2)}) collective-permute-start(bf16[112,1536]{1,0:T(8,128)(2,1)S(1)} %get-tuple-element.306), channel_id=1, source_target_pairs={{0,16},{4,20},{8,24},{12,28},{16,0},{20,4},{24,8},{28,12},{1,17},{... | collective-permute-start | bytes 1032200 | tf_op jit(solution)/shard_map/ppermute | solution.py:44
  218.9 25.3 %collective-permute-start.22 = (bf16[112,1536]{1,0:T(8,128)(2,1)S(1)}, bf16[112,1536]{1,0:T(8,128)(2,1)S(1)}, u32[]{:S(2)}, u32[]{:S(2)}) collective-permute-start(bf16[112,1536]{1,0:T(8,128)(2,1)S(1)} %get-tuple-element.305), channel_id=1, source_target_pairs={{0,24},{4,28},{8,16},{12,20},{16,8},{20,12},{24,0},{28,4},{1,25},{... | collective-permute-start | bytes 1032200 | tf_op jit(solution)/shard_map/ppermute | solution.py:44
  223.6 63.0 %collective-permute-start.18 = (bf16[512,768]{1,0:T(8,128)(2,1)}, bf16[512,768]{1,0:T(8,128)(2,1)}, u32[]{:S(2)}, u32[]{:S(2)}) collective-permute-start(bf16[512,768]{1,0:T(8,128)(2,1)} %fusion.11), channel_id=1, source_target_pairs={{0,2},{1,3},{2,0},{3,1},{4,6},{5,7},{6,4},{7,5},{8,10},{9,11},{10,... | collective-permute-start | bytes 2359304 | tf_op jit(solution)/shard_map/ppermute | solution.py:44
  224.9 64.4 %collective-permute-start.14 = (bf16[512,768]{1,0:T(8,128)(2,1)}, bf16[512,768]{1,0:T(8,128)(2,1)}, u32[]{:S(2)}, u32[]{:S(2)}) collective-permute-start(bf16[512,768]{1,0:T(8,128)(2,1)} %fusion.10), channel_id=1, source_target_pairs={{0,2},{1,3},{2,0},{3,1},{4,6},{5,7},{6,4},{7,5},{8,10},{9,11},{10,... | collective-permute-start | bytes 2359304 | tf_op jit(solution)/shard_map/ppermute | solution.py:44
  244.9 16.7 %all-to-all-start.2 = ((f32[4,32,256]{2,1,0:T(8,128)}), f32[4,32,256]{2,1,0:T(8,128)S(1)}, u32[]{:S(2)}, u32[]{:S(2)}) async-start(f32[4,32,256]{2,1,0:T(8,128)} %pack_maps.1), calls=%async_computation.2 | async-start | bytes 262144 | tf_op jit(solution)/shard_map/all_to_all | solution.py:946
  267.8 14.1 %all-to-all-start.3 = ((f32[32,1,128]{2,1,0:T(1,128)}), f32[32,1,128]{2,1,0:T(1,128)S(1)}, u32[]{:S(2)}, u32[]{:S(2)}) async-start(f32[32,1,128]{2,1,0:T(1,128)} %get-tuple-element.135), calls=%async_computation.3 | async-start | bytes 32768 | tf_op jit(solution)/shard_map/all_to_all | solution.py:971
  (63 other events, 721.5 us)

commit v2 on v1

--- a/solution.py
+++ b/solution.py
@@ -16,6 +16,7 @@
 MAPS = 2 * STATE
 LANES = 128
 SMALL = 16
+VMEM = 60 * 1024 * 1024
 
 EPSILON = 1e-05
 ADAM_EPSILON = 1e-06
@@ -51,11 +52,18 @@
     return low
 
 
-def gather_pieces(own, axis, low):
+def together(*values):
+    return lax.optimization_barrier(values)
+
+
+def gather_far(own, axis, low):
+    return {high: exchange(own, axis, high) for high in range(low, lax.axis_size(axis), low)}
+
+
+def gather_near(own, far, axis, low):
     count = lax.axis_size(axis)
-    pieces = {0: own}
-    for high in range(low, count, low):
-        pieces[high] = exchange(own, axis, high)
+    pieces = dict(far)
+    pieces[0] = own
     for high in range(0, count, low):
         for near in range(1, low):
             pieces[high + near] = exchange(pieces[high], axis, near)
@@ -66,29 +74,20 @@
     return [high + near for near in range(low) for high in range(0, count, low)]
 
 
-def scatter_parts(slots, axis, low, small=0):
-    count = lax.axis_size(axis)
-    highs = count // low
-    total = slots[:highs].astype(F32)
+def near_sum(kept, sent, axis, low):
+    highs = kept.shape[0]
+    total = kept.astype(F32)
     for near in range(1, low):
-        sent = slots[near * highs : (near + 1) * highs]
-        total = total + exchange(sent, axis, near).astype(F32)
-    if small > 0:
-        joined = total[:, :small] + total[:, small : 2 * small]
-        high = lax.reduce_precision(joined, 8, 7)
-        total = jnp.concatenate([high, joined - high, total[:, 2 * small :]], axis=1)
-    received = [
-        exchange(total[position].astype(slots.dtype), axis, position * low)
-        for position in range(1, highs)
+        part = sent if low == 2 else sent[(near - 1) * highs : near * highs]
+        total = total + exchange(part, axis, near).astype(F32)
+    return total
+
+
+def far_parts(total, axis, low):
+    return [
+        exchange(total[position].astype(BF), axis, position * low)
+        for position in range(1, total.shape[0])
     ]
-    return total[0], received
-
-
-def scatter_sum(slots, axis, low):
-    kept, received = scatter_parts(slots, axis, low)
-    for values in received:
-        kept = kept + values.astype(F32)
-    return kept
 
 
 def lane_ids(shape):
@@ -138,12 +137,12 @@
     return 1.0 / (1.0 + jnp.exp(-values))
 
 
-def forward_kernel(
-    channels, pieces, blocks_per, ids, u_ref, *refs
-):
+def forward_kernel(channels, pieces, masks, owners, own_chunks, ids, *refs):
     width = channels
     heads = width // HEAD
     mixed_width = width + MAPS
+    u_refs = refs[:owners]
+    refs = refs[owners:]
     piece_refs = refs[:pieces]
     (
         state_w_ref,
@@ -162,17 +161,25 @@
         weight_ref,
         tail,
         carried,
+        u_own,
     ) = refs[pieces:]
     at = pl.program_id(0)
 
     @pl.when(at == 0)
     def _():
-        rows = weight_ref.shape[0] // pieces
-        for mask in range(pieces):
-            block = ids[0] ^ mask if pieces > 1 else 0
-            where_ = pl.ds(pl.multiple_of(block * rows, 8), rows) if pieces > 1 else slice(None)
-            weight_ref[where_, : 2 * width] = piece_refs[mask][:, : 2 * width]
-            weight_ref[where_, 2 * width + MAPS :] = piece_refs[mask][:, 2 * width :]
+        place_rows(
+            ids,
+            masks,
+            piece_refs,
+            (
+                (slice(0, 2 * width), weight_ref, slice(0, 2 * width)),
+                (
+                    slice(2 * width, 2 * width + LANES),
+                    weight_ref,
+                    slice(2 * width + MAPS, 2 * width + MAPS + LANES),
+                ),
+            ),
+        )
         weight_ref[:, 2 * width : 2 * width + MAPS] = state_w_ref[...]
 
     @pl.when(at % (LMAX // SPAN) == 0)
@@ -180,7 +187,8 @@
         tail[0:8, :] = jnp.zeros((8, mixed_width), F32)
         carried[...] = jnp.zeros_like(carried)
 
-    inputs = u_ref[0].astype(F32)
+    pick_piece(ids, at, own_chunks, u_refs, u_own)
+    inputs = u_own[...].astype(F32)
     scale = lax.rsqrt(jnp.mean(inputs * inputs, axis=-1, keepdims=True) + EPSILON)
     normed = (inputs * scale * gain_ref[0:1, :]).astype(BF)
     normed_ref[...] = normed
@@ -238,17 +246,76 @@
         carried[rows, :] = kept_rate[:, head : head + 1] * state[rows, :] + fresh[rows, :]
 
 
+def place_rows(ids, masks, refs, stores):
+    at = 0
+    for ref in refs:
+        stacked = len(ref.shape) == 3
+        for inner in range(ref.shape[0] if stacked else 1):
+            rows = ref.shape[-2]
+            if masks[at] is None:
+                target = slice(None)
+            else:
+                target = pl.ds(pl.multiple_of((ids[0] ^ masks[at]) * rows, 8), rows)
+            for columns, into, lanes in stores:
+                into[target, lanes] = ref[inner, :, columns] if stacked else ref[:, columns]
+            at += 1
+
+
+def pick_piece(ids, block, own_chunks, refs, scratch):
+    mask = (block // own_chunks) ^ ids[1]
+    for at, ref in enumerate(refs):
+
+        @pl.when(mask == at)
+        def _():
+            scratch[...] = ref[...]
+
+
+def store_part(ids, block, own_chunks, refs, value):
+    odd = ((block // own_chunks) ^ ids[1]) & 1
+    for at, ref in enumerate(refs):
+
+        @pl.when(odd == at)
+        def _():
+            ref[0] = value
+
+
 def rows_live(ids, at, lengths):
     sequence = at // (LMAX // SPAN)
     position = (at % (LMAX // SPAN)) * SPAN + lax.broadcasted_iota(jnp.int32, (SPAN, 1), 0)
     return position < lengths[sequence]
 
 
-def middle_kernel(ids, lengths, grad_ref, gate_ref, mixed_ref, *refs):
-    weight, gain_ref, merged_grad_ref, branch_ref, sums_ref = refs
+def middle_kernel(owners, pieces, masks, own_chunks, ids, lengths, *refs):
+    grad_refs = refs[:owners]
+    piece_refs = refs[owners : owners + pieces]
+    (
+        gate_ref,
+        mixed_ref,
+        gain_ref,
+        merged_grad_ref,
+        kept_ref,
+        sent_ref,
+        sums_ref,
+        grad_own,
+        weight,
+    ) = refs[owners + pieces :]
     at = pl.program_id(0)
 
-    upstream = grad_ref[0]
+    @pl.when(at == 0)
+    def _():
+        at_mask = 0
+        for ref in piece_refs:
+            count = ref.shape[0] if len(ref.shape) == 3 else 1
+            place_rows(
+                ids,
+                masks[at_mask : at_mask + count],
+                [ref],
+                ((slice(ref.shape[-1] - weight.shape[1], ref.shape[-1]), weight, slice(None)),),
+            )
+            at_mask += count
+
+    pick_piece(ids, at, own_chunks, grad_refs, grad_own)
+    upstream = grad_own[...]
     upstream = jnp.where(rows_live(ids, at, lengths), upstream, jnp.zeros_like(upstream))
     merged_grad = dot(upstream, weight[...])
     merged_grad_ref[...] = merged_grad
@@ -257,20 +324,31 @@
     gained = gated * gain_ref[0:1, :]
     squares = jnp.sum(gated * gated, axis=1, keepdims=True)
     products = jnp.sum(merged_grad * gained, axis=1, keepdims=True)
-    branch_ref[0] = dot(gained.astype(BF), weight[...], 1, 1).astype(BF)
+    branch = dot(gained.astype(BF), weight[...], 1, 1).astype(BF)
+    store_part(ids, at, own_chunks, (kept_ref, sent_ref), branch)
     lanes = lane_ids((SPAN, LANES))
     both = jnp.where(lanes == 0, squares, jnp.where(lanes == 1, products, 0.0))
     sums_ref[...] = jnp.transpose(both)[0:2, :]
 
 
-def backward_kernel(
+def backward_kernel(channels, masks, owners, own_chunks, ids, lengths, *refs):
+    u_refs = refs[:owners]
+    grad_refs = refs[owners : 2 * owners]
+    sums_refs = refs[2 * owners : 3 * owners]
+    backward_step(
+        channels, masks, own_chunks, ids, lengths, u_refs, grad_refs, sums_refs, *refs[3 * owners :]
+    )
+
+
+def backward_step(
     channels,
     masks,
+    own_chunks,
     ids,
     lengths,
+    u_refs,
+    grad_refs,
     sums_ref,
-    u_ref,
-    grad_ref,
     normed_ref,
     gate_ref,
     mixed_ref,
@@ -286,8 +364,42 @@
     heads_ref,
     skip_ref,
     gain_ref,
-    part_ref,
-    slots_ref,
+    part_kept_ref,
+    part_sent_ref,
+    first_kept_ref,
+    first_sent_ref,
+    *refs,
+):
+    low = low_count(len(masks))
+    second_refs = refs[: len(masks) // low]
+    backward_body(
+        channels,
+        masks,
+        own_chunks,
+        ids,
+        lengths,
+        u_refs,
+        grad_refs,
+        (sums_ref, normed_ref, gate_ref, mixed_ref, merged_grad_ref, raw_ref, pre_ref, act_ref),
+        (step_ref, state_ref, state_next_ref, weight_ref, taps_ref, heads_ref, skip_ref, gain_ref),
+        (part_kept_ref, part_sent_ref),
+        (first_kept_ref, first_sent_ref, second_refs),
+        *refs[len(masks) // low :],
+    )
+
+
+def backward_body(
+    channels,
+    masks,
+    own_chunks,
+    ids,
+    lengths,
+    u_refs,
+    grad_refs,
+    token_refs,
+    other_refs,
+    part_refs,
+    slot_refs,
     carried,
     ahead,
     weight_sum,
@@ -295,7 +407,12 @@
     tap_sum,
     head_sum,
     gain_sum,
+    u_own,
+    grad_own,
 ):
+    sums_ref, normed_ref, gate_ref, mixed_ref, merged_grad_ref, raw_ref, pre_ref, act_ref = token_refs
+    step_ref, state_ref, state_next_ref, weight_ref, taps_ref, heads_ref, skip_ref, gain_ref = other_refs
+    first_kept_ref, first_sent_ref, second_refs = slot_refs
     width = channels
     heads = width // HEAD
     mixed_width = width + MAPS
@@ -315,7 +432,9 @@
         carried[...] = jnp.zeros_like(carried)
         ahead[SPAN:, :] = jnp.zeros((8, mixed_width), F32)
 
-    sums = sums_ref[...]
+    pick_piece(ids, at, own_chunks, u_refs, u_own)
+    pick_piece(ids, at, own_chunks, grad_refs, grad_own)
+    sums = sum(ref[...] for ref in sums_ref)
     scale_row = lax.rsqrt(sums[0:1, :] / INNER + EPSILON)
     cross_row = scale_row * scale_row * scale_row * (sums[1:2, :] / INNER)
     row_ids = lax.broadcasted_iota(jnp.int32, (LANES, SPAN), 0)
@@ -333,7 +452,7 @@
     scaled = gated * gate_scale
     tap_sum[5:6, :width] += jnp.sum(merged_grad * scaled, axis=0, keepdims=True)
     merged = (scaled * gain).astype(BF)
-    upstream = grad_ref[0]
+    upstream = grad_own[...]
     upstream = jnp.where(rows_live(ids, at, lengths), upstream, jnp.zeros_like(upstream))
     out_sum[...] += dot(upstream, merged, 0, 0)
     gated_grad = gate_scale * (merged_grad * gain) - gated * cross
@@ -457,17 +576,21 @@
     normed = normed_ref[...]
     weight_sum[...] += dot(normed, low, 0, 0)
     part = dot(low, weight_ref[...], 1, 1)
-    part_ref[0] = part.astype(BF)
-    inputs = u_ref[0].astype(F32)
+    store_part(ids, at, own_chunks, part_refs, part.astype(BF))
+    inputs = u_own[...].astype(F32)
     scale = lax.rsqrt(jnp.mean(inputs * inputs, axis=-1, keepdims=True) + EPSILON)
     gain_sum[0:1, :] += jnp.sum(part * (inputs * scale), axis=0, keepdims=True)
 
     @pl.when(step_at == pl.num_programs(0) - 1)
     def _():
-        columns_in = weight_sum.shape[1]
         rows = weight_sum.shape[0] // len(masks)
-        channel_count = rows * len(masks)
-        for position, mask in enumerate(masks):
+        model = weight_sum.shape[0]
+        first = first_kept_ref.shape[2]
+        kept_count = first_kept_ref.shape[0]
+        step_lanes = weight_sum.shape[1] - first
+        for place, mask in enumerate(masks):
+            first_ref = first_kept_ref if place < kept_count else first_sent_ref
+            position = place if place < kept_count else place - kept_count
             block = ids[0] ^ mask
             small = jnp.concatenate(
                 [
@@ -476,20 +599,21 @@
                     pltpu.roll(
                         tap_sum[:, width:], (MAPS - block * (MAPS // len(masks))) % MAPS, 1
                     )[:, :LANES],
-                    pltpu.roll(gain_sum[...], (channel_count - block * rows) % channel_count, 1)[
-                        :, :LANES
-                    ],
+                    pltpu.roll(gain_sum[...], (model - block * rows) % model, 1)[:, :LANES],
                 ],
                 axis=1,
             )
             both = jnp.concatenate(halves(small), axis=0)
             picked = pl.ds(pl.multiple_of(block * rows, 8), rows)
-            slots_ref[position, 0:SMALL, : both.shape[1]] = both
-            slots_ref[position, 0:SMALL, both.shape[1] :] = jnp.zeros(
-                (SMALL, slots_ref.shape[2] - both.shape[1]), BF
+            first_ref[position, 0:SMALL, : both.shape[1]] = both
+            first_ref[position, 0:SMALL, both.shape[1] :] = jnp.zeros(
+                (SMALL, first - both.shape[1]), BF
             )
-            slots_ref[position, SMALL:, :columns_in] = weight_sum[picked, :].astype(BF)
-            slots_ref[position, SMALL:, columns_in:] = out_sum[picked, :].astype(BF)
+            first_ref[position, SMALL:, :] = weight_sum[picked, :first].astype(BF)
+            second_ref = second_refs[place % kept_count]
+            near = place // kept_count
+            second_ref[near, :, :step_lanes] = weight_sum[picked, first:].astype(BF)
+            second_ref[near, :, step_lanes:] = out_sum[picked, :].astype(BF)
 
 
 def pad_to(values, axis, size):
@@ -536,7 +660,7 @@
     )
 
 
-def pack_kernel(width, tensor_count, kept_ref, *refs):
+def pack_kernel(width, tensor_count, ids, kept_ref, *refs):
     received = refs[:-1]
     packed_ref = refs[-1]
     maps_rows = packed_ref.shape[1] - 8
@@ -552,21 +676,19 @@
         packed_ref[at, 8:, :] = state[at * maps_rows : (at + 1) * maps_rows, :]
 
 
-def lamb_wide_kernel(width, channels, heads, copies, count, kept_ref, *refs):
-    received = refs[:count]
+def lamb_wide_kernel(width, channels, heads, copies, firsts, seconds, ids, *refs):
+    whole = sum(ref[...].astype(F32) for ref in refs[:firsts])
+    rest = sum(ref[...].astype(F32) for ref in refs[firsts : firsts + seconds])
+    count = firsts + seconds
     olds = refs[count : count + 15]
     outs = refs[count + 15 : count + 35]
     norms_ref = refs[count + 35]
-    whole = kept_ref[...]
-    for ref in received:
-        whole = whole + ref[...].astype(F32)
-    columns = 2 * width + MAPS + LANES
     block = whole[SMALL:]
     small = whole[:8] + whole[8:SMALL]
     norms = jnp.zeros((1, LANES), F32)
     in_grad = jnp.stack([block[:, :channels], block[:, width : width + channels]], axis=1)
-    step_grad = block[:, 2 * width + MAPS : 2 * width + MAPS + heads]
-    out_grad = block[:, columns : columns + channels]
+    step_grad = jnp.transpose(rest[:, :LANES])[:heads]
+    out_grad = rest[:, LANES : LANES + channels]
     channel_grad = small[: CONV + 2, :channels]
     picker = (
         lax.broadcasted_iota(jnp.int32, (width, LANES), 0) // HEAD
@@ -614,7 +736,7 @@
     norms_ref[...] = jnp.broadcast_to(norms[None], norms_ref.shape)
 
 
-def update_kernel(norms_ref, *refs):
+def update_kernel(ids, norms_ref, *refs):
     norms = jnp.sqrt(jnp.sum(norms_ref[...], axis=0))
     refs[-1][...] = jnp.concatenate([norms[:, :8], norms[:, 8:16]], axis=0)
     for position in range(8):
@@ -674,8 +796,19 @@
         axis=1,
     )
     out_low = pad_to(out_proj.astype(BF), 1, width)
-    u_pieces = jnp.stack(gather_pieces(block_input, "tensor", 2))
-    in_pieces = gather_pieces(in_low, "dp", dp_low)
+    both_low = jnp.concatenate([in_low, out_low], axis=1)
+    split = in_low.shape[1]
+    highs = list(range(dp_low, dp_count, dp_low))
+    nears = list(range(1, dp_low))
+    tensor_highs = list(range(2, tensor_count, 2))
+    landed = together(
+        *[exchange(block_input, "tensor", mask) for mask in tensor_highs],
+        *[exchange(both_low, "dp", mask) for mask in highs],
+        *[exchange(both_low, "dp", mask) for mask in nears],
+    )
+    u_far = dict(zip(tensor_highs, landed))
+    both_far = list(landed[len(tensor_highs) : len(tensor_highs) + len(highs)])
+    both_near = list(landed[len(tensor_highs) + len(highs) :])
     maps_rows = state_proj.shape[0]
     conv_rows = state_conv.shape[0]
     small_own = jnp.concatenate(
@@ -684,12 +817,38 @@
     shared_own = jnp.concatenate(
         [state_proj.astype(BF), pad_to(small_own, 0, MAPS)[None, :]], axis=0
     )
+    shared_own, *both_far = together(shared_own, *both_far)
+    in_stack = jnp.stack([piece[:, :split] for piece in both_far])
+    out_stack = jnp.stack([piece[:, split:] for piece in both_far])
     shared = lax.all_to_all(
         jnp.broadcast_to(shared_own[None], (everywhere,) + shared_own.shape),
         ("dp", "tensor"),
         0,
         0,
     )
+    u_pieces = gather_near(block_input, u_far, "tensor", 2)
+    shared, *landed = together(
+        shared, *u_pieces[1:], *[exchange(in_stack, "dp", near) for near in nears]
+    )
+    u_pieces = [block_input] + landed[: tensor_count - 1]
+    in_near = landed[tensor_count - 1 :]
+    grad_own, out_stack, *_ = together(output_grad, out_stack, u_far[2])
+    grad_far = gather_far(grad_own, "tensor", 2)
+    out_near = [exchange(out_stack, "dp", near) for near in nears]
+    in_pieces = [both_low] + both_near + both_far + in_near
+    piece_masks = [0] + nears + highs + [high + near for near in nears for high in highs]
+    direct = rows % 16 == 0
+    if not direct:
+        order = dp_at ^ jnp.arange(dp_count)
+        order = jnp.array([piece_masks.index(mask) for mask in range(dp_count)])[order]
+
+        def ordered(pieces):
+            parts = [piece if piece.ndim == 3 else piece[None] for piece in pieces]
+            return jnp.concatenate(parts, axis=0)[order].reshape(model, -1)
+
+        in_pieces = [
+            ordered([piece[:, :split] for piece in [both_low] + both_near + both_far] + in_near)
+        ]
     state_weight = shared[:, :maps_rows].reshape(-1, MAPS)
     small_all = shared[:, maps_rows].astype(F32)
     conv_size = conv_rows * (CONV + 1)
@@ -702,17 +861,6 @@
         small_all[:, gain_base + part * gain_size : gain_base + (part + 1) * gain_size]
         for part in range(3)
     ).reshape(-1)
-    grad_far = {
-        high: exchange(output_grad, "tensor", high) for high in range(2, tensor_count, 2)
-    }
-    out_spread = lax.all_to_all(
-        jnp.broadcast_to(out_low[None], (dp_count,) + out_low.shape), "dp", 0, 0
-    ).reshape(model, width)
-    if rows % 16 != 0:
-        order = dp_at ^ jnp.arange(dp_count)
-        in_pieces = [jnp.stack(in_pieces)[order].reshape(model, -1)]
-    pieces = len(in_pieces)
-
     channel_wide = pad_to(channel_params, 1, width)
     taps = pad_to(
         jnp.concatenate([channel_wide[: CONV + 1], conv_whole.T], axis=1), 0, 8
@@ -727,25 +875,52 @@
             return pl.BlockSpec((SPAN, size), lambda at, *_: (chunks - 1 - at, 0))
         return pl.BlockSpec((SPAN, size), lambda at, *_: (at, 0))
 
-    def piece_spec(reverse=False):
-        def index(at, ids_ref, *_):
-            block = chunks - 1 - at if reverse else at
-            return ((block // own_chunks) ^ ids_ref[1], block % own_chunks, 0)
-
-        return pl.BlockSpec((1, SPAN, model), index)
+    def piece_specs(reverse=False):
+        def spec(mask):
+            def index(at, ids_ref, *_):
+                block = chunks - 1 - at if reverse else at
+                mine = (block // own_chunks) ^ ids_ref[1] == mask
+                return (jnp.where(mine, block % own_chunks, 0), 0)
+
+            return pl.BlockSpec((SPAN, model), index)
+
+        return [spec(mask) for mask in range(tensor_count)]
+
+    def part_specs(reverse=False):
+        def spec(odd):
+            def index(at, ids_ref, *_):
+                block = chunks - 1 - at if reverse else at
+                owner = block // own_chunks
+                inner = block % own_chunks
+                mine = ((owner ^ ids_ref[1]) & 1) == odd
+                if reverse:
+                    other = jnp.where(owner > 0, owner - 1, 1)
+                    other_inner = jnp.where(owner > 0, own_chunks - 1, 0)
+                else:
+                    last = tensor_count - 1
+                    other = jnp.where(owner < last, owner + 1, last - 1)
+                    other_inner = jnp.where(owner < last, 0, own_chunks - 1)
+                owner = jnp.where(mine, owner, other)
+                return ((owner ^ ids_ref[1]) >> 1, jnp.where(mine, inner, other_inner), 0)
+
+            return pl.BlockSpec((1, SPAN, model), index)
+
+        return [spec(0), spec(1)]
 
     def struct(shape, dtype=F32):
         return jax.ShapeDtypeStruct(shape, dtype)
 
     arbitrary = pltpu.CompilerParams(
-        dimension_semantics=("arbitrary",), vmem_limit_bytes=56 * 1024 * 1024
-    )
+        dimension_semantics=("arbitrary",), vmem_limit_bytes=VMEM
+    )
+    if not direct:
+        piece_masks = [None]
     normed, gate_raw, raw, pre, act, step_in, states, mixed, weight = pl.pallas_call(
-        functools.partial(forward_kernel, width, pieces, own_chunks),
+        functools.partial(forward_kernel, width, len(in_pieces), piece_masks, tensor_count, own_chunks),
         grid_spec=pltpu.PrefetchScalarGridSpec(
             num_scalar_prefetch=1,
             grid=(chunks,),
-            in_specs=[piece_spec()]
+            in_specs=piece_specs()
             + [whole_spec(piece.shape) for piece in in_pieces]
             + [
                 whole_spec(state_weight.shape),
@@ -768,6 +943,7 @@
             scratch_shapes=[
                 pltpu.VMEM((SPAN + 8, mixed_width), F32),
                 pltpu.VMEM((width, STATE), F32),
+                pltpu.VMEM((SPAN, model), BF),
             ],
         ),
         out_shape=[
@@ -783,64 +959,66 @@
         ],
         compiler_params=arbitrary,
         name="ssd_forward",
-    )(ids, u_pieces, *in_pieces, state_weight, gain_rows, taps, heads_wide, skip_gain)
-
-    masks_far = list(grad_far)
-    *far, gate_raw = lax.optimization_barrier([grad_far[mask] for mask in masks_far] + [gate_raw])
-    grad_far = dict(zip(masks_far, far))
-    grad_far[0] = output_grad
-    grad_pieces = jnp.stack(
-        [
-            exchange(grad_far[mask & ~1], "tensor", 1) if mask & 1 else grad_far[mask]
-            for mask in range(tensor_count)
+    )(ids, *u_pieces, *in_pieces, state_weight, gain_rows, taps, heads_wide, skip_gain)
+
+    gate_raw, *landed = together(gate_raw, *grad_far.values(), *out_near)
+    grad_far = dict(zip(grad_far, landed))
+    out_near = landed[len(grad_far) :]
+    grad_pieces = gather_near(grad_own, grad_far, "tensor", 2)
+    out_pieces = [both_low] + both_near + both_far + out_near
+    if not direct:
+        out_pieces = [
+            ordered([piece[:, split:] for piece in [both_low] + both_near + both_far] + out_near)
         ]
-    )
     gate_gain_rows = pad_to(channel_wide[CONV + 1][None, :], 0, 8)
-    merged_grad, branch_part, sums_part = pl.pallas_call(
-        middle_kernel,
+    merged_grad, *branch_parts, sums_part = pl.pallas_call(
+        functools.partial(middle_kernel, tensor_count, len(out_pieces), piece_masks, own_chunks),
         grid_spec=pltpu.PrefetchScalarGridSpec(
             num_scalar_prefetch=2,
             grid=(chunks,),
             in_specs=[
-                piece_spec(),
+                *piece_specs(),
+                *[whole_spec(piece.shape) for piece in out_pieces],
                 token_spec(width),
                 token_spec(width),
-                whole_spec(out_spread.shape),
                 whole_spec(gate_gain_rows.shape),
             ],
             out_specs=[
                 token_spec(width),
-                piece_spec(),
+                *part_specs(),
                 pl.BlockSpec((2, SPAN), lambda at, *_: (0, at)),
             ],
+            scratch_shapes=[pltpu.VMEM((SPAN, model), BF), pltpu.VMEM((model, width), BF)],
         ),
         out_shape=[
             struct((tokens, width)),
-            struct((tensor_count, own_count, model), BF),
+            *[struct((tensor_count // 2, own_count, model), BF)] * 2,
             struct((2, tokens)),
         ],
         compiler_params=arbitrary,
         name="gate_middle",
-    )(ids, lengths, grad_pieces, gate_raw, mixed, out_spread, gate_gain_rows)
-
-    sums = sums_part
-    bit = 1
-    while bit < tensor_count:
-        sums = sums + exchange(sums, "tensor", bit)
-        bit *= 2
-
+    )(ids, lengths, *grad_pieces, *out_pieces, gate_raw, mixed, gate_gain_rows)
+
+    branch_total = near_sum(*branch_parts, "tensor", 2)
+    branch_total, *sums = together(
+        branch_total, *[exchange(sums_part, "tensor", mask) for mask in range(1, tensor_count)]
+    )
+    sums = [sums_part] + sums
+    branch_far = far_parts(branch_total, "tensor", 2)
     masks = slot_masks(dp_count, dp_low)
-    slot_columns = columns + width
+    first_columns = 2 * width + MAPS
+    second_columns = LANES + width
+    kept_slots = dp_count // dp_low
     token_back = functools.partial(token_spec, reverse=True)
-    normed_part, slots = pl.pallas_call(
-        functools.partial(backward_kernel, width, masks),
+    normed_kept, normed_sent, first_kept, first_sent, *seconds_out = pl.pallas_call(
+        functools.partial(backward_kernel, width, masks, tensor_count, own_chunks),
         grid_spec=pltpu.PrefetchScalarGridSpec(
             num_scalar_prefetch=2,
             grid=(chunks,),
             in_specs=[
-                pl.BlockSpec((2, SPAN), lambda at, *_: (0, chunks - 1 - at)),
-                piece_spec(True),
-                piece_spec(True),
+                *piece_specs(True),
+                *piece_specs(True),
+                *[pl.BlockSpec((2, SPAN), lambda at, *_: (0, chunks - 1 - at))] * tensor_count,
                 token_back(model),
                 token_back(width),
                 token_back(width),
@@ -860,8 +1038,10 @@
                 whole_spec(gain_rows.shape),
             ],
             out_specs=[
-                piece_spec(True),
-                whole_spec((dp_count, SMALL + rows, slot_columns)),
+                *part_specs(True),
+                whole_spec((kept_slots, SMALL + rows, first_columns)),
+                whole_spec((dp_count - kept_slots, SMALL + rows, first_columns)),
+                *[whole_spec((dp_low, rows, second_columns))] * kept_slots,
             ],
             scratch_shapes=[
                 pltpu.VMEM((width, STATE), F32),
@@ -871,20 +1051,24 @@
                 pltpu.VMEM((8, mixed_width), F32),
                 pltpu.VMEM((8, LANES), F32),
                 pltpu.VMEM((8, model), F32),
+                pltpu.VMEM((SPAN, model), BF),
+                pltpu.VMEM((SPAN, model), BF),
             ],
         ),
         out_shape=[
-            struct((tensor_count, own_count, model), BF),
-            struct((dp_count, SMALL + rows, slot_columns), BF),
+            *[struct((tensor_count // 2, own_count, model), BF)] * 2,
+            struct((kept_slots, SMALL + rows, first_columns), BF),
+            struct((dp_count - kept_slots, SMALL + rows, first_columns), BF),
+            *[struct((dp_low, rows, second_columns), BF)] * kept_slots,
         ],
         compiler_params=arbitrary,
         name="ssd_backward",
     )(
         ids,
         lengths,
-        sums,
-        u_pieces,
-        grad_pieces,
+        *u_pieces,
+        *grad_pieces,
+        *sums,
         normed,
         gate_raw,
         mixed,
@@ -902,12 +1086,44 @@
         gain_rows,
     )
 
-    def owner_sum(parts):
-        ordered = jnp.stack([parts[mask] for mask in slot_masks(tensor_count, 2)])
-        return scatter_sum(ordered, "tensor", 2)
+    first_kept, first_sent, *branch_far = together(first_kept, first_sent, *branch_far)
+    highs_count = first_kept.shape[0]
+    first_near = [
+        exchange(
+            first_sent
+            if dp_low == 2
+            else first_sent[(near - 1) * highs_count : near * highs_count],
+            "dp",
+            near,
+        )
+        for near in nears
+    ]
+    second_far = [
+        exchange(seconds_out[position], "dp", position * dp_low)
+        for position in range(1, kept_slots)
+    ]
+    normed_near = exchange(normed_sent, "tensor", 1)
+    landed = together(normed_near, *first_near, *second_far)
+    normed_total = normed_kept.astype(F32) + landed[0].astype(F32)
+    first_total = first_kept.astype(F32)
+    for values in landed[1 : 1 + len(first_near)]:
+        first_total = first_total + values.astype(F32)
+    second_far = landed[1 + len(first_near) :]
+    joined = first_total[:, : SMALL // 2] + first_total[:, SMALL // 2 : SMALL]
+    high = lax.reduce_precision(joined, 8, 7)
+    first_total = jnp.concatenate([high, joined - high, first_total[:, SMALL:]], axis=1)
+    first_parts = [first_total[0]] + far_parts(first_total, "dp", dp_low)
+    second_total = seconds_out[0].astype(F32)
+    for values in second_far:
+        second_total = second_total + values.astype(F32)
+    second_parts = [second_total[0]] + [
+        exchange(second_total[near].astype(BF), "dp", near) for near in range(1, dp_low)
+    ]
+    landed = together(*first_parts, *second_parts)
+    first_parts = landed[: len(first_parts)]
+    second_parts = landed[len(first_parts) :]
 
     inputs = block_input.astype(F32)
-    branch = owner_sum(branch_part)
     position_all = tensor_at * own_count + jnp.arange(own_count, dtype=jnp.int32)
     length_of = jnp.sum(
         jnp.where(
@@ -919,11 +1135,15 @@
         axis=1,
     )
     live_own = (position_all % LMAX < length_of)[:, None]
-    own_squares = lax.dynamic_slice(sums[0], (tensor_at * own_count,), (own_count,))
+    own_squares = lax.dynamic_slice(sum(part[0] for part in sums), (tensor_at * own_count,), (own_count,))
     own_scale = lax.rsqrt(own_squares / INNER + EPSILON)[:, None]
+    branch = branch_total[0]
+    for values in branch_far:
+        branch = branch + values.astype(F32)
     output = (inputs + jnp.where(live_own, branch * own_scale, 0.0)).astype(BF)
-
-    normed_grad = owner_sum(normed_part)
+    normed_grad = normed_total[0]
+    for values in far_parts(normed_total, "tensor", 2):
+        normed_grad = normed_grad + values.astype(F32)
     scale = lax.rsqrt(jnp.mean(inputs * inputs, axis=-1, keepdims=True) + EPSILON)
     scaled_grad = normed_grad * gain_whole[None, :]
     input_grad = (
@@ -932,62 +1152,80 @@
         - inputs * scale**3 * jnp.mean(scaled_grad * inputs, axis=-1, keepdims=True)
     )
 
-    kept, received = scatter_parts(slots, "dp", dp_low, SMALL // 2)
-    whole_vmem = pl.BlockSpec(memory_space=pltpu.VMEM)
-    plain = pltpu.CompilerParams(vmem_limit_bytes=48 * 1024 * 1024)
-    packed = pl.pallas_call(
+    plain = pltpu.CompilerParams(
+        dimension_semantics=("arbitrary",), vmem_limit_bytes=VMEM
+    )
+
+    def whole_call(kernel, operands, shapes, name):
+        return pl.pallas_call(
+            kernel,
+            grid_spec=pltpu.PrefetchScalarGridSpec(
+                num_scalar_prefetch=1,
+                grid=(1,),
+                in_specs=[whole_spec(value.shape) for value in operands],
+                out_specs=[whole_spec(shape.shape) for shape in shapes],
+            ),
+            out_shape=shapes,
+            compiler_params=plain,
+            name=name,
+        )(ids, *operands)
+
+    (packed,) = whole_call(
         functools.partial(pack_kernel, width, tensor_count),
-        in_specs=[whole_vmem] * (1 + len(received)),
-        out_specs=whole_vmem,
-        out_shape=struct((tensor_count, maps_rows + 8, MAPS)),
-        compiler_params=plain,
-        name="pack_maps",
-    )(kept, *received)
+        first_parts,
+        [struct((tensor_count, maps_rows + 8, MAPS))],
+        "pack_maps",
+    )
     maps_parts = lax.all_to_all(packed, "tensor", 0, 0)
-    wide_shapes = [struct(weight_.shape) for weight_ in masters[:5]]
-    wide = pl.pallas_call(
+    def wide_of(values):
+        return [values[0], values[1].T] + list(values[2:5])
+
+    wide_shapes = [struct(values.shape) for values in wide_of(masters)]
+    wide = whole_call(
         functools.partial(
-            lamb_wide_kernel, width, channels, heads, float(dp_count), len(received)
+            lamb_wide_kernel,
+            width,
+            channels,
+            heads,
+            float(dp_count),
+            len(first_parts),
+            len(second_parts),
         ),
-        in_specs=[whole_vmem] * (1 + len(received) + 15),
-        out_specs=[whole_vmem] * 21,
-        out_shape=wide_shapes * 4 + [struct((1, LANES))],
-        compiler_params=plain,
-        name="lamb_wide",
-    )(kept, *received, *masters[:5], *firsts[:5], *seconds[:5])
+        [*first_parts, *second_parts, *wide_of(masters), *wide_of(firsts), *wide_of(seconds)],
+        wide_shapes * 4 + [struct((1, LANES))],
+        "lamb_wide",
+    )
 
     def flat(values):
         return [values[5], values[6], values[7][None, :]]
 
     maps_shapes = [struct(values.shape) for values in flat(masters)]
-    maps = pl.pallas_call(
+    maps = whole_call(
         lamb_maps_kernel,
-        in_specs=[pl.BlockSpec(memory_space=pltpu.SMEM)] + [whole_vmem] * 11,
-        out_specs=[whole_vmem] * 13,
-        out_shape=maps_shapes * 4 + [struct((everywhere, 1, LANES))],
-        compiler_params=plain,
-        name="lamb_maps",
-    )(ids, maps_parts, *flat(masters), *flat(firsts), *flat(seconds), wide[20])
+        [maps_parts, *flat(masters), *flat(firsts), *flat(seconds), wide[20]],
+        maps_shapes * 4 + [struct((everywhere, 1, LANES))],
+        "lamb_maps",
+    )
     spread = lax.all_to_all(maps[12], ("dp", "tensor"), 0, 0)
-    updates = pl.pallas_call(
+    spread, input_grad, output = together(spread, input_grad, output)
+    updates = whole_call(
         update_kernel,
-        in_specs=[whole_vmem] * 9,
-        out_specs=[whole_vmem] * 9,
-        out_shape=wide_shapes + maps_shapes + [struct((2, 8))],
-        compiler_params=plain,
-        name="lamb_update",
-    )(spread, *wide[15:20], *maps[9:12])
+        [spread, *wide[15:20], *maps[9:12]],
+        wide_shapes + maps_shapes + [struct((2, 8))],
+        "lamb_update",
+    )
 
     def joined(kind):
         values = list(wide[5 * kind : 5 * kind + 5]) + list(maps[3 * kind : 3 * kind + 3])
-        return tuple(values[:7]) + (values[7][0],)
+        return (values[0], values[1].T) + tuple(values[2:7]) + (values[7][0],)
 
     return (
         (output, input_grad)
         + joined(0)
         + joined(1)
         + joined(2)
-        + tuple(updates[:7])
+        + (updates[0], updates[1].T)
+        + tuple(updates[2:7])
         + (updates[7][0], updates[8])
     )
 

time: 295 us -> 251 us (0.85)
  waiting for transfers between devices: 91.4 us -> 62.4 us
  local copies, waits for them, and re-layouts: 38.6 us -> 21.8 us
  Pallas kernels: 93.1 us -> 107 us
  other arithmetic: 23.2 us -> 16.3 us
  starting transfers between devices: 44.9 us -> 39.9 us
    unnamed x129 -> x62, local copies, waits for them, and re-layouts: 25.9 us -> 7.73 us
    ppermute x23 -> x27, waiting for transfers between devices: 76.6 us -> 60.8 us  [exchange(): return lax.ppermute(values, axis, [(at, at ^ mask) for at in range(count)])]
    pallas_call x7, Pallas kernels: 93.1 us -> 107 us  [the longest x1 53 us: local(): pl.pallas_call(functools.partial(backward_kernel, width, masks, tensor_co...]
    all_to_all x1 -> x0, waiting for transfers between devices: 12.8 us -> none  [local(): lax.all_to_all(jnp.broadcast_to(out_low[None], (dp_count,) + out_low.shap...]
    ppermute x23 -> x27, starting transfers between devices: 21.5 us -> 28.2 us  [exchange(): return lax.ppermute(values, axis, [(at, at ^ mask) for at in range(count)])]
    another operation x5 -> x3, other arithmetic: 6.69 us -> 0.92 us  [the longest x1 0.72 us: local(): out_stack = jnp.stack([piece[:, split:] for piece in both_far])]
    all_to_all x1 -> x0, starting transfers between devices: 5.48 us -> none  [local(): lax.all_to_all(jnp.broadcast_to(out_low[None], (dp_count,) + out_low.shap...]
    sub x1 -> x0, other arithmetic: 3.87 us -> none  [local(): output_grad.astype(F32) + scale * scaled_grad]
  transfers between devices with their start and end apart: 27 -> 30, of which waited for: 12 -> 11; matrix products, arithmetic and copies ran while one was open for 11% -> 11% of each run, Pallas kernels for 12% -> 37%
where the time goes in v2:
time: 251 us; the launch traced here: 250 us
  Pallas kernels  107 us (43%)
  waiting for transfers between devices  62.4 us (25%)
  starting transfers between devices  39.9 us (16%)
  local copies, waits for them, and re-layouts  21.8 us (9%)
  other arithmetic  16.3 us (6%)
    ppermute x27, waiting for transfers between devices, exchange(): return lax.ppermute(values, axis, [(at, at ^ mask) for at in range(count)])  60.8 us
    pallas_call x1, Pallas kernels, local(): pl.pallas_call(functools.partial(backward_kernel, width, masks, tensor_co...  53 us
    pallas_call x1, Pallas kernels, local(): pl.pallas_call(functools.partial(forward_kernel, width, len(in_pieces), p...  29.3 us
    ppermute x27, starting transfers between devices, exchange(): return lax.ppermute(values, axis, [(at, at ^ mask) for at in range(count)])  28.2 us
    pallas_call x4, Pallas kernels, whole_call(): pl.pallas_call(kernel, grid_spec=pltpu.PrefetchScalarGridSpec(num_scalar_...  13.2 us
    pallas_call x1, Pallas kernels, local(): pl.pallas_call(functools.partial(middle_kernel, tensor_count, len(out_pie...  11.9 us
    unnamed x62, local copies, waits for them, and re-layouts  7.73 us
  transfers between devices with their start and end apart: 30, of which 11 were waited for; matrix products, arithmetic and copies ran while one was open for 11% of the time, Pallas kernels for 37%

profile of v2, /device:TPU:0, one launch (start us, length us, event | category | flops | bytes accessed | tf_op | source)
XLA Modules:
  0.0 249.8 jit_solution(8901834915434699600)
XLA Ops:
  3.6 3.0 %collective-permute-start.4 = (bf16[96,1280]{1,0:T(8,128)(2,1)S(1)}, bf16[96,1280]{1,0:T(8,128)(2,1)}, u32[]{:S(2)}, u32[]{:S(2)}) collective-permute-start(bf16[96,1280]{1,0:T(8,128)(2,1)S(1)} %fusion.14.refs_4_), channel_id=1, source_target_pairs={{0,4},{4,0},{8,12},{12,8},{16,20},{20,16},{24,28},{28,24},{1,5},{5... | collective-permute-start | bytes 737288 | tf_op jit(solution)/shard_map/ppermute | solution.py:45
  6.6 3.6 %collective-permute-start.3 = (bf16[96,1280]{1,0:T(8,128)(2,1)S(1)}, bf16[96,1280]{1,0:T(8,128)(2,1)S(1)}, u32[]{:S(2)}, u32[]{:S(2)}) collective-permute-start(bf16[96,1280]{1,0:T(8,128)(2,1)S(1)} %fusion.14.refs_4_), channel_id=1, source_target_pairs={{0,24},{4,28},{8,16},{12,20},{16,8},{20,12},{24,0},{28,4},{1,25},{... | collective-permute-start | bytes 737288 | tf_op jit(solution)/shard_map/ppermute | solution.py:45
  18.9 11.9 %collective-permute-done.2.refs_7_ = bf16[96,1280]{1,0:T(8,128)(2,1)S(1)} collective-permute-done((bf16[96,1280]{1,0:T(8,128)(2,1)S(1)}, bf16[96,1280]{1,0:T(8,128)(2,1)S(1)}, u32[]{:S(2)}, u32[]{:S(2)}) %collective-permute-start.2) | collective-permute-done | bytes 245792 | tf_op jit(solution)/shard_map/ppermute | solution.py:45
  31.8 3.9 %all-to-all-start = ((bf16[32,25,256]{2,1,0:T(8,128)(2,1)}), bf16[32,25,256]{2,1,0:T(8,128)(2,1)}, u32[]{:S(2)}, u32[]{:S(2)}) async-start(bf16[32,25,256]{2,1,0:T(8,128)(2,1)} %broadcast_in_dim.52), calls=%async_computation | async-start | bytes 1048576 | tf_op jit(solution)/shard_map/all_to_all | solution.py:823
  44.5 11.4 %collective-permute-done.7.refs_9_ = bf16[3,96,896]{2,1,0:T(8,128)(2,1)} collective-permute-done((bf16[3,96,896]{2,1,0:T(8,128)(2,1)S(1)}, bf16[3,96,896]{2,1,0:T(8,128)(2,1)}, u32[]{:S(2)}, u32[]{:S(2)}) %collective-permute-start.7) | collective-permute-done | bytes 516128 | tf_op jit(solution)/shard_map/ppermute | solution.py:45
  60.2 29.3 %ssd_forward.1 = (bf16[2048,768]{1,0:T(8,128)(2,1)}, f32[2048,384]{1,0:T(8,128)}, f32[2048,640]{1,0:T(8,128)}, f32[2048,640]{1,0:T(8,128)}, bf16[2048,640]{1,0:T...) custom-call(s32[2]{0:T(128)} %pad_add_fusion.ids, ...), custom_call_target="tpu_custom_call" | custom-call | tf_op jit(solution)/shard_map/ssd_forward/pallas_call | solution.py:918
  90.3 1.8 collective-permute-done.11.refs_3_.refs_7_
  93.0 11.9 %gate_middle.1 = (f32[2048,384]{1,0:T(8,128)}, bf16[2,512,768]{2,1,0:T(8,128)(2,1)}, bf16[2,512,768]{2,1,0:T(8,128)(2,1)}, f32[2,2048]{1,0:T(2,128)}) custom-call(s32[2]{0:T(128)} %pad_add_fusion.ids, s32[1]{0:T(128)} %copy.80.lengths, bf16[512,768]{1,0:T(8,128)(2,1)} %refs_4_.1, bf16[512,768]{1,0:T(8,128)(2,1)} %collective-permute-done.8.refs_1_.refs_5_, ...), custom_call_target="tpu_custom_call" | custom-call | tf_op jit(solution)/shard_map/gate_middle/pallas_call | solution.py:974
  114.0 53.0 %ssd_backward.1 = (bf16[2,512,768]{2,1,0:T(8,128)(2,1)}, bf16[2,512,768]{2,1,0:T(8,128)(2,1)}, bf16[4,112,1024]{2,1,0:T(8,128)(2,1)}, bf16[4,112,1024]{2,1,0:T(8...) custom-call(s32[2]{0:T(128)} %pad_add_fusion.ids, ...), custom_call_target="tpu_custom_call" | custom-call | tf_op jit(solution)/shard_map/ssd_backward/pallas_call | solution.py:1013
  170.5 1.9 collective-permute-start.20
  173.4 6.2 %collective-permute-done.19 = bf16[2,96,512]{2,1,0:T(8,128)(2,1)S(1)} collective-permute-done((bf16[2,96,512]{2,1,0:T(8,128)(2,1)}, bf16[2,96,512]{2,1,0:T(8,128)(2,1)S(1)}, u32[]{:S(2)}, u32[]{:S(2)}) %collective-permute-start.19) | collective-permute-done | bytes 196640 | tf_op jit(solution)/shard_map/ppermute | solution.py:45
  179.6 8.2 %collective-permute-done.20 = bf16[2,96,512]{2,1,0:T(8,128)(2,1)S(1)} collective-permute-done((bf16[2,96,512]{2,1,0:T(8,128)(2,1)}, bf16[2,96,512]{2,1,0:T(8,128)(2,1)S(1)}, u32[]{:S(2)}, u32[]{:S(2)}) %collective-permute-start.20) | collective-permute-done | bytes 196640 | tf_op jit(solution)/shard_map/ppermute | solution.py:45
  187.8 3.1 %collective-permute-done.18 = bf16[4,112,1024]{2,1,0:T(8,128)(2,1)S(1)} collective-permute-done((bf16[4,112,1024]{2,1,0:T(8,128)(2,1)}, bf16[4,112,1024]{2,1,0:T(8,128)(2,1)S(1)}, u32[]{:S(2)}, u32[]{:S(2)}) %collective-permute-start.18) | collective-permute-done | bytes 917536 | tf_op jit(solution)/shard_map/ppermute | solution.py:45
  196.6 3.0 %collective-permute-start.24 = (bf16[112,1024]{1,0:T(8,128)(2,1)S(1)}, bf16[112,1024]{1,0:T(8,128)(2,1)S(1)}, u32[]{:S(2)}, u32[]{:S(2)}) collective-permute-start(bf16[112,1024]{1,0:T(8,128)(2,1)S(1)} %get-tuple-element.247), channel_id=1, source_target_pairs={{0,24},{4,28},{8,16},{12,20},{16,8},{20,12},{24,0},{28,4},{1,25},{... | collective-permute-start | bytes 688136 | tf_op jit(solution)/shard_map/ppermute | solution.py:45
  202.7 4.4 %collective-permute-done.24.refs_2_.refs_3_ = bf16[112,1024]{1,0:T(8,128)(2,1)S(1)} collective-permute-done((bf16[112,1024]{1,0:T(8,128)(2,1)S(1)}, bf16[112,1024]{1,0:T(8,128)(2,1)S(1)}, u32[]{:S(2)}, u32[]{:S(2)}) %collective-permute-start.24) | collective-permute-done | bytes 229408 | tf_op jit(solution)/shard_map/ppermute | solution.py:45
  207.1 11.8 %collective-permute-done.23.refs_1_.refs_2_ = bf16[112,1024]{1,0:T(8,128)(2,1)S(1)} collective-permute-done((bf16[112,1024]{1,0:T(8,128)(2,1)S(1)}, bf16[112,1024]{1,0:T(8,128)(2,1)S(1)}, u32[]{:S(2)}, u32[]{:S(2)}) %collective-permute-start.23) | collective-permute-done | bytes 229408 | tf_op jit(solution)/shard_map/ppermute | solution.py:45
  220.3 2.6 %pack_maps.1 = f32[4,32,256]{2,1,0:T(8,128)} custom-call(s32[2]{0:T(128)} %pad_add_fusion.ids, f32[112,1024]{1,0:T(8,128)} %slice_bitcast_fusion.1.kept_ref.refs_0_, bf16[112,1024]{1,0:T(8,128)(2,1)} %copy-done.17, bf16[112,1024]{1,0:T(8,128)(2,1)} %copy-done.16, bf16[112,1024]{1,0:T(8,128)(2,1)} %copy-done.15), custom_call_target="tpu_custom_call" | custom-call | tf_op jit(solution)/shard_map/pack_maps/pallas_call | solution.py:1160
  222.9 3.3 %all-to-all-start.1 = ((f32[4,32,256]{2,1,0:T(8,128)}), f32[4,32,256]{2,1,0:T(8,128)S(1)}, u32[]{:S(2)}, u32[]{:S(2)}) async-start(f32[4,32,256]{2,1,0:T(8,128)} %pack_maps.1), calls=%async_computation.1 | async-start | bytes 262144 | tf_op jit(solution)/shard_map/all_to_all | solution.py:1179
  226.3 5.4 %lamb_wide.1 = (f32[96,2,384]{2,1,0:T(2,128)}, f32[6,96]{1,0:T(8,128)}, f32[96,384]{1,0:T(8,128)}, f32[6,384]{1,0:T(8,128)}, f32[3,6]{1,0:T(4,128)}, /*index=5*/...) custom-call(s32[2]{0:T(128)} %pad_add_fusion.ids, ...), custom_call_target="tpu_custom_call" | custom-call | tf_op jit(solution)/shard_map/lamb_wide/pallas_call | solution.py:1160
  232.4 2.5 %lamb_maps.1 = (f32[24,256]{1,0:T(8,128)}, f32[8,5]{1,0:T(8,128)}, f32[1,24]{1,0:T(1,128)}, f32[24,256]{1,0:T(8,128)}, f32[8,5]{1,0:T(8,128)}, /*index=5*/f32[1,...) custom-call(s32[2]{0:T(128)} %pad_add_fusion.ids, ...), custom_call_target="tpu_custom_call" | custom-call | tf_op jit(solution)/shard_map/lamb_maps/pallas_call | solution.py:1160
  234.9 4.4 %all-to-all-start.2 = ((f32[32,1,128]{2,1,0:T(1,128)}), f32[32,1,128]{2,1,0:T(1,128)S(1)}, u32[]{:S(2)}, u32[]{:S(2)}) async-start(f32[32,1,128]{2,1,0:T(1,128)} %get-tuple-element.195), calls=%async_computation.2 | async-start | bytes 32768 | tf_op jit(solution)/shard_map/all_to_all | solution.py:1209
  239.4 2.0 fusion
  241.5 3.4 %fusion.4 = (bf16[512,768]{1,0:T(8,128)(2,1)}, f32[512,768]{1,0:T(8,128)}) fusion(bf16[512,768]{1,0:T(8,128)(2,1)S(1)} %copy-done.1, bf16[512,768]{1,0:T(8,128)(2,1)S(1)} %copy-done.19, f32[2,512,768]{2,1,0:T(8,128)} %copy-done.2, f32[512]{0:T(512)S(1)} %bitcast.83, pred[512]{0:T(512)(128)(4,1)S(1)} %fusion.17, f32[512]{0:T(512)S(1)} %broadcast_multiply_fusion, ...), kind=kLoop, calls=%fused_computation.12 | loop fusion | flops 6291456 | bytes 8662528 | tf_op jit(solution)/shard_map/convert_element_type | solution.py:1143
  247.0 2.7 %lamb_update.1 = (f32[96,2,384]{2,1,0:T(2,128)}, f32[6,96]{1,0:T(8,128)}, f32[96,384]{1,0:T(8,128)}, f32[6,384]{1,0:T(8,128)}, f32[3,6]{1,0:T(4,128)}, /*index=5...) custom-call(s32[2]{0:T(128)} %pad_add_fusion.ids, f32[32,1,128]{2,1,0:T(1,128)} %copy-done.24, ...), custom_call_target="tpu_custom_call" | custom-call | tf_op jit(solution)/shard_map/lamb_update/pallas_call | solution.py:1160
  (169 shorter events, 52.8 us)
Async XLA Ops:
  3.6 15.3 %collective-permute-start.4 = (bf16[96,1280]{1,0:T(8,128)(2,1)S(1)}, bf16[96,1280]{1,0:T(8,128)(2,1)}, u32[]{:S(2)}, u32[]{:S(2)}) collective-permute-start(bf16[96,1280]{1,0:T(8,128)(2,1)S(1)} %fusion.14.refs_4_), channel_id=1, source_target_pairs={{0,4},{4,0},{8,12},{12,8},{16,20},{20,16},{24,28},{28,24},{1,5},{5... | collective-permute-start | bytes 737288 | tf_op jit(solution)/shard_map/ppermute | solution.py:45
  6.6 12.3 %collective-permute-start.3 = (bf16[96,1280]{1,0:T(8,128)(2,1)S(1)}, bf16[96,1280]{1,0:T(8,128)(2,1)S(1)}, u32[]{:S(2)}, u32[]{:S(2)}) collective-permute-start(bf16[96,1280]{1,0:T(8,128)(2,1)S(1)} %fusion.14.refs_4_), channel_id=1, source_target_pairs={{0,24},{4,28},{8,16},{12,20},{16,8},{20,12},{24,0},{28,4},{1,25},{... | collective-permute-start | bytes 737288 | tf_op jit(solution)/shard_map/ppermute | solution.py:45
  10.2 20.6 %collective-permute-start.2 = (bf16[96,1280]{1,0:T(8,128)(2,1)S(1)}, bf16[96,1280]{1,0:T(8,128)(2,1)S(1)}, u32[]{:S(2)}, u32[]{:S(2)}) collective-permute-start(bf16[96,1280]{1,0:T(8,128)(2,1)S(1)} %fusion.14.refs_4_), channel_id=1, source_target_pairs={{0,16},{4,20},{8,24},{12,28},{16,0},{20,4},{24,8},{28,12},{1,17},{... | collective-permute-start | bytes 737288 | tf_op jit(solution)/shard_map/ppermute | solution.py:45
  10.2 20.6 %collective-permute-start.1 = (bf16[96,1280]{1,0:T(8,128)(2,1)S(1)}, bf16[96,1280]{1,0:T(8,128)(2,1)S(1)}, u32[]{:S(2)}, u32[]{:S(2)}) collective-permute-start(bf16[96,1280]{1,0:T(8,128)(2,1)S(1)} %fusion.14.refs_4_), channel_id=1, source_target_pairs={{0,8},{4,12},{8,0},{12,4},{16,24},{20,28},{24,16},{28,20},{1,9},{5... | collective-permute-start | bytes 737288 | tf_op jit(solution)/shard_map/ppermute | solution.py:45
  11.0 19.8 %collective-permute-start = (bf16[512,768]{1,0:T(8,128)(2,1)}, bf16[512,768]{1,0:T(8,128)(2,1)S(1)}, u32[]{:S(2)}, u32[]{:S(2)}) collective-permute-start(bf16[512,768]{1,0:T(8,128)(2,1)} %refs_0_.5), channel_id=1, source_target_pairs={{0,2},{1,3},{2,0},{3,1},{4,6},{5,7},{6,4},{7,5},{8,10},{9,11},{10,... | collective-permute-start | bytes 2359304 | tf_op jit(solution)/shard_map/ppermute | solution.py:45
  18.8 25.0 %collective-permute-start.5 = (bf16[512,768]{1,0:T(8,128)(2,1)S(1)}, bf16[512,768]{1,0:T(8,128)(2,1)S(1)}, u32[]{:S(2)}, u32[]{:S(2)}) collective-permute-start(bf16[512,768]{1,0:T(8,128)(2,1)S(1)} %copy-done), channel_id=1, source_target_pairs={{0,1},{1,0},{2,3},{3,2},{4,5},{5,4},{6,7},{7,6},{8,9},{9,8},{10,11... | collective-permute-start | bytes 2359304 | tf_op jit(solution)/shard_map/ppermute | solution.py:45
  31.8 24.1 %all-to-all-start = ((bf16[32,25,256]{2,1,0:T(8,128)(2,1)}), bf16[32,25,256]{2,1,0:T(8,128)(2,1)}, u32[]{:S(2)}, u32[]{:S(2)}) async-start(bf16[32,25,256]{2,1,0:T(8,128)(2,1)} %broadcast_in_dim.52), calls=%async_computation | async-start | bytes 1048576 | tf_op jit(solution)/shard_map/all_to_all | solution.py:823
  35.7 20.1 %collective-permute-start.6 = (bf16[512,768]{1,0:T(8,128)(2,1)S(1)}, bf16[512,768]{1,0:T(8,128)(2,1)}, u32[]{:S(2)}, u32[]{:S(2)}) collective-permute-start(bf16[512,768]{1,0:T(8,128)(2,1)S(1)} %collective-permute-done.refs_2_), channel_id=1, source_target_pairs={{0,1},{1,0},{2,3},{3,2},{4,5},{5,4},{6,7},{7,6},{8,9},{9,8},{10,11... | collective-permute-start | bytes 2359304 | tf_op jit(solution)/shard_map/ppermute | solution.py:45
  38.0 17.8 %collective-permute-start.7 = (bf16[3,96,896]{2,1,0:T(8,128)(2,1)S(1)}, bf16[3,96,896]{2,1,0:T(8,128)(2,1)}, u32[]{:S(2)}, u32[]{:S(2)}) collective-permute-start(bf16[3,96,896]{2,1,0:T(8,128)(2,1)S(1)} %pad_maximum_fusion.1), channel_id=1, source_target_pairs={{0,4},{4,0},{8,12},{12,8},{16,20},{20,16},{24,28},{28,24},{1,5},{5... | collective-permute-start | bytes 1548296 | tf_op jit(solution)/shard_map/ppermute | solution.py:45
  42.4 47.2 %collective-permute-start.9 = (bf16[512,768]{1,0:T(8,128)(2,1)S(1)}, bf16[512,768]{1,0:T(8,128)(2,1)}, u32[]{:S(2)}, u32[]{:S(2)}) collective-permute-start(bf16[512,768]{1,0:T(8,128)(2,1)S(1)} %copy-done.3), channel_id=1, source_target_pairs={{0,2},{1,3},{2,0},{3,1},{4,6},{5,7},{6,4},{7,5},{8,10},{9,11},{10,... | collective-permute-start | bytes 2359304 | tf_op jit(solution)/shard_map/ppermute | solution.py:45
  43.8 46.5 %collective-permute-start.8 = (bf16[512,768]{1,0:T(8,128)(2,1)S(1)}, bf16[512,768]{1,0:T(8,128)(2,1)}, u32[]{:S(2)}, u32[]{:S(2)}) collective-permute-start(bf16[512,768]{1,0:T(8,128)(2,1)S(1)} %copy-done.3), channel_id=1, source_target_pairs={{0,1},{1,0},{2,3},{3,2},{4,5},{5,4},{6,7},{7,6},{8,9},{9,8},{10,11... | collective-permute-start | bytes 2359304 | tf_op jit(solution)/shard_map/ppermute | solution.py:45
  43.8 45.7 %collective-permute-start.10 = (bf16[3,96,384]{2,1,0:T(8,128)(2,1)}, bf16[3,96,384]{2,1,0:T(8,128)(2,1)S(1)}, u32[]{:S(2)}, u32[]{:S(2)}) collective-permute-start(bf16[3,96,384]{2,1,0:T(8,128)(2,1)} %pad_maximum_fusion.2), channel_id=1, source_target_pairs={{0,4},{4,0},{8,12},{12,8},{16,20},{20,16},{24,28},{28,24},{1,5},{5... | collective-permute-start | bytes 663560 | tf_op jit(solution)/shard_map/ppermute | solution.py:45
  112.3 54.8 %collective-permute-start.16 = (bf16[512,768]{1,0:T(8,128)(2,1)S(1)}, bf16[512,768]{1,0:T(8,128)(2,1)S(1)}, u32[]{:S(2)}, u32[]{:S(2)}) collective-permute-start(bf16[512,768]{1,0:T(8,128)(2,1)S(1)} %fusion.9), channel_id=1, source_target_pairs={{0,2},{1,3},{2,0},{3,1},{4,6},{5,7},{6,4},{7,5},{8,10},{9,11},{10,... | collective-permute-start | bytes 2359304 | tf_op jit(solution)/shard_map/ppermute | solution.py:45
  167.0 20.8 %collective-permute-start.17 = (bf16[2,512,768]{2,1,0:T(8,128)(2,1)}, bf16[2,512,768]{2,1,0:T(8,128)(2,1)S(1)}, u32[]{:S(2)}, u32[]{:S(2)}) collective-permute-start(bf16[2,512,768]{2,1,0:T(8,128)(2,1)} %get-tuple-element.178), channel_id=1, source_target_pairs={{0,1},{1,0},{2,3},{3,2},{4,5},{5,4},{6,7},{7,6},{8,9},{9,8},{10,11... | collective-permute-start | bytes 4718600 | tf_op jit(solution)/shard_map/ppermute | solution.py:45
  168.0 23.0 %collective-permute-start.18 = (bf16[4,112,1024]{2,1,0:T(8,128)(2,1)}, bf16[4,112,1024]{2,1,0:T(8,128)(2,1)S(1)}, u32[]{:S(2)}, u32[]{:S(2)}) collective-permute-start(bf16[4,112,1024]{2,1,0:T(8,128)(2,1)} %get-tuple-element.179), channel_id=1, source_target_pairs={{0,4},{4,0},{8,12},{12,8},{16,20},{20,16},{24,28},{28,24},{1,5},{5... | collective-permute-start | bytes 2752520 | tf_op jit(solution)/shard_map/ppermute | solution.py:45
  168.8 10.7 %collective-permute-start.19 = (bf16[2,96,512]{2,1,0:T(8,128)(2,1)}, bf16[2,96,512]{2,1,0:T(8,128)(2,1)S(1)}, u32[]{:S(2)}, u32[]{:S(2)}) collective-permute-start(bf16[2,96,512]{2,1,0:T(8,128)(2,1)} %get-tuple-element.180), channel_id=1, source_target_pairs={{0,8},{4,12},{8,0},{12,4},{16,24},{20,28},{24,16},{28,20},{1,9},{5... | collective-permute-start | bytes 589832 | tf_op jit(solution)/shard_map/ppermute | solution.py:45
  170.5 17.3 %collective-permute-start.20 = (bf16[2,96,512]{2,1,0:T(8,128)(2,1)}, bf16[2,96,512]{2,1,0:T(8,128)(2,1)S(1)}, u32[]{:S(2)}, u32[]{:S(2)}) collective-permute-start(bf16[2,96,512]{2,1,0:T(8,128)(2,1)} %get-tuple-element.181), channel_id=1, source_target_pairs={{0,16},{4,20},{8,24},{12,28},{16,0},{20,4},{24,8},{28,12},{1,17},{... | collective-permute-start | bytes 589832 | tf_op jit(solution)/shard_map/ppermute | solution.py:45
  172.4 15.5 %collective-permute-start.21 = (bf16[2,96,512]{2,1,0:T(8,128)(2,1)}, bf16[2,96,512]{2,1,0:T(8,128)(2,1)S(1)}, u32[]{:S(2)}, u32[]{:S(2)}) collective-permute-start(bf16[2,96,512]{2,1,0:T(8,128)(2,1)} %get-tuple-element.182), channel_id=1, source_target_pairs={{0,24},{4,28},{8,16},{12,20},{16,8},{20,12},{24,0},{28,4},{1,25},{... | collective-permute-start | bytes 589832 | tf_op jit(solution)/shard_map/ppermute | solution.py:45
  193.6 9.1 %collective-permute-start.25 = (bf16[96,512]{1,0:T(8,128)(2,1)S(1)}, bf16[96,512]{1,0:T(8,128)(2,1)S(1)}, u32[]{:S(2)}, u32[]{:S(2)}) collective-permute-start(bf16[96,512]{1,0:T(8,128)(2,1)S(1)} %fusion.15), channel_id=1, source_target_pairs={{0,4},{4,0},{8,12},{12,8},{16,20},{20,16},{24,28},{28,24},{1,5},{5... | collective-permute-start | bytes 294920 | tf_op jit(solution)/shard_map/ppermute | solution.py:45
  195.8 43.6 %collective-permute-start.26 = (bf16[512,768]{1,0:T(8,128)(2,1)}, bf16[512,768]{1,0:T(8,128)(2,1)}, u32[]{:S(2)}, u32[]{:S(2)}) collective-permute-start(bf16[512,768]{1,0:T(8,128)(2,1)} %fusion.10), channel_id=1, source_target_pairs={{0,2},{1,3},{2,0},{3,1},{4,6},{5,7},{6,4},{7,5},{8,10},{9,11},{10,... | collective-permute-start | bytes 2359304 | tf_op jit(solution)/shard_map/ppermute | solution.py:45
  196.6 10.5 %collective-permute-start.24 = (bf16[112,1024]{1,0:T(8,128)(2,1)S(1)}, bf16[112,1024]{1,0:T(8,128)(2,1)S(1)}, u32[]{:S(2)}, u32[]{:S(2)}) collective-permute-start(bf16[112,1024]{1,0:T(8,128)(2,1)S(1)} %get-tuple-element.247), channel_id=1, source_target_pairs={{0,24},{4,28},{8,16},{12,20},{16,8},{20,12},{24,0},{28,4},{1,25},{... | collective-permute-start | bytes 688136 | tf_op jit(solution)/shard_map/ppermute | solution.py:45
  199.6 19.4 %collective-permute-start.23 = (bf16[112,1024]{1,0:T(8,128)(2,1)S(1)}, bf16[112,1024]{1,0:T(8,128)(2,1)S(1)}, u32[]{:S(2)}, u32[]{:S(2)}) collective-permute-start(bf16[112,1024]{1,0:T(8,128)(2,1)S(1)} %get-tuple-element.248), channel_id=1, source_target_pairs={{0,16},{4,20},{8,24},{12,28},{16,0},{20,4},{24,8},{28,12},{1,17},{... | collective-permute-start | bytes 688136 | tf_op jit(solution)/shard_map/ppermute | solution.py:45
  199.6 19.3 %collective-permute-start.22 = (bf16[112,1024]{1,0:T(8,128)(2,1)S(1)}, bf16[112,1024]{1,0:T(8,128)(2,1)S(1)}, u32[]{:S(2)}, u32[]{:S(2)}) collective-permute-start(bf16[112,1024]{1,0:T(8,128)(2,1)S(1)} %get-tuple-element.249), channel_id=1, source_target_pairs={{0,8},{4,12},{8,0},{12,4},{16,24},{20,28},{24,16},{28,20},{1,9},{5... | collective-permute-start | bytes 688136 | tf_op jit(solution)/shard_map/ppermute | solution.py:45
  234.9 11.5 %all-to-all-start.2 = ((f32[32,1,128]{2,1,0:T(1,128)}), f32[32,1,128]{2,1,0:T(1,128)S(1)}, u32[]{:S(2)}, u32[]{:S(2)}) async-start(f32[32,1,128]{2,1,0:T(1,128)} %get-tuple-element.195), calls=%async_computation.2 | async-start | bytes 32768 | tf_op jit(solution)/shard_map/all_to_all | solution.py:1209
  (39 other events, 350.2 us)

commit v3 on v2

--- a/solution.py
+++ b/solution.py
@@ -94,31 +94,19 @@
     return lax.broadcasted_iota(jnp.int32, shape, len(shape) - 1)
 
 
-def spread_heads(columns, heads):
-    rows = columns.shape[0]
-    left = lane_ids((rows, LANES)) < HEAD
-    return jnp.concatenate(
-        [
-            jnp.where(left, columns[:, head : head + 1], columns[:, head + 1 : head + 2])
-            for head in range(0, heads, 2)
-        ],
-        axis=1,
-    )
-
-
-def causal_mask():
-    rows = lax.broadcasted_iota(jnp.int32, (SPAN, SPAN), 0)
-    columns = lax.broadcasted_iota(jnp.int32, (SPAN, SPAN), 1)
+def lower_mask(size):
+    rows = lax.broadcasted_iota(jnp.int32, (size, size), 0)
+    columns = lax.broadcasted_iota(jnp.int32, (size, size), 1)
     return rows >= columns
 
 
-def step_terms(step_in, heads_ref):
-    step = jnp.maximum(step_in, 0.0) + jnp.log1p(jnp.exp(-jnp.abs(step_in)))
-    rate = jnp.exp(heads_ref[0:1, :])
-    decay = -rate * step
-    lower = causal_mask().astype(F32).astype(BF)
-    cumulative = sum(dot(lower, part) for part in thirds(decay))
-    return step, rate, decay, cumulative
+def paired(left, values, head):
+    return jnp.where(left, values[:, head : head + 1], values[:, head + 1 : head + 2])
+
+
+HALF = SPAN // 2
+UP = slice(0, HALF)
+DOWN = slice(HALF, SPAN)
 
 
 def halves(values):
@@ -134,7 +122,7 @@
 
 
 def sigmoid(values):
-    return 1.0 / (1.0 + jnp.exp(-values))
+    return 0.5 * jnp.tanh(0.5 * values) + 0.5
 
 
 def forward_kernel(channels, pieces, masks, owners, own_chunks, ids, *refs):
@@ -197,7 +185,7 @@
     raw_ref[...] = raw
     tail[8:, :] = raw
     step_in = dot(normed, weight_ref[:, 2 * width + MAPS :]) + heads_ref[1:2, :]
-    step_ref[...] = step_in
+    step_ref[:, :LANES] = step_in
     pre = taps_ref[CONV : CONV + 1, :] + taps_ref[0:1, :] * tail[5 : 5 + SPAN, :]
     for tap in range(1, CONV):
         pre = pre + taps_ref[tap : tap + 1, :] * tail[5 + tap : 5 + tap + SPAN, :]
@@ -208,42 +196,60 @@
     signal = act[:, :width].astype(F32)
     b_rows = act[:, width : width + STATE]
     c_rows = act[:, width + STATE :]
-    step, rate, decay, cumulative = step_terms(step_in, heads_ref)
+    step = jnp.maximum(step_in, 0.0) + jnp.log1p(jnp.exp(-jnp.abs(step_in)))
+    decay = -jnp.exp(heads_ref[0:1, :]) * step
+    lower = lower_mask(SPAN).astype(F32).astype(BF)
+    cumulative = sum(dot(lower, part) for part in thirds(decay))
+    step_ref[:, LANES : 2 * LANES] = step
+    step_ref[:, 2 * LANES :] = cumulative
     across_rows = jnp.transpose(cumulative)
     closing = cumulative[SPAN - 1 : SPAN, :]
-    held = jnp.where(causal_mask(), dot(c_rows, b_rows, 1, 1), 0.0)
-    weighted = (spread_heads(step, heads) * signal).astype(BF)
+    mask = lower_mask(HALF)
+    held_first = jnp.where(mask, dot(c_rows[UP], b_rows[UP], 1, 1), 0.0)
+    held_cross = dot(c_rows[DOWN], b_rows[UP], 1, 1)
+    held_last = jnp.where(mask, dot(c_rows[DOWN], b_rows[DOWN], 1, 1), 0.0)
     left = lane_ids((SPAN, LANES)) < HEAD
+    left_row = left[0:1]
     state = carried[...]
     state_ref[0] = state
     across = dot(
-        jnp.concatenate([c_rows, c_rows], axis=1),
-        jnp.concatenate(halves(state), axis=1),
-        1,
-        1,
-    ) * spread_heads(jnp.exp(cumulative), heads)
-    within = []
+        jnp.concatenate([c_rows, c_rows], axis=1), jnp.concatenate(halves(state), axis=0)
+    )
+    ended = []
+    ends = []
     for head in range(0, heads, 2):
         lanes = slice(head * HEAD, head * HEAD + LANES)
-        pair = weighted[:, lanes]
-        total = None
+        wide = [
+            jnp.broadcast_to(cumulative[:, head + side : head + side + 1], (SPAN, LANES))
+            for side in range(2)
+        ]
+        own = jnp.where(left, wide[0], wide[1])
+        end = paired(left_row, closing, head)
+        pair = (paired(left, step, head) * signal[:, lanes]).astype(BF)
+        first = None
         for side in range(2):
-            spread = (
-                cumulative[:, head + side : head + side + 1]
-                - across_rows[head + side : head + side + 1, :]
-            )
-            mixing = (held * jnp.exp(jnp.minimum(spread, 0.0))).astype(BF)
+            column = wide[side]
+            row = across_rows[head + side : head + side + 1, :]
+            top = (held_first * jnp.exp(jnp.minimum(column[UP] - row[:, UP], 0.0))).astype(BF)
+            cross = (held_cross * jnp.exp(column[DOWN] - row[:, UP])).astype(BF)
+            last = (
+                held_last * jnp.exp(jnp.minimum(column[DOWN] - row[:, DOWN], 0.0))
+            ).astype(BF)
             kept = jnp.where(left if side == 0 else ~left, pair, jnp.zeros_like(pair))
-            part = dot(mixing, kept)
-            total = part if total is None else total + part
-        within.append(total)
-    mixed_ref[...] = jnp.concatenate(within, axis=1) + across + skip_ref[0:1, :] * signal
-    ended = weighted.astype(F32) * spread_heads(jnp.exp(closing - cumulative), heads)
-    fresh = sum(dot(part, b_rows, 0, 0) for part in halves(ended))
-    kept_rate = jnp.exp(closing)
-    for head in range(heads):
-        rows = slice(head * HEAD, (head + 1) * HEAD)
-        carried[rows, :] = kept_rate[:, head : head + 1] * state[rows, :] + fresh[rows, :]
+            up = dot(top, kept[UP])
+            down = dot(jnp.concatenate([cross, last], axis=1), kept)
+            first, second = (up, down) if first is None else (first + up, second + down)
+        mixed_ref[:, lanes] = (
+            jnp.concatenate([first, second], axis=0)
+            + across[:, lanes] * jnp.exp(own)
+            + skip_ref[0:1, lanes] * signal[:, lanes]
+        )
+        ended.append(pair.astype(F32) * jnp.exp(end - own))
+        ends.append(jnp.exp(end))
+    fresh = sum(
+        dot(b_rows, part, 0, 0) for part in halves(jnp.concatenate(ended, axis=1))
+    )
+    carried[...] = jnp.concatenate(ends, axis=1) * state + fresh
 
 
 def place_rows(ids, masks, refs, stores):
@@ -409,6 +415,7 @@
     gain_sum,
     u_own,
     grad_own,
+    out_rows,
 ):
     sums_ref, normed_ref, gate_ref, mixed_ref, merged_grad_ref, raw_ref, pre_ref, act_ref = token_refs
     step_ref, state_ref, state_next_ref, weight_ref, taps_ref, heads_ref, skip_ref, gain_ref = other_refs
@@ -454,7 +461,7 @@
     merged = (scaled * gain).astype(BF)
     upstream = grad_own[...]
     upstream = jnp.where(rows_live(ids, at, lengths), upstream, jnp.zeros_like(upstream))
-    out_sum[...] += dot(upstream, merged, 0, 0)
+    out_sum[...] += dot(merged, upstream, 0, 0)
     gated_grad = gate_scale * (merged_grad * gain) - gated * cross
     mixed_grad = gated_grad * gate_act
     gate_grad = gated_grad * mixed * (gate_s * (1.0 + gate * (1.0 - gate_s)))
@@ -468,45 +475,55 @@
     grad_high, grad_rest = halves(mixed_grad)
     grad_rows = grad_high.astype(F32) + grad_rest.astype(F32)
 
-    step_in = step_ref[...]
-    step, rate, decay, cumulative = step_terms(step_in, heads_ref)
+    step_in = step_ref[:, :LANES]
+    step = step_ref[:, LANES : 2 * LANES]
+    cumulative = step_ref[:, 2 * LANES :]
+    rate = jnp.exp(heads_ref[0:1, :])
+    decay = -rate * step
     across_rows = jnp.transpose(cumulative)
     closing = cumulative[SPAN - 1 : SPAN, :]
-    causal = causal_mask()
-    held = jnp.where(causal, dot(c_rows, b_rows, 1, 1), 0.0)
-    step_wide = spread_heads(step, heads)
-    weighted = (step_wide * signal).astype(BF)
-    weighted_rows = weighted.astype(F32)
-    end_wide = spread_heads(jnp.exp(closing - cumulative), heads)
+    mask = lower_mask(HALF)
+    upper = lax.broadcasted_iota(jnp.int32, (HALF, HALF), 0) <= lax.broadcasted_iota(
+        jnp.int32, (HALF, HALF), 1
+    )
+    held_first = jnp.where(upper, dot(b_rows[UP], c_rows[UP], 1, 1), 0.0)
+    held_cross = dot(b_rows[UP], c_rows[DOWN], 1, 1)
+    held_last = jnp.where(upper, dot(b_rows[DOWN], c_rows[DOWN], 1, 1), 0.0)
+    left = lane_ids((SPAN, LANES)) < HEAD
+    left_row = left[0:1]
     state_grad = carried[...]
     state_parts = halves(state_grad)
-    grown = halves(grad_rows * spread_heads(jnp.exp(cumulative), heads))
-    before = halves(state_ref[0])
-    c_grad = dot(grown[0], before[0]) + dot(grown[0], before[1]) + dot(grown[1], before[0])
-    ended = halves(weighted_rows * end_wide)
-    b_grad = (
-        dot(ended[0], state_parts[0])
-        + dot(ended[0], state_parts[1])
-        + dot(ended[1], state_parts[0])
-    )
-    from_state = end_wide * dot(
-        jnp.concatenate([b_rows, b_rows], axis=1), jnp.concatenate(state_parts, axis=1), 1, 1
-    )
-    left = lane_ids((SPAN, LANES)) < HEAD
-    held_grad = None
-    within = []
+    state_before = halves(state_ref[0])
+    from_state = dot(
+        jnp.concatenate([b_rows, b_rows], axis=1), jnp.concatenate(state_parts, axis=0)
+    )
+    grads_first = grads_last = grads_cross = None
+    grown, ended, ends, weighted_grads, shaped_grads, signal_grads = [], [], [], [], [], []
     for head in range(0, heads, 2):
         lanes = slice(head * HEAD, head * HEAD + LANES)
-        pair = weighted[:, lanes]
+        wide = [
+            jnp.broadcast_to(cumulative[:, head + side : head + side + 1], (SPAN, LANES))
+            for side in range(2)
+        ]
+        own = jnp.where(left, wide[0], wide[1])
+        end = paired(left_row, closing, head)
+        end_wide = jnp.exp(end - own)
+        ends.append(jnp.exp(end))
+        step_wide = paired(left, step, head)
+        signal_own = signal[:, lanes]
+        pair = (step_wide * signal_own).astype(BF)
+        pair_rows = pair.astype(F32)
         pair_twice = jnp.concatenate([pair, pair], axis=1)
-        total = None
+        grad_own_rows = grad_rows[:, lanes]
+        grown.append(grad_own_rows * jnp.exp(own))
+        ended.append(pair_rows * end_wide)
+        total_up = None
         for side in range(2):
-            spread = (
-                cumulative[:, head + side : head + side + 1]
-                - across_rows[head + side : head + side + 1, :]
-            )
-            damping = jnp.exp(jnp.minimum(spread, 0.0))
-            mixing = (held * damping).astype(BF)
+            column = wide[side]
+            row = across_rows[head + side : head + side + 1, :]
+            damp_first = jnp.exp(jnp.minimum(row[:, UP] - column[UP], 0.0))
+            damp_cross = jnp.exp(row[:, DOWN] - column[UP])
+            damp_last = jnp.exp(jnp.minimum(row[:, DOWN] - column[DOWN], 0.0))
             side_lanes = left if side == 0 else ~left
             kept = jnp.concatenate(
                 [
@@ -515,49 +532,82 @@
                 ],
                 axis=1,
             )
-            term = dot(kept, pair_twice, 1, 1) * damping
-            held_grad = term if held_grad is None else held_grad + term
-            part = dot(mixing, kept, 0, 0)
-            total = part if total is None else total + part
-        within.append(total[:, :LANES] + total[:, LANES:])
-    held_low = jnp.where(causal, held_grad, 0.0).astype(BF)
-    c_grad = c_grad + dot(held_low, b_rows)
-    b_grad = b_grad + dot(held_low, c_rows, 0, 0)
-    weighted_grad = jnp.concatenate(within, axis=1) + from_state
-    fresh = sum(dot(part, c_rows, 0, 0) for part in grown)
-    kept_rate = jnp.exp(closing)
-    overlap = jnp.sum(state_grad * state_next_ref[0], axis=1, keepdims=True)
-    lane_row = lane_ids((1, LANES))
-    closing_grad = jnp.zeros((1, LANES), F32)
-    for head in range(heads):
-        rows = slice(head * HEAD, (head + 1) * HEAD)
-        carried[rows, :] = kept_rate[:, head : head + 1] * state_grad[rows, :] + fresh[rows, :]
-        closing_grad = closing_grad + jnp.where(
-            lane_row == head, jnp.sum(overlap[rows, :], axis=0, keepdims=True), 0.0
-        )
+            terms_up = dot(pair_twice[UP], kept, 1, 1)
+            terms_first = terms_up[:, UP] * damp_first
+            terms_cross = terms_up[:, DOWN] * damp_cross
+            terms_last = dot(pair_twice[DOWN], kept[DOWN], 1, 1) * damp_last
+            if grads_first is None:
+                grads_first, grads_cross, grads_last = terms_first, terms_cross, terms_last
+            else:
+                grads_first = grads_first + terms_first
+                grads_cross = grads_cross + terms_cross
+                grads_last = grads_last + terms_last
+            mixing_up = jnp.concatenate(
+                [(held_first * damp_first).astype(BF), (held_cross * damp_cross).astype(BF)],
+                axis=1,
+            )
+            up = dot(mixing_up, kept)
+            down = dot((held_last * damp_last).astype(BF), kept[DOWN])
+            total_up, total_down = (
+                (up, down) if total_up is None else (total_up + up, total_down + down)
+            )
+        total = jnp.concatenate([total_up, total_down], axis=0)
+        own_grad = total[:, :LANES] + total[:, LANES:] + end_wide * from_state[:, lanes]
+        shaped = mixed[:, lanes] - skip[:, lanes] * signal_own
+        weighted_grads.append(signal_own * own_grad)
+        shaped_grads.append(grad_own_rows * shaped - pair_rows * own_grad)
+        signal_grads.append(step_wide * own_grad + skip[:, lanes] * mixed_grad[:, lanes])
+    held_low = jnp.concatenate(
+        [
+            jnp.concatenate(
+                [jnp.where(upper, grads_first, 0.0).astype(BF), grads_cross.astype(BF)], axis=1
+            ),
+            jnp.concatenate(
+                [jnp.zeros((HALF, HALF), BF), jnp.where(upper, grads_last, 0.0).astype(BF)], axis=1
+            ),
+        ],
+        axis=0,
+    )
+    grown = halves(jnp.concatenate(grown, axis=1))
+    ended = halves(jnp.concatenate(ended, axis=1))
+    c_grad = (
+        dot(held_low, b_rows, 0, 0)
+        + dot(grown[0], state_before[0], 1, 1)
+        + dot(grown[0], state_before[1], 1, 1)
+        + dot(grown[1], state_before[0], 1, 1)
+    )
+    b_grad = (
+        dot(held_low, c_rows)
+        + dot(ended[0], state_parts[0], 1, 1)
+        + dot(ended[0], state_parts[1], 1, 1)
+        + dot(ended[1], state_parts[0], 1, 1)
+    )
+    fresh = sum(dot(c_rows, part, 0, 0) for part in grown)
+    carried[...] = jnp.concatenate(ends, axis=1) * state_grad + fresh
     picker = (
         lax.broadcasted_iota(jnp.int32, (width, LANES), 0) // HEAD
         == lax.broadcasted_iota(jnp.int32, (width, LANES), 1)
     ).astype(F32).astype(BF)
-    shaped = mixed - skip * signal
+    overlap = jnp.sum(state_grad * state_next_ref[0], axis=0, keepdims=True)
+    closing_grad = sum(
+        dot(part, picker) for part in thirds(jnp.broadcast_to(overlap, (8, width)))
+    )[0:1]
     cumulative_grad = sum(
-        dot(part, picker)
-        for part in halves(grad_rows * shaped - weighted_rows * weighted_grad)
-    )
-    lower = causal.astype(F32).astype(BF)
+        dot(part, picker) for part in halves(jnp.concatenate(shaped_grads, axis=1))
+    )
+    lower = lower_mask(SPAN).astype(F32).astype(BF)
     decay_grad = sum(dot(lower, part, 0, 0) for part in halves(cumulative_grad)) + closing_grad
     step_grad = (
-        sum(dot(part, picker) for part in halves(signal * weighted_grad)) - rate * decay_grad
+        sum(dot(part, picker) for part in halves(jnp.concatenate(weighted_grads, axis=1)))
+        - rate * decay_grad
     )
     step_in_grad = step_grad * sigmoid(step_in)
     head_sum[0:1, :] += jnp.sum(decay * decay_grad, axis=0, keepdims=True)
     head_sum[1:2, :] += jnp.sum(step_in_grad, axis=0, keepdims=True)
-    signal_grad = step_wide * weighted_grad + skip * mixed_grad
-
     pre = pre_ref[...]
     pre_s = sigmoid(pre)
     slope = pre_s * (1.0 + pre * (1.0 - pre_s))
-    ahead[:SPAN, :] = jnp.concatenate([signal_grad, b_grad, c_grad], axis=1) * slope
+    ahead[:SPAN, :] = jnp.concatenate(signal_grads + [b_grad, c_grad], axis=1) * slope
     raw = raw_ref[...]
     raw_grad = None
     for shift in range(CONV):
@@ -587,6 +637,7 @@
         model = weight_sum.shape[0]
         first = first_kept_ref.shape[2]
         kept_count = first_kept_ref.shape[0]
+        out_rows[...] = jnp.transpose(out_sum[...])
         step_lanes = weight_sum.shape[1] - first
         for place, mask in enumerate(masks):
             first_ref = first_kept_ref if place < kept_count else first_sent_ref
@@ -613,7 +664,7 @@
             second_ref = second_refs[place % kept_count]
             near = place // kept_count
             second_ref[near, :, :step_lanes] = weight_sum[picked, first:].astype(BF)
-            second_ref[near, :, step_lanes:] = out_sum[picked, :].astype(BF)
+            second_ref[near, :, step_lanes:] = out_rows[picked, :].astype(BF)
 
 
 def pad_to(values, axis, size):
@@ -935,14 +986,14 @@
                 token_spec(mixed_width),
                 token_spec(mixed_width),
                 token_spec(mixed_width),
-                token_spec(LANES),
-                pl.BlockSpec((1, width, STATE), lambda at, *_: (at, 0, 0)),
+                token_spec(3 * LANES),
+                pl.BlockSpec((1, STATE, width), lambda at, *_: (at, 0, 0)),
                 token_spec(width),
                 whole_spec((model, columns)),
             ],
             scratch_shapes=[
                 pltpu.VMEM((SPAN + 8, mixed_width), F32),
-                pltpu.VMEM((width, STATE), F32),
+                pltpu.VMEM((STATE, width), F32),
                 pltpu.VMEM((SPAN, model), BF),
             ],
         ),
@@ -952,8 +1003,8 @@
             struct((tokens, mixed_width)),
             struct((tokens, mixed_width)),
             struct((tokens, mixed_width), BF),
-            struct((tokens, LANES)),
-            struct((chunks, width, STATE)),
+            struct((tokens, 3 * LANES)),
+            struct((chunks, STATE, width)),
             struct((tokens, width)),
             struct((model, columns), BF),
         ],
@@ -1026,10 +1077,10 @@
                 token_back(mixed_width),
                 token_back(mixed_width),
                 token_back(mixed_width),
-                token_back(LANES),
-                pl.BlockSpec((1, width, STATE), lambda at, *_: (chunks - 1 - at, 0, 0)),
+                token_back(3 * LANES),
+                pl.BlockSpec((1, STATE, width), lambda at, *_: (chunks - 1 - at, 0, 0)),
                 pl.BlockSpec(
-                    (1, width, STATE), lambda at, *_: (jnp.minimum(chunks - at, chunks - 1), 0, 0)
+                    (1, STATE, width), lambda at, *_: (jnp.minimum(chunks - at, chunks - 1), 0, 0)
                 ),
                 whole_spec((model, columns)),
                 whole_spec(taps.shape),
@@ -1044,15 +1095,16 @@
                 *[whole_spec((dp_low, rows, second_columns))] * kept_slots,
             ],
             scratch_shapes=[
-                pltpu.VMEM((width, STATE), F32),
+                pltpu.VMEM((STATE, width), F32),
                 pltpu.VMEM((SPAN + 8, mixed_width), F32),
                 pltpu.VMEM((model, columns), F32),
-                pltpu.VMEM((model, width), F32),
+                pltpu.VMEM((width, model), F32),
                 pltpu.VMEM((8, mixed_width), F32),
                 pltpu.VMEM((8, LANES), F32),
                 pltpu.VMEM((8, model), F32),
                 pltpu.VMEM((SPAN, model), BF),
                 pltpu.VMEM((SPAN, model), BF),
+                pltpu.VMEM((model, width), F32),
             ],
         ),
         out_shape=[

time: 251 us -> 239 us (0.952)
  Pallas kernels: 107 us -> 95.2 us
    pallas_call x1, Pallas kernels: 53 us -> 45.8 us  [local(): pl.pallas_call(functools.partial(backward_kernel, width, masks, tensor_co...]
    pallas_call x1, Pallas kernels: 29.3 us -> 24.2 us  [local(): pl.pallas_call(functools.partial(forward_kernel, width, len(in_pieces), p...]
  transfers between devices with their start and end apart: 30 -> 30, of which waited for: 11 -> 11; matrix products, arithmetic and copies ran while one was open for 11% -> 11% of each run, Pallas kernels for 37% -> 34%
where the time goes in v3:
time: 239 us; the launch traced here: 238 us
  Pallas kernels  95.2 us (40%)
  waiting for transfers between devices  62.2 us (26%)
  starting transfers between devices  39.9 us (17%)
  local copies, waits for them, and re-layouts  21.8 us (9%)
  other arithmetic  16.4 us (7%)
    ppermute x27, waiting for transfers between devices, exchange(): return lax.ppermute(values, axis, [(at, at ^ mask) for at in range(count)])  60.6 us
    pallas_call x1, Pallas kernels, local(): pl.pallas_call(functools.partial(backward_kernel, width, masks, tensor_co...  45.8 us
    ppermute x27, starting transfers between devices, exchange(): return lax.ppermute(values, axis, [(at, at ^ mask) for at in range(count)])  28.2 us
    pallas_call x1, Pallas kernels, local(): pl.pallas_call(functools.partial(forward_kernel, width, len(in_pieces), p...  24.2 us
    pallas_call x4, Pallas kernels, whole_call(): pl.pallas_call(kernel, grid_spec=pltpu.PrefetchScalarGridSpec(num_scalar_...  13.2 us
    pallas_call x1, Pallas kernels, local(): pl.pallas_call(functools.partial(middle_kernel, tensor_count, len(out_pie...  12 us
    unnamed x62, local copies, waits for them, and re-layouts  7.76 us
  transfers between devices with their start and end apart: 30, of which 11 were waited for; matrix products, arithmetic and copies ran while one was open for 11% of the time, Pallas kernels for 34%

profile of v3, /device:TPU:0, one launch (start us, length us, event | category | flops | bytes accessed | tf_op | source)
XLA Modules:
  0.0 237.6 jit_solution(12260793804100686338)
XLA Ops:
  3.6 3.0 %collective-permute-start.4 = (bf16[96,1280]{1,0:T(8,128)(2,1)S(1)}, bf16[96,1280]{1,0:T(8,128)(2,1)}, u32[]{:S(2)}, u32[]{:S(2)}) collective-permute-start(bf16[96,1280]{1,0:T(8,128)(2,1)S(1)} %fusion.14.refs_4_), channel_id=1, source_target_pairs={{0,4},{4,0},{8,12},{12,8},{16,20},{20,16},{24,28},{28,24},{1,5},{5... | collective-permute-start | bytes 737288 | tf_op jit(solution)/shard_map/ppermute | solution.py:45
  6.6 3.6 %collective-permute-start.3 = (bf16[96,1280]{1,0:T(8,128)(2,1)S(1)}, bf16[96,1280]{1,0:T(8,128)(2,1)S(1)}, u32[]{:S(2)}, u32[]{:S(2)}) collective-permute-start(bf16[96,1280]{1,0:T(8,128)(2,1)S(1)} %fusion.14.refs_4_), channel_id=1, source_target_pairs={{0,24},{4,28},{8,16},{12,20},{16,8},{20,12},{24,0},{28,4},{1,25},{... | collective-permute-start | bytes 737288 | tf_op jit(solution)/shard_map/ppermute | solution.py:45
  18.9 11.9 %collective-permute-done.2.refs_7_ = bf16[96,1280]{1,0:T(8,128)(2,1)S(1)} collective-permute-done((bf16[96,1280]{1,0:T(8,128)(2,1)S(1)}, bf16[96,1280]{1,0:T(8,128)(2,1)S(1)}, u32[]{:S(2)}, u32[]{:S(2)}) %collective-permute-start.2) | collective-permute-done | bytes 245792 | tf_op jit(solution)/shard_map/ppermute | solution.py:45
  31.8 3.9 %all-to-all-start = ((bf16[32,25,256]{2,1,0:T(8,128)(2,1)}), bf16[32,25,256]{2,1,0:T(8,128)(2,1)}, u32[]{:S(2)}, u32[]{:S(2)}) async-start(bf16[32,25,256]{2,1,0:T(8,128)(2,1)} %broadcast_in_dim.52), calls=%async_computation | async-start | bytes 1048576 | tf_op jit(solution)/shard_map/all_to_all | solution.py:874
  44.5 11.3 %collective-permute-done.7.refs_9_ = bf16[3,96,896]{2,1,0:T(8,128)(2,1)} collective-permute-done((bf16[3,96,896]{2,1,0:T(8,128)(2,1)S(1)}, bf16[3,96,896]{2,1,0:T(8,128)(2,1)}, u32[]{:S(2)}, u32[]{:S(2)}) %collective-permute-start.7) | collective-permute-done | bytes 516128 | tf_op jit(solution)/shard_map/ppermute | solution.py:45
  60.2 24.2 %ssd_forward.1 = (bf16[2048,768]{1,0:T(8,128)(2,1)}, f32[2048,384]{1,0:T(8,128)}, f32[2048,640]{1,0:T(8,128)}, f32[2048,640]{1,0:T(8,128)}, bf16[2048,640]{1,0:T...) custom-call(s32[2]{0:T(128)} %pad_add_fusion.ids, ...), custom_call_target="tpu_custom_call" | custom-call | tf_op jit(solution)/shard_map/ssd_forward/pallas_call | solution.py:969
  85.2 1.8 collective-permute-done.11.refs_3_.refs_7_
  87.9 12.0 %gate_middle.1 = (f32[2048,384]{1,0:T(8,128)}, bf16[2,512,768]{2,1,0:T(8,128)(2,1)}, bf16[2,512,768]{2,1,0:T(8,128)(2,1)}, f32[2,2048]{1,0:T(2,128)}) custom-call(s32[2]{0:T(128)} %pad_add_fusion.ids, s32[1]{0:T(128)} %copy.80.lengths, bf16[512,768]{1,0:T(8,128)(2,1)} %refs_4_.1, bf16[512,768]{1,0:T(8,128)(2,1)} %collective-permute-done.8.refs_1_.refs_5_, ...), custom_call_target="tpu_custom_call" | custom-call | tf_op jit(solution)/shard_map/gate_middle/pallas_call | solution.py:1025
  108.9 45.8 %ssd_backward.1 = (bf16[2,512,768]{2,1,0:T(8,128)(2,1)}, bf16[2,512,768]{2,1,0:T(8,128)(2,1)}, bf16[4,112,1024]{2,1,0:T(8,128)(2,1)}, bf16[4,112,1024]{2,1,0:T(8...) custom-call(s32[2]{0:T(128)} %pad_add_fusion.ids, ...), custom_call_target="tpu_custom_call" | custom-call | tf_op jit(solution)/shard_map/ssd_backward/pallas_call | solution.py:1064
  158.2 1.9 collective-permute-start.20
  161.1 6.2 %collective-permute-done.19 = bf16[2,96,512]{2,1,0:T(8,128)(2,1)S(1)} collective-permute-done((bf16[2,96,512]{2,1,0:T(8,128)(2,1)}, bf16[2,96,512]{2,1,0:T(8,128)(2,1)S(1)}, u32[]{:S(2)}, u32[]{:S(2)}) %collective-permute-start.19) | collective-permute-done | bytes 196640 | tf_op jit(solution)/shard_map/ppermute | solution.py:45
  167.3 8.2 %collective-permute-done.20 = bf16[2,96,512]{2,1,0:T(8,128)(2,1)S(1)} collective-permute-done((bf16[2,96,512]{2,1,0:T(8,128)(2,1)}, bf16[2,96,512]{2,1,0:T(8,128)(2,1)S(1)}, u32[]{:S(2)}, u32[]{:S(2)}) %collective-permute-start.20) | collective-permute-done | bytes 196640 | tf_op jit(solution)/shard_map/ppermute | solution.py:45
  175.5 3.2 %collective-permute-done.18 = bf16[4,112,1024]{2,1,0:T(8,128)(2,1)S(1)} collective-permute-done((bf16[4,112,1024]{2,1,0:T(8,128)(2,1)}, bf16[4,112,1024]{2,1,0:T(8,128)(2,1)S(1)}, u32[]{:S(2)}, u32[]{:S(2)}) %collective-permute-start.18) | collective-permute-done | bytes 917536 | tf_op jit(solution)/shard_map/ppermute | solution.py:45
  184.3 2.8 %collective-permute-start.24 = (bf16[112,1024]{1,0:T(8,128)(2,1)S(1)}, bf16[112,1024]{1,0:T(8,128)(2,1)S(1)}, u32[]{:S(2)}, u32[]{:S(2)}) collective-permute-start(bf16[112,1024]{1,0:T(8,128)(2,1)S(1)} %get-tuple-element.247), channel_id=1, source_target_pairs={{0,24},{4,28},{8,16},{12,20},{16,8},{20,12},{24,0},{28,4},{1,25},{... | collective-permute-start | bytes 688136 | tf_op jit(solution)/shard_map/ppermute | solution.py:45
  190.4 4.4 %collective-permute-done.24.refs_2_.refs_3_ = bf16[112,1024]{1,0:T(8,128)(2,1)S(1)} collective-permute-done((bf16[112,1024]{1,0:T(8,128)(2,1)S(1)}, bf16[112,1024]{1,0:T(8,128)(2,1)S(1)}, u32[]{:S(2)}, u32[]{:S(2)}) %collective-permute-start.24) | collective-permute-done | bytes 229408 | tf_op jit(solution)/shard_map/ppermute | solution.py:45
  194.8 11.8 %collective-permute-done.23.refs_1_.refs_2_ = bf16[112,1024]{1,0:T(8,128)(2,1)S(1)} collective-permute-done((bf16[112,1024]{1,0:T(8,128)(2,1)S(1)}, bf16[112,1024]{1,0:T(8,128)(2,1)S(1)}, u32[]{:S(2)}, u32[]{:S(2)}) %collective-permute-start.23) | collective-permute-done | bytes 229408 | tf_op jit(solution)/shard_map/ppermute | solution.py:45
  208.0 2.6 %pack_maps.1 = f32[4,32,256]{2,1,0:T(8,128)} custom-call(s32[2]{0:T(128)} %pad_add_fusion.ids, f32[112,1024]{1,0:T(8,128)} %slice_bitcast_fusion.1.kept_ref.refs_0_, bf16[112,1024]{1,0:T(8,128)(2,1)} %copy-done.17, bf16[112,1024]{1,0:T(8,128)(2,1)} %copy-done.16, bf16[112,1024]{1,0:T(8,128)(2,1)} %copy-done.15), custom_call_target="tpu_custom_call" | custom-call | tf_op jit(solution)/shard_map/pack_maps/pallas_call | solution.py:1212
  210.6 3.3 %all-to-all-start.1 = ((f32[4,32,256]{2,1,0:T(8,128)}), f32[4,32,256]{2,1,0:T(8,128)S(1)}, u32[]{:S(2)}, u32[]{:S(2)}) async-start(f32[4,32,256]{2,1,0:T(8,128)} %pack_maps.1), calls=%async_computation.1 | async-start | bytes 262144 | tf_op jit(solution)/shard_map/all_to_all | solution.py:1231
  214.0 5.4 %lamb_wide.1 = (f32[96,2,384]{2,1,0:T(2,128)}, f32[6,96]{1,0:T(8,128)}, f32[96,384]{1,0:T(8,128)}, f32[6,384]{1,0:T(8,128)}, f32[3,6]{1,0:T(4,128)}, /*index=5*/...) custom-call(s32[2]{0:T(128)} %pad_add_fusion.ids, ...), custom_call_target="tpu_custom_call" | custom-call | tf_op jit(solution)/shard_map/lamb_wide/pallas_call | solution.py:1212
  220.1 2.5 %lamb_maps.1 = (f32[24,256]{1,0:T(8,128)}, f32[8,5]{1,0:T(8,128)}, f32[1,24]{1,0:T(1,128)}, f32[24,256]{1,0:T(8,128)}, f32[8,5]{1,0:T(8,128)}, /*index=5*/f32[1,...) custom-call(s32[2]{0:T(128)} %pad_add_fusion.ids, ...), custom_call_target="tpu_custom_call" | custom-call | tf_op jit(solution)/shard_map/lamb_maps/pallas_call | solution.py:1212
  222.6 4.5 %all-to-all-start.2 = ((f32[32,1,128]{2,1,0:T(1,128)}), f32[32,1,128]{2,1,0:T(1,128)S(1)}, u32[]{:S(2)}, u32[]{:S(2)}) async-start(f32[32,1,128]{2,1,0:T(1,128)} %get-tuple-element.195), calls=%async_computation.2 | async-start | bytes 32768 | tf_op jit(solution)/shard_map/all_to_all | solution.py:1261
  227.1 2.0 fusion
  229.2 3.4 %fusion.4 = (bf16[512,768]{1,0:T(8,128)(2,1)}, f32[512,768]{1,0:T(8,128)}) fusion(bf16[512,768]{1,0:T(8,128)(2,1)S(1)} %copy-done.1, bf16[512,768]{1,0:T(8,128)(2,1)S(1)} %copy-done.19, f32[2,512,768]{2,1,0:T(8,128)} %copy-done.2, f32[512]{0:T(512)S(1)} %bitcast.83, pred[512]{0:T(512)(128)(4,1)S(1)} %fusion.17, f32[512]{0:T(512)S(1)} %broadcast_multiply_fusion, ...), kind=kLoop, calls=%fused_computation.12 | loop fusion | flops 6291456 | bytes 8662528 | tf_op jit(solution)/shard_map/convert_element_type | solution.py:1195
  234.7 2.7 %lamb_update.1 = (f32[96,2,384]{2,1,0:T(2,128)}, f32[6,96]{1,0:T(8,128)}, f32[96,384]{1,0:T(8,128)}, f32[6,384]{1,0:T(8,128)}, f32[3,6]{1,0:T(4,128)}, /*index=5...) custom-call(s32[2]{0:T(128)} %pad_add_fusion.ids, f32[32,1,128]{2,1,0:T(1,128)} %copy-done.24, ...), custom_call_target="tpu_custom_call" | custom-call | tf_op jit(solution)/shard_map/lamb_update/pallas_call | solution.py:1212
  (169 shorter events, 53.0 us)
Async XLA Ops:
  3.6 15.3 %collective-permute-start.4 = (bf16[96,1280]{1,0:T(8,128)(2,1)S(1)}, bf16[96,1280]{1,0:T(8,128)(2,1)}, u32[]{:S(2)}, u32[]{:S(2)}) collective-permute-start(bf16[96,1280]{1,0:T(8,128)(2,1)S(1)} %fusion.14.refs_4_), channel_id=1, source_target_pairs={{0,4},{4,0},{8,12},{12,8},{16,20},{20,16},{24,28},{28,24},{1,5},{5... | collective-permute-start | bytes 737288 | tf_op jit(solution)/shard_map/ppermute | solution.py:45
  6.6 12.3 %collective-permute-start.3 = (bf16[96,1280]{1,0:T(8,128)(2,1)S(1)}, bf16[96,1280]{1,0:T(8,128)(2,1)S(1)}, u32[]{:S(2)}, u32[]{:S(2)}) collective-permute-start(bf16[96,1280]{1,0:T(8,128)(2,1)S(1)} %fusion.14.refs_4_), channel_id=1, source_target_pairs={{0,24},{4,28},{8,16},{12,20},{16,8},{20,12},{24,0},{28,4},{1,25},{... | collective-permute-start | bytes 737288 | tf_op jit(solution)/shard_map/ppermute | solution.py:45
  10.2 20.6 %collective-permute-start.2 = (bf16[96,1280]{1,0:T(8,128)(2,1)S(1)}, bf16[96,1280]{1,0:T(8,128)(2,1)S(1)}, u32[]{:S(2)}, u32[]{:S(2)}) collective-permute-start(bf16[96,1280]{1,0:T(8,128)(2,1)S(1)} %fusion.14.refs_4_), channel_id=1, source_target_pairs={{0,16},{4,20},{8,24},{12,28},{16,0},{20,4},{24,8},{28,12},{1,17},{... | collective-permute-start | bytes 737288 | tf_op jit(solution)/shard_map/ppermute | solution.py:45
  10.2 20.6 %collective-permute-start.1 = (bf16[96,1280]{1,0:T(8,128)(2,1)S(1)}, bf16[96,1280]{1,0:T(8,128)(2,1)S(1)}, u32[]{:S(2)}, u32[]{:S(2)}) collective-permute-start(bf16[96,1280]{1,0:T(8,128)(2,1)S(1)} %fusion.14.refs_4_), channel_id=1, source_target_pairs={{0,8},{4,12},{8,0},{12,4},{16,24},{20,28},{24,16},{28,20},{1,9},{5... | collective-permute-start | bytes 737288 | tf_op jit(solution)/shard_map/ppermute | solution.py:45
  11.0 19.8 %collective-permute-start = (bf16[512,768]{1,0:T(8,128)(2,1)}, bf16[512,768]{1,0:T(8,128)(2,1)S(1)}, u32[]{:S(2)}, u32[]{:S(2)}) collective-permute-start(bf16[512,768]{1,0:T(8,128)(2,1)} %refs_0_.5), channel_id=1, source_target_pairs={{0,2},{1,3},{2,0},{3,1},{4,6},{5,7},{6,4},{7,5},{8,10},{9,11},{10,... | collective-permute-start | bytes 2359304 | tf_op jit(solution)/shard_map/ppermute | solution.py:45
  18.9 25.0 %collective-permute-start.5 = (bf16[512,768]{1,0:T(8,128)(2,1)S(1)}, bf16[512,768]{1,0:T(8,128)(2,1)S(1)}, u32[]{:S(2)}, u32[]{:S(2)}) collective-permute-start(bf16[512,768]{1,0:T(8,128)(2,1)S(1)} %copy-done), channel_id=1, source_target_pairs={{0,1},{1,0},{2,3},{3,2},{4,5},{5,4},{6,7},{7,6},{8,9},{9,8},{10,11... | collective-permute-start | bytes 2359304 | tf_op jit(solution)/shard_map/ppermute | solution.py:45
  31.8 24.1 %all-to-all-start = ((bf16[32,25,256]{2,1,0:T(8,128)(2,1)}), bf16[32,25,256]{2,1,0:T(8,128)(2,1)}, u32[]{:S(2)}, u32[]{:S(2)}) async-start(bf16[32,25,256]{2,1,0:T(8,128)(2,1)} %broadcast_in_dim.52), calls=%async_computation | async-start | bytes 1048576 | tf_op jit(solution)/shard_map/all_to_all | solution.py:874
  35.7 20.1 %collective-permute-start.6 = (bf16[512,768]{1,0:T(8,128)(2,1)S(1)}, bf16[512,768]{1,0:T(8,128)(2,1)}, u32[]{:S(2)}, u32[]{:S(2)}) collective-permute-start(bf16[512,768]{1,0:T(8,128)(2,1)S(1)} %collective-permute-done.refs_2_), channel_id=1, source_target_pairs={{0,1},{1,0},{2,3},{3,2},{4,5},{5,4},{6,7},{7,6},{8,9},{9,8},{10,11... | collective-permute-start | bytes 2359304 | tf_op jit(solution)/shard_map/ppermute | solution.py:45
  38.0 17.8 %collective-permute-start.7 = (bf16[3,96,896]{2,1,0:T(8,128)(2,1)S(1)}, bf16[3,96,896]{2,1,0:T(8,128)(2,1)}, u32[]{:S(2)}, u32[]{:S(2)}) collective-permute-start(bf16[3,96,896]{2,1,0:T(8,128)(2,1)S(1)} %pad_maximum_fusion.1), channel_id=1, source_target_pairs={{0,4},{4,0},{8,12},{12,8},{16,20},{20,16},{24,28},{28,24},{1,5},{5... | collective-permute-start | bytes 1548296 | tf_op jit(solution)/shard_map/ppermute | solution.py:45
  42.4 42.1 %collective-permute-start.9 = (bf16[512,768]{1,0:T(8,128)(2,1)S(1)}, bf16[512,768]{1,0:T(8,128)(2,1)}, u32[]{:S(2)}, u32[]{:S(2)}) collective-permute-start(bf16[512,768]{1,0:T(8,128)(2,1)S(1)} %copy-done.3), channel_id=1, source_target_pairs={{0,2},{1,3},{2,0},{3,1},{4,6},{5,7},{6,4},{7,5},{8,10},{9,11},{10,... | collective-permute-start | bytes 2359304 | tf_op jit(solution)/shard_map/ppermute | solution.py:45
  43.8 41.4 %collective-permute-start.8 = (bf16[512,768]{1,0:T(8,128)(2,1)S(1)}, bf16[512,768]{1,0:T(8,128)(2,1)}, u32[]{:S(2)}, u32[]{:S(2)}) collective-permute-start(bf16[512,768]{1,0:T(8,128)(2,1)S(1)} %copy-done.3), channel_id=1, source_target_pairs={{0,1},{1,0},{2,3},{3,2},{4,5},{5,4},{6,7},{7,6},{8,9},{9,8},{10,11... | collective-permute-start | bytes 2359304 | tf_op jit(solution)/shard_map/ppermute | solution.py:45
  43.8 40.6 %collective-permute-start.10 = (bf16[3,96,384]{2,1,0:T(8,128)(2,1)}, bf16[3,96,384]{2,1,0:T(8,128)(2,1)S(1)}, u32[]{:S(2)}, u32[]{:S(2)}) collective-permute-start(bf16[3,96,384]{2,1,0:T(8,128)(2,1)} %pad_maximum_fusion.2), channel_id=1, source_target_pairs={{0,4},{4,0},{8,12},{12,8},{16,20},{20,16},{24,28},{28,24},{1,5},{5... | collective-permute-start | bytes 663560 | tf_op jit(solution)/shard_map/ppermute | solution.py:45
  107.2 47.6 %collective-permute-start.16 = (bf16[512,768]{1,0:T(8,128)(2,1)S(1)}, bf16[512,768]{1,0:T(8,128)(2,1)S(1)}, u32[]{:S(2)}, u32[]{:S(2)}) collective-permute-start(bf16[512,768]{1,0:T(8,128)(2,1)S(1)} %fusion.9), channel_id=1, source_target_pairs={{0,2},{1,3},{2,0},{3,1},{4,6},{5,7},{6,4},{7,5},{8,10},{9,11},{10,... | collective-permute-start | bytes 2359304 | tf_op jit(solution)/shard_map/ppermute | solution.py:45
  154.8 20.8 %collective-permute-start.17 = (bf16[2,512,768]{2,1,0:T(8,128)(2,1)}, bf16[2,512,768]{2,1,0:T(8,128)(2,1)S(1)}, u32[]{:S(2)}, u32[]{:S(2)}) collective-permute-start(bf16[2,512,768]{2,1,0:T(8,128)(2,1)} %get-tuple-element.178), channel_id=1, source_target_pairs={{0,1},{1,0},{2,3},{3,2},{4,5},{5,4},{6,7},{7,6},{8,9},{9,8},{10,11... | collective-permute-start | bytes 4718600 | tf_op jit(solution)/shard_map/ppermute | solution.py:45
  155.7 23.0 %collective-permute-start.18 = (bf16[4,112,1024]{2,1,0:T(8,128)(2,1)}, bf16[4,112,1024]{2,1,0:T(8,128)(2,1)S(1)}, u32[]{:S(2)}, u32[]{:S(2)}) collective-permute-start(bf16[4,112,1024]{2,1,0:T(8,128)(2,1)} %get-tuple-element.179), channel_id=1, source_target_pairs={{0,4},{4,0},{8,12},{12,8},{16,20},{20,16},{24,28},{28,24},{1,5},{5... | collective-permute-start | bytes 2752520 | tf_op jit(solution)/shard_map/ppermute | solution.py:45
  156.5 10.7 %collective-permute-start.19 = (bf16[2,96,512]{2,1,0:T(8,128)(2,1)}, bf16[2,96,512]{2,1,0:T(8,128)(2,1)S(1)}, u32[]{:S(2)}, u32[]{:S(2)}) collective-permute-start(bf16[2,96,512]{2,1,0:T(8,128)(2,1)} %get-tuple-element.180), channel_id=1, source_target_pairs={{0,8},{4,12},{8,0},{12,4},{16,24},{20,28},{24,16},{28,20},{1,9},{5... | collective-permute-start | bytes 589832 | tf_op jit(solution)/shard_map/ppermute | solution.py:45
  158.2 17.3 %collective-permute-start.20 = (bf16[2,96,512]{2,1,0:T(8,128)(2,1)}, bf16[2,96,512]{2,1,0:T(8,128)(2,1)S(1)}, u32[]{:S(2)}, u32[]{:S(2)}) collective-permute-start(bf16[2,96,512]{2,1,0:T(8,128)(2,1)} %get-tuple-element.181), channel_id=1, source_target_pairs={{0,16},{4,20},{8,24},{12,28},{16,0},{20,4},{24,8},{28,12},{1,17},{... | collective-permute-start | bytes 589832 | tf_op jit(solution)/shard_map/ppermute | solution.py:45
  160.1 15.5 %collective-permute-start.21 = (bf16[2,96,512]{2,1,0:T(8,128)(2,1)}, bf16[2,96,512]{2,1,0:T(8,128)(2,1)S(1)}, u32[]{:S(2)}, u32[]{:S(2)}) collective-permute-start(bf16[2,96,512]{2,1,0:T(8,128)(2,1)} %get-tuple-element.182), channel_id=1, source_target_pairs={{0,24},{4,28},{8,16},{12,20},{16,8},{20,12},{24,0},{28,4},{1,25},{... | collective-permute-start | bytes 589832 | tf_op jit(solution)/shard_map/ppermute | solution.py:45
  181.3 9.2 %collective-permute-start.25 = (bf16[96,512]{1,0:T(8,128)(2,1)S(1)}, bf16[96,512]{1,0:T(8,128)(2,1)S(1)}, u32[]{:S(2)}, u32[]{:S(2)}) collective-permute-start(bf16[96,512]{1,0:T(8,128)(2,1)S(1)} %fusion.15), channel_id=1, source_target_pairs={{0,4},{4,0},{8,12},{12,8},{16,20},{20,16},{24,28},{28,24},{1,5},{5... | collective-permute-start | bytes 294920 | tf_op jit(solution)/shard_map/ppermute | solution.py:45
  183.5 43.6 %collective-permute-start.26 = (bf16[512,768]{1,0:T(8,128)(2,1)}, bf16[512,768]{1,0:T(8,128)(2,1)}, u32[]{:S(2)}, u32[]{:S(2)}) collective-permute-start(bf16[512,768]{1,0:T(8,128)(2,1)} %fusion.10), channel_id=1, source_target_pairs={{0,2},{1,3},{2,0},{3,1},{4,6},{5,7},{6,4},{7,5},{8,10},{9,11},{10,... | collective-permute-start | bytes 2359304 | tf_op jit(solution)/shard_map/ppermute | solution.py:45
  184.3 10.5 %collective-permute-start.24 = (bf16[112,1024]{1,0:T(8,128)(2,1)S(1)}, bf16[112,1024]{1,0:T(8,128)(2,1)S(1)}, u32[]{:S(2)}, u32[]{:S(2)}) collective-permute-start(bf16[112,1024]{1,0:T(8,128)(2,1)S(1)} %get-tuple-element.247), channel_id=1, source_target_pairs={{0,24},{4,28},{8,16},{12,20},{16,8},{20,12},{24,0},{28,4},{1,25},{... | collective-permute-start | bytes 688136 | tf_op jit(solution)/shard_map/ppermute | solution.py:45
  187.2 19.5 %collective-permute-start.23 = (bf16[112,1024]{1,0:T(8,128)(2,1)S(1)}, bf16[112,1024]{1,0:T(8,128)(2,1)S(1)}, u32[]{:S(2)}, u32[]{:S(2)}) collective-permute-start(bf16[112,1024]{1,0:T(8,128)(2,1)S(1)} %get-tuple-element.248), channel_id=1, source_target_pairs={{0,16},{4,20},{8,24},{12,28},{16,0},{20,4},{24,8},{28,12},{1,17},{... | collective-permute-start | bytes 688136 | tf_op jit(solution)/shard_map/ppermute | solution.py:45
  187.3 19.3 %collective-permute-start.22 = (bf16[112,1024]{1,0:T(8,128)(2,1)S(1)}, bf16[112,1024]{1,0:T(8,128)(2,1)S(1)}, u32[]{:S(2)}, u32[]{:S(2)}) collective-permute-start(bf16[112,1024]{1,0:T(8,128)(2,1)S(1)} %get-tuple-element.249), channel_id=1, source_target_pairs={{0,8},{4,12},{8,0},{12,4},{16,24},{20,28},{24,16},{28,20},{1,9},{5... | collective-permute-start | bytes 688136 | tf_op jit(solution)/shard_map/ppermute | solution.py:45
  222.6 11.5 %all-to-all-start.2 = ((f32[32,1,128]{2,1,0:T(1,128)}), f32[32,1,128]{2,1,0:T(1,128)S(1)}, u32[]{:S(2)}, u32[]{:S(2)}) async-start(f32[32,1,128]{2,1,0:T(1,128)} %get-tuple-element.195), calls=%async_computation.2 | async-start | bytes 32768 | tf_op jit(solution)/shard_map/all_to_all | solution.py:1261
  (39 other events, 342.7 us)

commit v4 on v3

--- a/solution.py
+++ b/solution.py
@@ -15,7 +15,7 @@
 HEAD = 64
 MAPS = 2 * STATE
 LANES = 128
-SMALL = 16
+SMALL = 8
 VMEM = 60 * 1024 * 1024
 
 EPSILON = 1e-05
@@ -53,7 +53,7 @@
 
 
 def together(*values):
-    return lax.optimization_barrier(values)
+    return list(lax.optimization_barrier(values))
 
 
 def gather_far(own, axis, low):
@@ -147,6 +147,8 @@
         state_ref,
         mixed_ref,
         weight_ref,
+        gained_ref,
+        squares_ref,
         tail,
         carried,
         u_own,
@@ -217,6 +219,7 @@
     )
     ended = []
     ends = []
+    squares = None
     for head in range(0, heads, 2):
         lanes = slice(head * HEAD, head * HEAD + LANES)
         wide = [
@@ -239,17 +242,24 @@
             up = dot(top, kept[UP])
             down = dot(jnp.concatenate([cross, last], axis=1), kept)
             first, second = (up, down) if first is None else (first + up, second + down)
-        mixed_ref[:, lanes] = (
+        mixed_own = (
             jnp.concatenate([first, second], axis=0)
             + across[:, lanes] * jnp.exp(own)
             + skip_ref[0:1, lanes] * signal[:, lanes]
         )
+        mixed_ref[:, lanes] = mixed_own
+        gate_own = gate_ref[:, lanes]
+        gated = mixed_own * (gate_own * sigmoid(gate_own))
+        gained_ref[:, lanes] = gated * skip_ref[1:2, lanes]
+        squares = gated * gated if squares is None else squares + gated * gated
         ended.append(pair.astype(F32) * jnp.exp(end - own))
         ends.append(jnp.exp(end))
     fresh = sum(
         dot(b_rows, part, 0, 0) for part in halves(jnp.concatenate(ended, axis=1))
     )
     carried[...] = jnp.concatenate(ends, axis=1) * state + fresh
+    total = jnp.sum(squares, axis=1, keepdims=True)
+    squares_ref[...] = jnp.transpose(jnp.broadcast_to(total, (SPAN, LANES)))[0:8, :]
 
 
 def place_rows(ids, masks, refs, stores):
@@ -285,9 +295,9 @@
             ref[0] = value
 
 
-def rows_live(ids, at, lengths):
-    sequence = at // (LMAX // SPAN)
-    position = (at % (LMAX // SPAN)) * SPAN + lax.broadcasted_iota(jnp.int32, (SPAN, 1), 0)
+def rows_live(ids, at, lengths, span=SPAN):
+    sequence = at // (LMAX // span)
+    position = (at % (LMAX // span)) * span + lax.broadcasted_iota(jnp.int32, (span, 1), 0)
     return position < lengths[sequence]
 
 
@@ -295,9 +305,8 @@
     grad_refs = refs[:owners]
     piece_refs = refs[owners : owners + pieces]
     (
-        gate_ref,
-        mixed_ref,
-        gain_ref,
+        gained_ref,
+        squares_ref,
         merged_grad_ref,
         kept_ref,
         sent_ref,
@@ -306,6 +315,7 @@
         weight,
     ) = refs[owners + pieces :]
     at = pl.program_id(0)
+    span = grad_own.shape[0]
 
     @pl.when(at == 0)
     def _():
@@ -322,19 +332,16 @@
 
     pick_piece(ids, at, own_chunks, grad_refs, grad_own)
     upstream = grad_own[...]
-    upstream = jnp.where(rows_live(ids, at, lengths), upstream, jnp.zeros_like(upstream))
+    upstream = jnp.where(rows_live(ids, at, lengths, span), upstream, jnp.zeros_like(upstream))
     merged_grad = dot(upstream, weight[...])
     merged_grad_ref[...] = merged_grad
-    gate = gate_ref[...]
-    gated = mixed_ref[...] * (gate * sigmoid(gate))
-    gained = gated * gain_ref[0:1, :]
-    squares = jnp.sum(gated * gated, axis=1, keepdims=True)
+    gained = gained_ref[...]
     products = jnp.sum(merged_grad * gained, axis=1, keepdims=True)
     branch = dot(gained.astype(BF), weight[...], 1, 1).astype(BF)
     store_part(ids, at, own_chunks, (kept_ref, sent_ref), branch)
-    lanes = lane_ids((SPAN, LANES))
-    both = jnp.where(lanes == 0, squares, jnp.where(lanes == 1, products, 0.0))
-    sums_ref[...] = jnp.transpose(both)[0:2, :]
+    flat = jnp.transpose(jnp.broadcast_to(products, (span, LANES)))
+    sums_ref[0:1, :] = squares_ref[0:1, :]
+    sums_ref[1:2, :] = flat[0:1, :]
 
 
 def backward_kernel(channels, masks, owners, own_chunks, ids, lengths, *refs):
@@ -643,23 +650,17 @@
             first_ref = first_kept_ref if place < kept_count else first_sent_ref
             position = place if place < kept_count else place - kept_count
             block = ids[0] ^ mask
-            small = jnp.concatenate(
-                [
-                    tap_sum[:, :width],
-                    head_sum[...],
-                    pltpu.roll(
-                        tap_sum[:, width:], (MAPS - block * (MAPS // len(masks))) % MAPS, 1
-                    )[:, :LANES],
-                    pltpu.roll(gain_sum[...], (model - block * rows) % model, 1)[:, :LANES],
-                ],
-                axis=1,
+            conv_part = pltpu.roll(
+                tap_sum[:, width:], (MAPS - block * (MAPS // len(masks))) % MAPS, 1
+            )[:, :LANES]
+            gain_part = pltpu.roll(gain_sum[...], (model - block * rows) % model, 1)[:, :LANES]
+            mixed_part = jnp.concatenate(
+                [conv_part[: CONV + 1], gain_part[0:1], head_sum[0:2, :]], axis=0
             )
-            both = jnp.concatenate(halves(small), axis=0)
+            small = jnp.concatenate([tap_sum[:, :width], mixed_part], axis=1)
+            both = jnp.concatenate(halves(small), axis=1)
             picked = pl.ds(pl.multiple_of(block * rows, 8), rows)
-            first_ref[position, 0:SMALL, : both.shape[1]] = both
-            first_ref[position, 0:SMALL, both.shape[1] :] = jnp.zeros(
-                (SMALL, first - both.shape[1]), BF
-            )
+            first_ref[position, 0:SMALL, :] = both
             first_ref[position, SMALL:, :] = weight_sum[picked, :first].astype(BF)
             second_ref = second_refs[place % kept_count]
             near = place // kept_count
@@ -711,19 +712,22 @@
     )
 
 
+def small_sum(rows):
+    half = rows.shape[1] // 2
+    return rows[:, :half] + rows[:, half:]
+
+
 def pack_kernel(width, tensor_count, ids, kept_ref, *refs):
     received = refs[:-1]
     packed_ref = refs[-1]
     maps_rows = packed_ref.shape[1] - 8
     lanes = slice(2 * width, 2 * width + MAPS)
-    state = kept_ref[SMALL:, lanes]
-    small = kept_ref[0:SMALL, width + LANES : width + LANES + MAPS]
-    for ref in received:
-        state = state + ref[SMALL:, lanes].astype(F32)
-        small = small + ref[0:SMALL, width + LANES : width + LANES + MAPS].astype(F32)
-    small = small[:8] + small[8:]
+    parts = [ref[...].astype(F32) for ref in [kept_ref, *received]]
+    state = sum(part[SMALL:, lanes] for part in parts)
+    small = small_sum(sum(part[:SMALL] for part in parts))[:, width:]
     for at in range(tensor_count):
-        packed_ref[at, 0:8, :] = small
+        packed_ref[at, 0:8, :LANES] = small
+        packed_ref[at, 0:8, LANES:] = small
         packed_ref[at, 8:, :] = state[at * maps_rows : (at + 1) * maps_rows, :]
 
 
@@ -735,7 +739,7 @@
     outs = refs[count + 15 : count + 35]
     norms_ref = refs[count + 35]
     block = whole[SMALL:]
-    small = whole[:8] + whole[8:SMALL]
+    small = small_sum(whole[:SMALL])
     norms = jnp.zeros((1, LANES), F32)
     in_grad = jnp.stack([block[:, :channels], block[:, width : width + channels]], axis=1)
     step_grad = jnp.transpose(rest[:, :LANES])[:heads]
@@ -747,7 +751,7 @@
     ).astype(F32)
     skips = dot(small[:, :width], picker, precision=HIGHEST)
     head_grad = jnp.concatenate(
-        [small[0:2, width : width + LANES], skips[6:7, :]], axis=0
+        [small[6:8, width : width + LANES], skips[6:7, :]], axis=0
     )[:, :heads]
     gradients = (in_grad, step_grad, out_grad, channel_grad, head_grad)
     for position, gradient in enumerate(gradients):
@@ -777,7 +781,7 @@
     ).astype(F32)
     conv_grad = dot(picker, small[:, :LANES], 1, 1, precision=HIGHEST)[:, : CONV + 1]
     gain_grad = pltpu.roll(small[:, LANES:], (LANES - ids[1] * gain_size) % LANES, 1)[
-        0:1, :gain_size
+        CONV + 1 : CONV + 2, :gain_size
     ]
     norms = norms_in_ref[...]
     for position, gradient in enumerate((whole[8:], conv_grad, gain_grad)):
@@ -847,19 +851,18 @@
         axis=1,
     )
     out_low = pad_to(out_proj.astype(BF), 1, width)
-    both_low = jnp.concatenate([in_low, out_low], axis=1)
-    split = in_low.shape[1]
     highs = list(range(dp_low, dp_count, dp_low))
     nears = list(range(1, dp_low))
     tensor_highs = list(range(2, tensor_count, 2))
     landed = together(
         *[exchange(block_input, "tensor", mask) for mask in tensor_highs],
-        *[exchange(both_low, "dp", mask) for mask in highs],
-        *[exchange(both_low, "dp", mask) for mask in nears],
+        *[exchange(in_low, "dp", mask) for mask in highs],
+        *[exchange(in_low, "dp", mask) for mask in nears],
     )
     u_far = dict(zip(tensor_highs, landed))
-    both_far = list(landed[len(tensor_highs) : len(tensor_highs) + len(highs)])
-    both_near = list(landed[len(tensor_highs) + len(highs) :])
+    in_far = landed[len(tensor_highs) : len(tensor_highs) + len(highs)]
+    in_own_near = landed[len(tensor_highs) + len(highs) :]
+    in_stack = jnp.stack(in_far)
     maps_rows = state_proj.shape[0]
     conv_rows = state_conv.shape[0]
     small_own = jnp.concatenate(
@@ -868,9 +871,7 @@
     shared_own = jnp.concatenate(
         [state_proj.astype(BF), pad_to(small_own, 0, MAPS)[None, :]], axis=0
     )
-    shared_own, *both_far = together(shared_own, *both_far)
-    in_stack = jnp.stack([piece[:, :split] for piece in both_far])
-    out_stack = jnp.stack([piece[:, split:] for piece in both_far])
+    in_stack, shared_own = together(in_stack, shared_own)
     shared = lax.all_to_all(
         jnp.broadcast_to(shared_own[None], (everywhere,) + shared_own.shape),
         ("dp", "tensor"),
@@ -878,28 +879,33 @@
         0,
     )
     u_pieces = gather_near(block_input, u_far, "tensor", 2)
+    out_start, in_stack = together(out_low, in_stack)
     shared, *landed = together(
-        shared, *u_pieces[1:], *[exchange(in_stack, "dp", near) for near in nears]
+        shared,
+        *u_pieces[1:],
+        *[exchange(in_stack, "dp", near) for near in nears],
+        *[exchange(out_start, "dp", mask) for mask in highs],
     )
     u_pieces = [block_input] + landed[: tensor_count - 1]
-    in_near = landed[tensor_count - 1 :]
+    in_near = landed[tensor_count - 1 : tensor_count - 1 + len(nears)]
+    out_far = landed[tensor_count - 1 + len(nears) :]
+    out_stack = jnp.stack([out_start] + out_far)
     grad_own, out_stack, *_ = together(output_grad, out_stack, u_far[2])
     grad_far = gather_far(grad_own, "tensor", 2)
     out_near = [exchange(out_stack, "dp", near) for near in nears]
-    in_pieces = [both_low] + both_near + both_far + in_near
+    in_pieces = [in_low] + in_own_near + in_far + in_near
     piece_masks = [0] + nears + highs + [high + near for near in nears for high in highs]
+    out_masks = [0] + highs + [high + near for near in nears for high in [0] + highs]
     direct = rows % 16 == 0
     if not direct:
         order = dp_at ^ jnp.arange(dp_count)
-        order = jnp.array([piece_masks.index(mask) for mask in range(dp_count)])[order]
-
-        def ordered(pieces):
+
+        def ordered(pieces, masks):
             parts = [piece if piece.ndim == 3 else piece[None] for piece in pieces]
-            return jnp.concatenate(parts, axis=0)[order].reshape(model, -1)
-
-        in_pieces = [
-            ordered([piece[:, :split] for piece in [both_low] + both_near + both_far] + in_near)
-        ]
+            places = jnp.array([masks.index(mask) for mask in range(dp_count)])[order]
+            return jnp.concatenate(parts, axis=0)[places].reshape(model, -1)
+
+        in_pieces = [ordered(in_pieces, piece_masks)]
     state_weight = shared[:, :maps_rows].reshape(-1, MAPS)
     small_all = shared[:, maps_rows].astype(F32)
     conv_size = conv_rows * (CONV + 1)
@@ -921,40 +927,46 @@
     skip_gain = pad_to(jnp.stack([skip_wide, channel_wide[CONV + 1]]), 0, 8)
     gain_rows = pad_to(gain_whole[None, :], 0, 8)
 
-    def token_spec(size, reverse=False):
+    block_rows = min(own_count, 2 * SPAN)
+
+    def token_spec(size, reverse=False, span=SPAN):
         if reverse:
             return pl.BlockSpec((SPAN, size), lambda at, *_: (chunks - 1 - at, 0))
-        return pl.BlockSpec((SPAN, size), lambda at, *_: (at, 0))
-
-    def piece_specs(reverse=False):
+        return pl.BlockSpec((span, size), lambda at, *_: (at, 0))
+
+    def piece_specs(reverse=False, span=SPAN):
+        inners = own_count // span
+
         def spec(mask):
             def index(at, ids_ref, *_):
                 block = chunks - 1 - at if reverse else at
-                mine = (block // own_chunks) ^ ids_ref[1] == mask
-                return (jnp.where(mine, block % own_chunks, 0), 0)
-
-            return pl.BlockSpec((SPAN, model), index)
+                mine = (block // inners) ^ ids_ref[1] == mask
+                return (jnp.where(mine, block % inners, 0), 0)
+
+            return pl.BlockSpec((span, model), index)
 
         return [spec(mask) for mask in range(tensor_count)]
 
-    def part_specs(reverse=False):
+    def part_specs(reverse=False, span=SPAN):
+        inners = own_count // span
+
         def spec(odd):
             def index(at, ids_ref, *_):
                 block = chunks - 1 - at if reverse else at
-                owner = block // own_chunks
-                inner = block % own_chunks
+                owner = block // inners
+                inner = block % inners
                 mine = ((owner ^ ids_ref[1]) & 1) == odd
                 if reverse:
                     other = jnp.where(owner > 0, owner - 1, 1)
-                    other_inner = jnp.where(owner > 0, own_chunks - 1, 0)
+                    other_inner = jnp.where(owner > 0, inners - 1, 0)
                 else:
                     last = tensor_count - 1
                     other = jnp.where(owner < last, owner + 1, last - 1)
-                    other_inner = jnp.where(owner < last, 0, own_chunks - 1)
+                    other_inner = jnp.where(owner < last, 0, inners - 1)
                 owner = jnp.where(mine, owner, other)
                 return ((owner ^ ids_ref[1]) >> 1, jnp.where(mine, inner, other_inner), 0)
 
-            return pl.BlockSpec((1, SPAN, model), index)
+            return pl.BlockSpec((1, span, model), index)
 
         return [spec(0), spec(1)]
 
@@ -966,7 +978,7 @@
     )
     if not direct:
         piece_masks = [None]
-    normed, gate_raw, raw, pre, act, step_in, states, mixed, weight = pl.pallas_call(
+    normed, gate_raw, raw, pre, act, step_in, states, mixed, weight, gained, squares = pl.pallas_call(
         functools.partial(forward_kernel, width, len(in_pieces), piece_masks, tensor_count, own_chunks),
         grid_spec=pltpu.PrefetchScalarGridSpec(
             num_scalar_prefetch=1,
@@ -990,6 +1002,8 @@
                 pl.BlockSpec((1, STATE, width), lambda at, *_: (at, 0, 0)),
                 token_spec(width),
                 whole_spec((model, columns)),
+                token_spec(width),
+                pl.BlockSpec((8, SPAN), lambda at, *_: (0, at)),
             ],
             scratch_shapes=[
                 pltpu.VMEM((SPAN + 8, mixed_width), F32),
@@ -1007,6 +1021,8 @@
             struct((chunks, STATE, width)),
             struct((tokens, width)),
             struct((model, columns), BF),
+            struct((tokens, width)),
+            struct((8, tokens)),
         ],
         compiler_params=arbitrary,
         name="ssd_forward",
@@ -1016,30 +1032,29 @@
     grad_far = dict(zip(grad_far, landed))
     out_near = landed[len(grad_far) :]
     grad_pieces = gather_near(grad_own, grad_far, "tensor", 2)
-    out_pieces = [both_low] + both_near + both_far + out_near
+    out_pieces = [out_start] + out_far + out_near
     if not direct:
-        out_pieces = [
-            ordered([piece[:, split:] for piece in [both_low] + both_near + both_far] + out_near)
-        ]
-    gate_gain_rows = pad_to(channel_wide[CONV + 1][None, :], 0, 8)
+        out_pieces = [ordered(out_pieces, out_masks)]
+        out_masks = [None]
     merged_grad, *branch_parts, sums_part = pl.pallas_call(
-        functools.partial(middle_kernel, tensor_count, len(out_pieces), piece_masks, own_chunks),
+        functools.partial(
+            middle_kernel, tensor_count, len(out_pieces), out_masks, own_count // block_rows
+        ),
         grid_spec=pltpu.PrefetchScalarGridSpec(
             num_scalar_prefetch=2,
-            grid=(chunks,),
+            grid=(tokens // block_rows,),
             in_specs=[
-                *piece_specs(),
+                *piece_specs(span=block_rows),
                 *[whole_spec(piece.shape) for piece in out_pieces],
-                token_spec(width),
-                token_spec(width),
-                whole_spec(gate_gain_rows.shape),
+                token_spec(width, span=block_rows),
+                pl.BlockSpec((8, block_rows), lambda at, *_: (0, at)),
             ],
             out_specs=[
-                token_spec(width),
-                *part_specs(),
-                pl.BlockSpec((2, SPAN), lambda at, *_: (0, at)),
+                token_spec(width, span=block_rows),
+                *part_specs(span=block_rows),
+                pl.BlockSpec((2, block_rows), lambda at, *_: (0, at)),
             ],
-            scratch_shapes=[pltpu.VMEM((SPAN, model), BF), pltpu.VMEM((model, width), BF)],
+            scratch_shapes=[pltpu.VMEM((block_rows, model), BF), pltpu.VMEM((model, width), BF)],
         ),
         out_shape=[
             struct((tokens, width)),
@@ -1048,14 +1063,19 @@
         ],
         compiler_params=arbitrary,
         name="gate_middle",
-    )(ids, lengths, *grad_pieces, *out_pieces, gate_raw, mixed, gate_gain_rows)
-
-    branch_total = near_sum(*branch_parts, "tensor", 2)
-    branch_total, *sums = together(
-        branch_total, *[exchange(sums_part, "tensor", mask) for mask in range(1, tensor_count)]
+    )(ids, lengths, *grad_pieces, *out_pieces, gained, squares)
+
+    branch_kept, branch_sent = branch_parts
+    branch_near, *sums = together(
+        exchange(branch_sent, "tensor", 1),
+        *[exchange(sums_part, "tensor", mask) for mask in range(1, tensor_count)],
     )
     sums = [sums_part] + sums
-    branch_far = far_parts(branch_total, "tensor", 2)
+    branch_out = branch_kept[1:].astype(F32) + branch_near[1:].astype(F32)
+    branch_far = [
+        exchange(branch_out[position].astype(BF), "tensor", 2 * position + 2)
+        for position in range(tensor_count // 2 - 1)
+    ]
     masks = slot_masks(dp_count, dp_low)
     first_columns = 2 * width + MAPS
     second_columns = LANES + width
@@ -1161,9 +1181,12 @@
     for values in landed[1 : 1 + len(first_near)]:
         first_total = first_total + values.astype(F32)
     second_far = landed[1 + len(first_near) :]
-    joined = first_total[:, : SMALL // 2] + first_total[:, SMALL // 2 : SMALL]
+    middle = first_columns // 2
+    joined = first_total[:, :SMALL, :middle] + first_total[:, :SMALL, middle:]
     high = lax.reduce_precision(joined, 8, 7)
-    first_total = jnp.concatenate([high, joined - high, first_total[:, SMALL:]], axis=1)
+    first_total = jnp.concatenate(
+        [jnp.concatenate([high, joined - high], axis=2), first_total[:, SMALL:]], axis=1
+    )
     first_parts = [first_total[0]] + far_parts(first_total, "dp", dp_low)
     second_total = seconds_out[0].astype(F32)
     for values in second_far:
@@ -1189,7 +1212,7 @@
     live_own = (position_all % LMAX < length_of)[:, None]
     own_squares = lax.dynamic_slice(sum(part[0] for part in sums), (tensor_at * own_count,), (own_count,))
     own_scale = lax.rsqrt(own_squares / INNER + EPSILON)[:, None]
-    branch = branch_total[0]
+    branch = branch_kept[0].astype(F32) + branch_near[0].astype(F32)
     for values in branch_far:
         branch = branch + values.astype(F32)
     output = (inputs + jnp.where(live_own, branch * own_scale, 0.0)).astype(BF)

time: 239 us -> 235 us (0.983)
  local copies, waits for them, and re-layouts: 21.8 us -> 16.6 us
  starting transfers between devices: 39.9 us -> 43.6 us
  waiting for transfers between devices: 62.2 us -> 58.5 us
    ppermute x27 -> x30, starting transfers between devices: 28.2 us -> 33.1 us  [exchange(): return lax.ppermute(values, axis, [(at, at ^ mask) for at in range(count)])]
    another operation x4 -> x0, local copies, waits for them, and re-layouts: 3.79 us -> none  [the longest x2 1.96 us: local(): in_stack = jnp.stack([piece[:, :split] for piece in both_far])]
    ppermute x27 -> x30, waiting for transfers between devices: 60.6 us -> 57.3 us  [exchange(): return lax.ppermute(values, axis, [(at, at ^ mask) for at in range(count)])]
    another operation x3 -> x4, other arithmetic: 0.94 us -> 3.63 us  [the longest x1 2.04 us: local(): out_stack = jnp.stack([out_start] + out_far)]
    unnamed x62 -> x72, local copies, waits for them, and re-layouts: 7.76 us -> 8.61 us
  transfers between devices with their start and end apart: 30 -> 33, of which waited for: 11 -> 13; matrix products, arithmetic and copies ran while one was open for 11% -> 10% of each run, Pallas kernels for 34% -> 35%
where the time goes in v4:
time: 235 us; the launch traced here: 234 us
  Pallas kernels  94.9 us (40%)
  waiting for transfers between devices  58.5 us (25%)
  starting transfers between devices  43.6 us (19%)
  other arithmetic  18.4 us (8%)
  local copies, waits for them, and re-layouts  16.6 us (7%)
    ppermute x30, waiting for transfers between devices, exchange(): return lax.ppermute(values, axis, [(at, at ^ mask) for at in range(count)])  57.3 us
    pallas_call x1, Pallas kernels, local(): pl.pallas_call(functools.partial(backward_kernel, width, masks, tensor_co...  45.9 us
    ppermute x30, starting transfers between devices, exchange(): return lax.ppermute(values, axis, [(at, at ^ mask) for at in range(count)])  33.1 us
    pallas_call x1, Pallas kernels, local(): pl.pallas_call(functools.partial(forward_kernel, width, len(in_pieces), p...  26.2 us
    pallas_call x4, Pallas kernels, whole_call(): pl.pallas_call(kernel, grid_spec=pltpu.PrefetchScalarGridSpec(num_scalar_...  13.1 us
    pallas_call x1, Pallas kernels, local(): pl.pallas_call(functools.partial(middle_kernel, tensor_count, len(out_pie...  9.75 us
    unnamed x72, local copies, waits for them, and re-layouts  8.61 us
  transfers between devices with their start and end apart: 33, of which 13 were waited for; matrix products, arithmetic and copies ran while one was open for 10% of the time, Pallas kernels for 35%

profile of v4, /device:TPU:0, one launch (start us, length us, event | category | flops | bytes accessed | tf_op | source)
XLA Modules:
  0.0 234.2 jit_solution(9463217230428999265)
XLA Ops:
  0.7 3.0 %collective-permute-start = (bf16[512,768]{1,0:T(8,128)(2,1)}, bf16[512,768]{1,0:T(8,128)(2,1)S(1)}, u32[]{:S(2)}, u32[]{:S(2)}) collective-permute-start(bf16[512,768]{1,0:T(8,128)(2,1)} %refs_0_.5), channel_id=1, source_target_pairs={{0,2},{1,3},{2,0},{3,1},{4,6},{5,7},{6,4},{7,5},{8,10},{9,11},{10,... | collective-permute-start | bytes 2359304 | tf_op jit(solution)/shard_map/ppermute | solution.py:45
  7.2 3.6 %collective-permute-start.3 = (bf16[96,896]{1,0:T(8,128)(2,1)S(1)}, bf16[96,896]{1,0:T(8,128)(2,1)S(1)}, u32[]{:S(2)}, u32[]{:S(2)}) collective-permute-start(bf16[96,896]{1,0:T(8,128)(2,1)S(1)} %fusion.12.refs_4_), channel_id=1, source_target_pairs={{0,24},{4,28},{8,16},{12,20},{16,8},{20,12},{24,0},{28,4},{1,25},{... | collective-permute-start | bytes 516104 | tf_op jit(solution)/shard_map/ppermute | solution.py:45
  13.9 2.4 %collective-permute-done.3.refs_8_ = bf16[96,896]{1,0:T(8,128)(2,1)S(1)} collective-permute-done((bf16[96,896]{1,0:T(8,128)(2,1)S(1)}, bf16[96,896]{1,0:T(8,128)(2,1)S(1)}, u32[]{:S(2)}, u32[]{:S(2)}) %collective-permute-start.3) | collective-permute-done | bytes 172064 | tf_op jit(solution)/shard_map/ppermute | solution.py:45
  16.3 8.5 %collective-permute-done.2.refs_7_ = bf16[96,896]{1,0:T(8,128)(2,1)S(1)} collective-permute-done((bf16[96,896]{1,0:T(8,128)(2,1)S(1)}, bf16[96,896]{1,0:T(8,128)(2,1)S(1)}, u32[]{:S(2)}, u32[]{:S(2)}) %collective-permute-start.2) | collective-permute-done | bytes 172064 | tf_op jit(solution)/shard_map/ppermute | solution.py:45
  26.5 3.3 %all-to-all-start = ((bf16[32,25,256]{2,1,0:T(8,128)(2,1)}), bf16[32,25,256]{2,1,0:T(8,128)(2,1)}, u32[]{:S(2)}, u32[]{:S(2)}) async-start(bf16[32,25,256]{2,1,0:T(8,128)(2,1)} %broadcast_in_dim.52), calls=%async_computation | async-start | bytes 1048576 | tf_op jit(solution)/shard_map/all_to_all | solution.py:875
  34.6 3.5 %collective-permute-start.10 = (bf16[96,384]{1,0:T(8,128)(2,1)}, bf16[96,384]{1,0:T(8,128)(2,1)S(1)}, u32[]{:S(2)}, u32[]{:S(2)}) collective-permute-start(bf16[96,384]{1,0:T(8,128)(2,1)} %convert_element_type.144.refs_4_), channel_id=1, source_target_pairs={{0,24},{4,28},{8,16},{12,20},{16,8},{20,12},{24,0},{28,4},{1,25},{... | collective-permute-start | bytes 221192 | tf_op jit(solution)/shard_map/ppermute | solution.py:45
  39.6 5.4 %collective-permute-done.10.refs_7_ = bf16[96,384]{1,0:T(8,128)(2,1)S(1)} collective-permute-done((bf16[96,384]{1,0:T(8,128)(2,1)}, bf16[96,384]{1,0:T(8,128)(2,1)S(1)}, u32[]{:S(2)}, u32[]{:S(2)}) %collective-permute-start.10) | collective-permute-done | bytes 73760 | tf_op jit(solution)/shard_map/ppermute | solution.py:45
  45.0 6.1 %collective-permute-done.9.refs_6_ = bf16[96,384]{1,0:T(8,128)(2,1)S(1)} collective-permute-done((bf16[96,384]{1,0:T(8,128)(2,1)}, bf16[96,384]{1,0:T(8,128)(2,1)S(1)}, u32[]{:S(2)}, u32[]{:S(2)}) %collective-permute-start.9) | collective-permute-done | bytes 73760 | tf_op jit(solution)/shard_map/ppermute | solution.py:45
  61.2 26.2 %ssd_forward.1 = (bf16[2048,768]{1,0:T(8,128)(2,1)}, f32[2048,384]{1,0:T(8,128)}, f32[2048,640]{1,0:T(8,128)}, f32[2048,640]{1,0:T(8,128)}, bf16[2048,640]{1,0:T...) custom-call(s32[2]{0:T(128)} %pad_add_fusion.ids, ...), custom_call_target="tpu_custom_call" | custom-call | tf_op jit(solution)/shard_map/ssd_forward/pallas_call | solution.py:981
  90.9 9.7 %gate_middle.1 = (f32[2048,384]{1,0:T(8,128)}, bf16[2,512,768]{2,1,0:T(8,128)(2,1)}, bf16[2,512,768]{2,1,0:T(8,128)(2,1)}, f32[2,2048]{1,0:T(2,128)}) custom-call(s32[2]{0:T(128)} %pad_add_fusion.ids, s32[1]{0:T(128)} %copy.80.lengths, bf16[512,768]{1,0:T(8,128)(2,1)} %refs_4_.1, bf16[512,768]{1,0:T(8,128)(2,1)} %copy-done.6, ...), custom_call_target="tpu_custom_call" | custom-call | tf_op jit(solution)/shard_map/gate_middle/pallas_call | solution.py:1039
  109.4 45.9 %ssd_backward.1 = (bf16[2,512,768]{2,1,0:T(8,128)(2,1)}, bf16[2,512,768]{2,1,0:T(8,128)(2,1)}, bf16[4,104,1024]{2,1,0:T(8,128)(2,1)}, bf16[4,104,1024]{2,1,0:T(8...) custom-call(s32[2]{0:T(128)} %pad_add_fusion.ids, ...), custom_call_target="tpu_custom_call" | custom-call | tf_op jit(solution)/shard_map/ssd_backward/pallas_call | solution.py:1084
  158.7 2.4 %collective-permute-start.24 = (bf16[2,96,512]{2,1,0:T(8,128)(2,1)}, bf16[2,96,512]{2,1,0:T(8,128)(2,1)S(1)}, u32[]{:S(2)}, u32[]{:S(2)}) collective-permute-start(bf16[2,96,512]{2,1,0:T(8,128)(2,1)} %get-tuple-element.192), channel_id=1, source_target_pairs={{0,24},{4,28},{8,16},{12,20},{16,8},{20,12},{24,0},{28,4},{1,25},{... | collective-permute-start | bytes 589832 | tf_op jit(solution)/shard_map/ppermute | solution.py:45
  161.3 5.8 %collective-permute-done.22 = bf16[2,96,512]{2,1,0:T(8,128)(2,1)S(1)} collective-permute-done((bf16[2,96,512]{2,1,0:T(8,128)(2,1)}, bf16[2,96,512]{2,1,0:T(8,128)(2,1)S(1)}, u32[]{:S(2)}, u32[]{:S(2)}) %collective-permute-start.22) | collective-permute-done | bytes 196640 | tf_op jit(solution)/shard_map/ppermute | solution.py:45
  167.0 7.1 %collective-permute-done.23 = bf16[2,96,512]{2,1,0:T(8,128)(2,1)S(1)} collective-permute-done((bf16[2,96,512]{2,1,0:T(8,128)(2,1)}, bf16[2,96,512]{2,1,0:T(8,128)(2,1)S(1)}, u32[]{:S(2)}, u32[]{:S(2)}) %collective-permute-start.23) | collective-permute-done | bytes 196640 | tf_op jit(solution)/shard_map/ppermute | solution.py:45
  174.2 3.6 %collective-permute-done.21 = bf16[4,104,1024]{2,1,0:T(8,128)(2,1)S(1)} collective-permute-done((bf16[4,104,1024]{2,1,0:T(8,128)(2,1)}, bf16[4,104,1024]{2,1,0:T(8,128)(2,1)S(1)}, u32[]{:S(2)}, u32[]{:S(2)}) %collective-permute-start.21) | collective-permute-done | bytes 852000 | tf_op jit(solution)/shard_map/ppermute | solution.py:45
  189.3 4.0 %collective-permute-done.27.refs_2_.refs_3_ = bf16[104,1024]{1,0:T(8,128)(2,1)S(1)} collective-permute-done((bf16[104,1024]{1,0:T(8,128)(2,1)S(1)}, bf16[104,1024]{1,0:T(8,128)(2,1)S(1)}, u32[]{:S(2)}, u32[]{:S(2)}) %collective-permute-start.27) | collective-permute-done | bytes 213024 | tf_op jit(solution)/shard_map/ppermute | solution.py:45
  193.4 10.5 %collective-permute-done.26.refs_1_.refs_2_ = bf16[104,1024]{1,0:T(8,128)(2,1)S(1)} collective-permute-done((bf16[104,1024]{1,0:T(8,128)(2,1)S(1)}, bf16[104,1024]{1,0:T(8,128)(2,1)S(1)}, u32[]{:S(2)}, u32[]{:S(2)}) %collective-permute-start.26) | collective-permute-done | bytes 213024 | tf_op jit(solution)/shard_map/ppermute | solution.py:45
  205.2 2.6 %pack_maps.1 = f32[4,32,256]{2,1,0:T(8,128)} custom-call(s32[2]{0:T(128)} %pad_add_fusion.ids, f32[104,1024]{1,0:T(8,128)} %slice_bitcast_fusion.1.kept_ref.refs_0_, bf16[104,1024]{1,0:T(8,128)(2,1)} %copy-done.15, bf16[104,1024]{1,0:T(8,128)(2,1)} %copy-done.14, bf16[104,1024]{1,0:T(8,128)(2,1)} %copy-done.13), custom_call_target="tpu_custom_call" | custom-call | tf_op jit(solution)/shard_map/pack_maps/pallas_call | solution.py:1235
  207.8 3.3 %all-to-all-start.1 = ((f32[4,32,256]{2,1,0:T(8,128)}), f32[4,32,256]{2,1,0:T(8,128)S(1)}, u32[]{:S(2)}, u32[]{:S(2)}) async-start(f32[4,32,256]{2,1,0:T(8,128)} %pack_maps.1), calls=%async_computation.1 | async-start | bytes 262144 | tf_op jit(solution)/shard_map/all_to_all | solution.py:1254
  211.2 5.3 %lamb_wide.1 = (f32[96,2,384]{2,1,0:T(2,128)}, f32[6,96]{1,0:T(8,128)}, f32[96,384]{1,0:T(8,128)}, f32[6,384]{1,0:T(8,128)}, f32[3,6]{1,0:T(4,128)}, /*index=5*/...) custom-call(s32[2]{0:T(128)} %pad_add_fusion.ids, ...), custom_call_target="tpu_custom_call" | custom-call | tf_op jit(solution)/shard_map/lamb_wide/pallas_call | solution.py:1235
  217.2 2.5 %lamb_maps.1 = (f32[24,256]{1,0:T(8,128)}, f32[8,5]{1,0:T(8,128)}, f32[1,24]{1,0:T(1,128)}, f32[24,256]{1,0:T(8,128)}, f32[8,5]{1,0:T(8,128)}, /*index=5*/f32[1,...) custom-call(s32[2]{0:T(128)} %pad_add_fusion.ids, ...), custom_call_target="tpu_custom_call" | custom-call | tf_op jit(solution)/shard_map/lamb_maps/pallas_call | solution.py:1235
  219.8 3.9 %all-to-all-start.2 = ((f32[32,1,128]{2,1,0:T(1,128)}), f32[32,1,128]{2,1,0:T(1,128)S(1)}, u32[]{:S(2)}, u32[]{:S(2)}) async-start(f32[32,1,128]{2,1,0:T(1,128)} %get-tuple-element.205), calls=%async_computation.2 | async-start | bytes 32768 | tf_op jit(solution)/shard_map/all_to_all | solution.py:1284
  226.0 3.5 %fusion.4 = (bf16[512,768]{1,0:T(8,128)(2,1)}, f32[512,768]{1,0:T(8,128)}) fusion(bf16[512,768]{1,0:T(8,128)(2,1)S(1)} %copy-done, bf16[512,768]{1,0:T(8,128)(2,1)} %copy-done.16, f32[512]{0:T(512)S(1)} %bitcast.85, bf16[2,512,768]{2,1,0:T(8,128)(2,1)} %copy-done.9, bf16[2,512,768]{2,1,0:T(8,128)(2,1)S(1)} %copy-done.8, pred[512]{0:T(512)(128)(4,1)S(1)} %fusion.15, ...), kind=kLoop, calls=%fused_computation.11 | loop fusion | flops 7471104 | bytes 8662528 | tf_op jit(solution)/shard_map/convert_element_type | solution.py:1218
  231.3 2.7 %lamb_update.1 = (f32[96,2,384]{2,1,0:T(2,128)}, f32[6,96]{1,0:T(8,128)}, f32[96,384]{1,0:T(8,128)}, f32[6,384]{1,0:T(8,128)}, f32[3,6]{1,0:T(4,128)}, /*index=5...) custom-call(s32[2]{0:T(128)} %pad_add_fusion.ids, f32[32,1,128]{2,1,0:T(1,128)} %copy-done.28, ...), custom_call_target="tpu_custom_call" | custom-call | tf_op jit(solution)/shard_map/lamb_update/pallas_call | solution.py:1235
  (179 shorter events, 57.3 us)
Async XLA Ops:
  0.7 24.1 %collective-permute-start = (bf16[512,768]{1,0:T(8,128)(2,1)}, bf16[512,768]{1,0:T(8,128)(2,1)S(1)}, u32[]{:S(2)}, u32[]{:S(2)}) collective-permute-start(bf16[512,768]{1,0:T(8,128)(2,1)} %refs_0_.5), channel_id=1, source_target_pairs={{0,2},{1,3},{2,0},{3,1},{4,6},{5,7},{6,4},{7,5},{8,10},{9,11},{10,... | collective-permute-start | bytes 2359304 | tf_op jit(solution)/shard_map/ppermute | solution.py:45
  10.8 14.0 %collective-permute-start.2 = (bf16[96,896]{1,0:T(8,128)(2,1)S(1)}, bf16[96,896]{1,0:T(8,128)(2,1)S(1)}, u32[]{:S(2)}, u32[]{:S(2)}) collective-permute-start(bf16[96,896]{1,0:T(8,128)(2,1)S(1)} %fusion.12.refs_4_), channel_id=1, source_target_pairs={{0,16},{4,20},{8,24},{12,28},{16,0},{20,4},{24,8},{28,12},{1,17},{... | collective-permute-start | bytes 516104 | tf_op jit(solution)/shard_map/ppermute | solution.py:45
  10.8 14.0 %collective-permute-start.1 = (bf16[96,896]{1,0:T(8,128)(2,1)S(1)}, bf16[96,896]{1,0:T(8,128)(2,1)S(1)}, u32[]{:S(2)}, u32[]{:S(2)}) collective-permute-start(bf16[96,896]{1,0:T(8,128)(2,1)S(1)} %fusion.12.refs_4_), channel_id=1, source_target_pairs={{0,8},{4,12},{8,0},{12,4},{16,24},{20,28},{24,16},{28,20},{1,9},{5... | collective-permute-start | bytes 516104 | tf_op jit(solution)/shard_map/ppermute | solution.py:45
  13.9 24.2 %collective-permute-start.5 = (bf16[512,768]{1,0:T(8,128)(2,1)}, bf16[512,768]{1,0:T(8,128)(2,1)S(1)}, u32[]{:S(2)}, u32[]{:S(2)}) collective-permute-start(bf16[512,768]{1,0:T(8,128)(2,1)} %refs_0_.5), channel_id=1, source_target_pairs={{0,1},{1,0},{2,3},{3,2},{4,5},{5,4},{6,7},{7,6},{8,9},{9,8},{10,11... | collective-permute-start | bytes 2359304 | tf_op jit(solution)/shard_map/ppermute | solution.py:45
  26.5 25.2 %all-to-all-start = ((bf16[32,25,256]{2,1,0:T(8,128)(2,1)}), bf16[32,25,256]{2,1,0:T(8,128)(2,1)}, u32[]{:S(2)}, u32[]{:S(2)}) async-start(bf16[32,25,256]{2,1,0:T(8,128)(2,1)} %broadcast_in_dim.52), calls=%async_computation | async-start | bytes 1048576 | tf_op jit(solution)/shard_map/all_to_all | solution.py:875
  29.9 21.8 %collective-permute-start.6 = (bf16[512,768]{1,0:T(8,128)(2,1)S(1)}, bf16[512,768]{1,0:T(8,128)(2,1)S(1)}, u32[]{:S(2)}, u32[]{:S(2)}) collective-permute-start(bf16[512,768]{1,0:T(8,128)(2,1)S(1)} %collective-permute-done.refs_2_), channel_id=1, source_target_pairs={{0,1},{1,0},{2,3},{3,2},{4,5},{5,4},{6,7},{7,6},{8,9},{9,8},{10,11... | collective-permute-start | bytes 2359304 | tf_op jit(solution)/shard_map/ppermute | solution.py:45
  31.5 19.5 %collective-permute-start.7 = (bf16[3,96,896]{2,1,0:T(8,128)(2,1)}, bf16[3,96,896]{2,1,0:T(8,128)(2,1)}, u32[]{:S(2)}, u32[]{:S(2)}) collective-permute-start(bf16[3,96,896]{2,1,0:T(8,128)(2,1)} %pad_maximum_fusion.1), channel_id=1, source_target_pairs={{0,4},{4,0},{8,12},{12,8},{16,20},{20,16},{24,28},{28,24},{1,5},{5... | collective-permute-start | bytes 1548296 | tf_op jit(solution)/shard_map/ppermute | solution.py:45
  34.6 10.3 %collective-permute-start.10 = (bf16[96,384]{1,0:T(8,128)(2,1)}, bf16[96,384]{1,0:T(8,128)(2,1)S(1)}, u32[]{:S(2)}, u32[]{:S(2)}) collective-permute-start(bf16[96,384]{1,0:T(8,128)(2,1)} %convert_element_type.144.refs_4_), channel_id=1, source_target_pairs={{0,24},{4,28},{8,16},{12,20},{16,8},{20,12},{24,0},{28,4},{1,25},{... | collective-permute-start | bytes 221192 | tf_op jit(solution)/shard_map/ppermute | solution.py:45
  38.1 13.0 %collective-permute-start.9 = (bf16[96,384]{1,0:T(8,128)(2,1)}, bf16[96,384]{1,0:T(8,128)(2,1)S(1)}, u32[]{:S(2)}, u32[]{:S(2)}) collective-permute-start(bf16[96,384]{1,0:T(8,128)(2,1)} %convert_element_type.144.refs_4_), channel_id=1, source_target_pairs={{0,16},{4,20},{8,24},{12,28},{16,0},{20,4},{24,8},{28,12},{1,17},{... | collective-permute-start | bytes 221192 | tf_op jit(solution)/shard_map/ppermute | solution.py:45
  38.1 13.0 %collective-permute-start.8 = (bf16[96,384]{1,0:T(8,128)(2,1)}, bf16[96,384]{1,0:T(8,128)(2,1)S(1)}, u32[]{:S(2)}, u32[]{:S(2)}) collective-permute-start(bf16[96,384]{1,0:T(8,128)(2,1)} %convert_element_type.144.refs_4_), channel_id=1, source_target_pairs={{0,8},{4,12},{8,0},{12,4},{16,24},{20,28},{24,16},{28,20},{1,9},{5... | collective-permute-start | bytes 221192 | tf_op jit(solution)/shard_map/ppermute | solution.py:45
  53.8 33.6 %collective-permute-start.12 = (bf16[512,768]{1,0:T(8,128)(2,1)S(1)}, bf16[512,768]{1,0:T(8,128)(2,1)}, u32[]{:S(2)}, u32[]{:S(2)}) collective-permute-start(bf16[512,768]{1,0:T(8,128)(2,1)S(1)} %copy-done.1), channel_id=1, source_target_pairs={{0,2},{1,3},{2,0},{3,1},{4,6},{5,7},{6,4},{7,5},{8,10},{9,11},{10,... | collective-permute-start | bytes 2359304 | tf_op jit(solution)/shard_map/ppermute | solution.py:45
  55.4 33.1 %collective-permute-start.11 = (bf16[512,768]{1,0:T(8,128)(2,1)S(1)}, bf16[512,768]{1,0:T(8,128)(2,1)S(1)}, u32[]{:S(2)}, u32[]{:S(2)}) collective-permute-start(bf16[512,768]{1,0:T(8,128)(2,1)S(1)} %copy-done.1), channel_id=1, source_target_pairs={{0,1},{1,0},{2,3},{3,2},{4,5},{5,4},{6,7},{7,6},{8,9},{9,8},{10,11... | collective-permute-start | bytes 2359304 | tf_op jit(solution)/shard_map/ppermute | solution.py:45
  58.9 28.5 %collective-permute-start.13 = (bf16[4,96,384]{2,1,0:T(8,128)(2,1)}, bf16[4,96,384]{2,1,0:T(8,128)(2,1)}, u32[]{:S(2)}, u32[]{:S(2)}) collective-permute-start(bf16[4,96,384]{2,1,0:T(8,128)(2,1)} %pad_maximum_fusion.2), channel_id=1, source_target_pairs={{0,4},{4,0},{8,12},{12,8},{16,20},{20,16},{24,28},{28,24},{1,5},{5... | collective-permute-start | bytes 884744 | tf_op jit(solution)/shard_map/ppermute | solution.py:45
  107.8 47.5 %collective-permute-start.19 = (bf16[512,768]{1,0:T(8,128)(2,1)S(1)}, bf16[512,768]{1,0:T(8,128)(2,1)S(1)}, u32[]{:S(2)}, u32[]{:S(2)}) collective-permute-start(bf16[512,768]{1,0:T(8,128)(2,1)S(1)} %fusion.9), channel_id=1, source_target_pairs={{0,2},{1,3},{2,0},{3,1},{4,6},{5,7},{6,4},{7,5},{8,10},{9,11},{10,... | collective-permute-start | bytes 2359304 | tf_op jit(solution)/shard_map/ppermute | solution.py:45
  155.2 18.9 %collective-permute-start.20 = (bf16[2,512,768]{2,1,0:T(8,128)(2,1)}, bf16[2,512,768]{2,1,0:T(8,128)(2,1)S(1)}, u32[]{:S(2)}, u32[]{:S(2)}) collective-permute-start(bf16[2,512,768]{2,1,0:T(8,128)(2,1)} %get-tuple-element.188), channel_id=1, source_target_pairs={{0,1},{1,0},{2,3},{3,2},{4,5},{5,4},{6,7},{7,6},{8,9},{9,8},{10,11... | collective-permute-start | bytes 4718600 | tf_op jit(solution)/shard_map/ppermute | solution.py:45
  156.2 21.5 %collective-permute-start.21 = (bf16[4,104,1024]{2,1,0:T(8,128)(2,1)}, bf16[4,104,1024]{2,1,0:T(8,128)(2,1)S(1)}, u32[]{:S(2)}, u32[]{:S(2)}) collective-permute-start(bf16[4,104,1024]{2,1,0:T(8,128)(2,1)} %get-tuple-element.189), channel_id=1, source_target_pairs={{0,4},{4,0},{8,12},{12,8},{16,20},{20,16},{24,28},{28,24},{1,5},{5... | collective-permute-start | bytes 2555912 | tf_op jit(solution)/shard_map/ppermute | solution.py:45
  156.8 10.3 %collective-permute-start.22 = (bf16[2,96,512]{2,1,0:T(8,128)(2,1)}, bf16[2,96,512]{2,1,0:T(8,128)(2,1)S(1)}, u32[]{:S(2)}, u32[]{:S(2)}) collective-permute-start(bf16[2,96,512]{2,1,0:T(8,128)(2,1)} %get-tuple-element.190), channel_id=1, source_target_pairs={{0,8},{4,12},{8,0},{12,4},{16,24},{20,28},{24,16},{28,20},{1,9},{5... | collective-permute-start | bytes 589832 | tf_op jit(solution)/shard_map/ppermute | solution.py:45
  156.8 17.3 %collective-permute-start.23 = (bf16[2,96,512]{2,1,0:T(8,128)(2,1)}, bf16[2,96,512]{2,1,0:T(8,128)(2,1)S(1)}, u32[]{:S(2)}, u32[]{:S(2)}) collective-permute-start(bf16[2,96,512]{2,1,0:T(8,128)(2,1)} %get-tuple-element.191), channel_id=1, source_target_pairs={{0,16},{4,20},{8,24},{12,28},{16,0},{20,4},{24,8},{28,12},{1,17},{... | collective-permute-start | bytes 589832 | tf_op jit(solution)/shard_map/ppermute | solution.py:45
  158.7 15.4 %collective-permute-start.24 = (bf16[2,96,512]{2,1,0:T(8,128)(2,1)}, bf16[2,96,512]{2,1,0:T(8,128)(2,1)S(1)}, u32[]{:S(2)}, u32[]{:S(2)}) collective-permute-start(bf16[2,96,512]{2,1,0:T(8,128)(2,1)} %get-tuple-element.192), channel_id=1, source_target_pairs={{0,24},{4,28},{8,16},{12,20},{16,8},{20,12},{24,0},{28,4},{1,25},{... | collective-permute-start | bytes 589832 | tf_op jit(solution)/shard_map/ppermute | solution.py:45
  182.5 41.2 %collective-permute-start.29 = (bf16[512,768]{1,0:T(8,128)(2,1)}, bf16[512,768]{1,0:T(8,128)(2,1)}, u32[]{:S(2)}, u32[]{:S(2)}) collective-permute-start(bf16[512,768]{1,0:T(8,128)(2,1)} %fusion.10), channel_id=1, source_target_pairs={{0,2},{1,3},{2,0},{3,1},{4,6},{5,7},{6,4},{7,5},{8,10},{9,11},{10,... | collective-permute-start | bytes 2359304 | tf_op jit(solution)/shard_map/ppermute | solution.py:45
  183.2 10.2 %collective-permute-start.27 = (bf16[104,1024]{1,0:T(8,128)(2,1)S(1)}, bf16[104,1024]{1,0:T(8,128)(2,1)S(1)}, u32[]{:S(2)}, u32[]{:S(2)}) collective-permute-start(bf16[104,1024]{1,0:T(8,128)(2,1)S(1)} %get-tuple-element.257), channel_id=1, source_target_pairs={{0,24},{4,28},{8,16},{12,20},{16,8},{20,12},{24,0},{28,4},{1,25},{... | collective-permute-start | bytes 638984 | tf_op jit(solution)/shard_map/ppermute | solution.py:45
  184.6 19.3 %collective-permute-start.26 = (bf16[104,1024]{1,0:T(8,128)(2,1)S(1)}, bf16[104,1024]{1,0:T(8,128)(2,1)S(1)}, u32[]{:S(2)}, u32[]{:S(2)}) collective-permute-start(bf16[104,1024]{1,0:T(8,128)(2,1)S(1)} %get-tuple-element.258), channel_id=1, source_target_pairs={{0,16},{4,20},{8,24},{12,28},{16,0},{20,4},{24,8},{28,12},{1,17},{... | collective-permute-start | bytes 638984 | tf_op jit(solution)/shard_map/ppermute | solution.py:45
  186.3 17.6 %collective-permute-start.25 = (bf16[104,1024]{1,0:T(8,128)(2,1)S(1)}, bf16[104,1024]{1,0:T(8,128)(2,1)S(1)}, u32[]{:S(2)}, u32[]{:S(2)}) collective-permute-start(bf16[104,1024]{1,0:T(8,128)(2,1)S(1)} %get-tuple-element.259), channel_id=1, source_target_pairs={{0,8},{4,12},{8,0},{12,4},{16,24},{20,28},{24,16},{28,20},{1,9},{5... | collective-permute-start | bytes 638984 | tf_op jit(solution)/shard_map/ppermute | solution.py:45
  219.8 11.0 %all-to-all-start.2 = ((f32[32,1,128]{2,1,0:T(1,128)}), f32[32,1,128]{2,1,0:T(1,128)S(1)}, u32[]{:S(2)}, u32[]{:S(2)}) async-start(f32[32,1,128]{2,1,0:T(1,128)} %get-tuple-element.205), calls=%async_computation.2 | async-start | bytes 32768 | tf_op jit(solution)/shard_map/all_to_all | solution.py:1284
  (47 other events, 498.0 us)

commit v5 on v4

--- a/solution.py
+++ b/solution.py
@@ -15,7 +15,7 @@
 HEAD = 64
 MAPS = 2 * STATE
 LANES = 128
-SMALL = 8
+SMALL = 16
 VMEM = 60 * 1024 * 1024
 
 EPSILON = 1e-05
@@ -344,13 +344,63 @@
     sums_ref[1:2, :] = flat[0:1, :]
 
 
+def early_kernel(owners, inners, ids, lengths, *refs):
+    grad_refs = refs[:owners]
+    (
+        sums_ref,
+        normed_ref,
+        gate_ref,
+        mixed_ref,
+        merged_grad_ref,
+        skip_ref,
+        slots_ref,
+        grad_own,
+        gate_sum,
+        out_sum,
+    ) = refs[owners:]
+    at = pl.program_id(0)
+    span = grad_own.shape[0]
+
+    @pl.when(at == 0)
+    def _():
+        gate_sum[...] = jnp.zeros_like(gate_sum)
+        out_sum[...] = jnp.zeros_like(out_sum)
+
+    pick_piece(ids, at, inners, grad_refs, grad_own)
+    upstream = grad_own[...]
+    upstream = jnp.where(rows_live(ids, at, lengths, span), upstream, jnp.zeros_like(upstream))
+    gate_scale, cross = scale_columns(sums_ref[...])
+    gate = gate_ref[...]
+    gate_s = sigmoid(gate)
+    mixed = mixed_ref[...]
+    gated = mixed * (gate * gate_s)
+    gain = skip_ref[1:2, :]
+    merged = (gated * gate_scale * gain).astype(BF)
+    gated_grad = gate_scale * (merged_grad_ref[...] * gain) - gated * cross
+    gate_grad = gated_grad * mixed * (gate_s * (1.0 + gate * (1.0 - gate_s)))
+    out_sum[...] += dot(merged, upstream, 0, 0)
+    gate_sum[...] += dot(gate_grad.astype(BF), normed_ref[...], 0, 0)
+
+    @pl.when(at == pl.num_programs(0) - 1)
+    def _():
+        count, rows, columns = slots_ref.shape
+        both = jnp.concatenate(
+            [jnp.transpose(gate_sum[...]), jnp.transpose(out_sum[...])], axis=1
+        ).astype(BF)
+        slots_ref[...] = both.reshape(count, rows, columns)
+
+
+def scale_columns(sums):
+    scale_row = lax.rsqrt(sums[0:1, :] / INNER + EPSILON)
+    cross_row = scale_row * scale_row * scale_row * (sums[1:2, :] / INNER)
+    row_ids = lax.broadcasted_iota(jnp.int32, (LANES, sums.shape[1]), 0)
+    columns = jnp.transpose(jnp.where(row_ids == 0, scale_row, cross_row))
+    return columns[:, 0:1], columns[:, 1:2]
+
+
 def backward_kernel(channels, masks, owners, own_chunks, ids, lengths, *refs):
     u_refs = refs[:owners]
-    grad_refs = refs[owners : 2 * owners]
-    sums_refs = refs[2 * owners : 3 * owners]
-    backward_step(
-        channels, masks, own_chunks, ids, lengths, u_refs, grad_refs, sums_refs, *refs[3 * owners :]
-    )
+    backward_step(channels, masks, own_chunks, ids, lengths, u_refs, (), *refs[owners:])
 
 
 def backward_step(
@@ -416,13 +466,10 @@
     carried,
     ahead,
     weight_sum,
-    out_sum,
     tap_sum,
     head_sum,
     gain_sum,
     u_own,
-    grad_own,
-    out_rows,
 ):
     sums_ref, normed_ref, gate_ref, mixed_ref, merged_grad_ref, raw_ref, pre_ref, act_ref = token_refs
     step_ref, state_ref, state_next_ref, weight_ref, taps_ref, heads_ref, skip_ref, gain_ref = other_refs
@@ -436,7 +483,6 @@
     @pl.when(step_at == 0)
     def _():
         weight_sum[...] = jnp.zeros_like(weight_sum)
-        out_sum[...] = jnp.zeros_like(out_sum)
         tap_sum[...] = jnp.zeros_like(tap_sum)
         head_sum[...] = jnp.zeros_like(head_sum)
         gain_sum[...] = jnp.zeros_like(gain_sum)
@@ -447,14 +493,7 @@
         ahead[SPAN:, :] = jnp.zeros((8, mixed_width), F32)
 
     pick_piece(ids, at, own_chunks, u_refs, u_own)
-    pick_piece(ids, at, own_chunks, grad_refs, grad_own)
-    sums = sum(ref[...] for ref in sums_ref)
-    scale_row = lax.rsqrt(sums[0:1, :] / INNER + EPSILON)
-    cross_row = scale_row * scale_row * scale_row * (sums[1:2, :] / INNER)
-    row_ids = lax.broadcasted_iota(jnp.int32, (LANES, SPAN), 0)
-    columns = jnp.transpose(jnp.where(row_ids == 0, scale_row, cross_row))
-    gate_scale = columns[:, 0:1]
-    cross = columns[:, 1:2]
+    gate_scale, cross = scale_columns(sums_ref[...])
 
     gate = gate_ref[...]
     gate_s = sigmoid(gate)
@@ -465,10 +504,6 @@
     gain = skip_ref[1:2, :]
     scaled = gated * gate_scale
     tap_sum[5:6, :width] += jnp.sum(merged_grad * scaled, axis=0, keepdims=True)
-    merged = (scaled * gain).astype(BF)
-    upstream = grad_own[...]
-    upstream = jnp.where(rows_live(ids, at, lengths), upstream, jnp.zeros_like(upstream))
-    out_sum[...] += dot(merged, upstream, 0, 0)
     gated_grad = gate_scale * (merged_grad * gain) - gated * cross
     mixed_grad = gated_grad * gate_act
     gate_grad = gated_grad * mixed * (gate_s * (1.0 + gate * (1.0 - gate_s)))
@@ -631,7 +666,7 @@
         [gate_grad.astype(BF), raw_grad.astype(BF), step_in_grad.astype(BF)], axis=1
     )
     normed = normed_ref[...]
-    weight_sum[...] += dot(normed, low, 0, 0)
+    weight_sum[...] += dot(normed, low[:, width:], 0, 0)
     part = dot(low, weight_ref[...], 1, 1)
     store_part(ids, at, own_chunks, part_refs, part.astype(BF))
     inputs = u_own[...].astype(F32)
@@ -644,8 +679,6 @@
         model = weight_sum.shape[0]
         first = first_kept_ref.shape[2]
         kept_count = first_kept_ref.shape[0]
-        out_rows[...] = jnp.transpose(out_sum[...])
-        step_lanes = weight_sum.shape[1] - first
         for place, mask in enumerate(masks):
             first_ref = first_kept_ref if place < kept_count else first_sent_ref
             position = place if place < kept_count else place - kept_count
@@ -658,14 +691,16 @@
                 [conv_part[: CONV + 1], gain_part[0:1], head_sum[0:2, :]], axis=0
             )
             small = jnp.concatenate([tap_sum[:, :width], mixed_part], axis=1)
-            both = jnp.concatenate(halves(small), axis=1)
+            both = jnp.concatenate(halves(small), axis=0)
             picked = pl.ds(pl.multiple_of(block * rows, 8), rows)
-            first_ref[position, 0:SMALL, :] = both
+            first_ref[position, 0:SMALL, : both.shape[1]] = both
+            first_ref[position, 0:SMALL, both.shape[1] :] = jnp.zeros(
+                (SMALL, first - both.shape[1]), BF
+            )
             first_ref[position, SMALL:, :] = weight_sum[picked, :first].astype(BF)
             second_ref = second_refs[place % kept_count]
             near = place // kept_count
-            second_ref[near, :, :step_lanes] = weight_sum[picked, first:].astype(BF)
-            second_ref[near, :, step_lanes:] = out_rows[picked, :].astype(BF)
+            second_ref[near, :, :] = weight_sum[picked, first:].astype(BF)
 
 
 def pad_to(values, axis, size):
@@ -713,25 +748,25 @@
 
 
 def small_sum(rows):
-    half = rows.shape[1] // 2
-    return rows[:, :half] + rows[:, half:]
+    return rows[: SMALL // 2] + rows[SMALL // 2 :]
 
 
 def pack_kernel(width, tensor_count, ids, kept_ref, *refs):
     received = refs[:-1]
     packed_ref = refs[-1]
     maps_rows = packed_ref.shape[1] - 8
-    lanes = slice(2 * width, 2 * width + MAPS)
+    lanes = slice(width, width + MAPS)
     parts = [ref[...].astype(F32) for ref in [kept_ref, *received]]
     state = sum(part[SMALL:, lanes] for part in parts)
-    small = small_sum(sum(part[:SMALL] for part in parts))[:, width:]
+    small = small_sum(sum(part[:SMALL] for part in parts))[:, width : width + LANES]
     for at in range(tensor_count):
         packed_ref[at, 0:8, :LANES] = small
         packed_ref[at, 0:8, LANES:] = small
         packed_ref[at, 8:, :] = state[at * maps_rows : (at + 1) * maps_rows, :]
 
 
-def lamb_wide_kernel(width, channels, heads, copies, firsts, seconds, ids, *refs):
+def lamb_wide_kernel(width, channels, heads, copies, firsts, seconds, ids, early_ref, *refs):
+    early = jnp.sum(early_ref[...].astype(F32), axis=0)
     whole = sum(ref[...].astype(F32) for ref in refs[:firsts])
     rest = sum(ref[...].astype(F32) for ref in refs[firsts : firsts + seconds])
     count = firsts + seconds
@@ -741,9 +776,9 @@
     block = whole[SMALL:]
     small = small_sum(whole[:SMALL])
     norms = jnp.zeros((1, LANES), F32)
-    in_grad = jnp.stack([block[:, :channels], block[:, width : width + channels]], axis=1)
+    in_grad = jnp.stack([early[:, :channels], block[:, :channels]], axis=1)
     step_grad = jnp.transpose(rest[:, :LANES])[:heads]
-    out_grad = rest[:, LANES : LANES + channels]
+    out_grad = early[:, width : width + channels]
     channel_grad = small[: CONV + 2, :channels]
     picker = (
         lax.broadcasted_iota(jnp.int32, (width, LANES), 0) // HEAD
@@ -1070,15 +1105,41 @@
         exchange(branch_sent, "tensor", 1),
         *[exchange(sums_part, "tensor", mask) for mask in range(1, tensor_count)],
     )
-    sums = [sums_part] + sums
+    sums = sum(sums, sums_part)
     branch_out = branch_kept[1:].astype(F32) + branch_near[1:].astype(F32)
     branch_far = [
         exchange(branch_out[position].astype(BF), "tensor", 2 * position + 2)
         for position in range(tensor_count // 2 - 1)
     ]
+    (early,) = pl.pallas_call(
+        functools.partial(early_kernel, tensor_count, own_count // block_rows),
+        grid_spec=pltpu.PrefetchScalarGridSpec(
+            num_scalar_prefetch=2,
+            grid=(tokens // block_rows,),
+            in_specs=[
+                *piece_specs(span=block_rows),
+                pl.BlockSpec((2, block_rows), lambda at, *_: (0, at)),
+                token_spec(model, span=block_rows),
+                token_spec(width, span=block_rows),
+                token_spec(width, span=block_rows),
+                token_spec(width, span=block_rows),
+                whole_spec(skip_gain.shape),
+            ],
+            out_specs=[whole_spec((dp_count, rows, 2 * width))],
+            scratch_shapes=[
+                pltpu.VMEM((block_rows, model), BF),
+                pltpu.VMEM((width, model), F32),
+                pltpu.VMEM((width, model), F32),
+            ],
+        ),
+        out_shape=[struct((dp_count, rows, 2 * width), BF)],
+        compiler_params=arbitrary,
+        name="early_grads",
+    )(ids, lengths, *grad_pieces, sums, normed, gate_raw, mixed, merged_grad, skip_gain)
+    early = lax.all_to_all(early, "dp", 0, 0)
     masks = slot_masks(dp_count, dp_low)
-    first_columns = 2 * width + MAPS
-    second_columns = LANES + width
+    first_columns = mixed_width
+    second_columns = LANES
     kept_slots = dp_count // dp_low
     token_back = functools.partial(token_spec, reverse=True)
     normed_kept, normed_sent, first_kept, first_sent, *seconds_out = pl.pallas_call(
@@ -1088,8 +1149,7 @@
             grid=(chunks,),
             in_specs=[
                 *piece_specs(True),
-                *piece_specs(True),
-                *[pl.BlockSpec((2, SPAN), lambda at, *_: (0, chunks - 1 - at))] * tensor_count,
+                pl.BlockSpec((2, SPAN), lambda at, *_: (0, chunks - 1 - at)),
                 token_back(model),
                 token_back(width),
                 token_back(width),
@@ -1117,14 +1177,11 @@
             scratch_shapes=[
                 pltpu.VMEM((STATE, width), F32),
                 pltpu.VMEM((SPAN + 8, mixed_width), F32),
-                pltpu.VMEM((model, columns), F32),
-                pltpu.VMEM((width, model), F32),
+                pltpu.VMEM((model, columns - width), F32),
                 pltpu.VMEM((8, mixed_width), F32),
                 pltpu.VMEM((8, LANES), F32),
                 pltpu.VMEM((8, model), F32),
                 pltpu.VMEM((SPAN, model), BF),
-                pltpu.VMEM((SPAN, model), BF),
-                pltpu.VMEM((model, width), F32),
             ],
         ),
         out_shape=[
@@ -1139,8 +1196,7 @@
         ids,
         lengths,
         *u_pieces,
-        *grad_pieces,
-        *sums,
+        sums,
         normed,
         gate_raw,
         mixed,
@@ -1158,7 +1214,7 @@
         gain_rows,
     )
 
-    first_kept, first_sent, *branch_far = together(first_kept, first_sent, *branch_far)
+    first_kept, first_sent, early = together(first_kept, first_sent, early)
     highs_count = first_kept.shape[0]
     first_near = [
         exchange(
@@ -1181,12 +1237,9 @@
     for values in landed[1 : 1 + len(first_near)]:
         first_total = first_total + values.astype(F32)
     second_far = landed[1 + len(first_near) :]
-    middle = first_columns // 2
-    joined = first_total[:, :SMALL, :middle] + first_total[:, :SMALL, middle:]
+    joined = first_total[:, : SMALL // 2] + first_total[:, SMALL // 2 : SMALL]
     high = lax.reduce_precision(joined, 8, 7)
-    first_total = jnp.concatenate(
-        [jnp.concatenate([high, joined - high], axis=2), first_total[:, SMALL:]], axis=1
-    )
+    first_total = jnp.concatenate([high, joined - high, first_total[:, SMALL:]], axis=1)
     first_parts = [first_total[0]] + far_parts(first_total, "dp", dp_low)
     second_total = seconds_out[0].astype(F32)
     for values in second_far:
@@ -1210,7 +1263,7 @@
         axis=1,
     )
     live_own = (position_all % LMAX < length_of)[:, None]
-    own_squares = lax.dynamic_slice(sum(part[0] for part in sums), (tensor_at * own_count,), (own_count,))
+    own_squares = lax.dynamic_slice(sums[0], (tensor_at * own_count,), (own_count,))
     own_scale = lax.rsqrt(own_squares / INNER + EPSILON)[:, None]
     branch = branch_kept[0].astype(F32) + branch_near[0].astype(F32)
     for values in branch_far:
@@ -1266,7 +1319,7 @@
             len(first_parts),
             len(second_parts),
         ),
-        [*first_parts, *second_parts, *wide_of(masters), *wide_of(firsts), *wide_of(seconds)],
+        [early, *first_parts, *second_parts, *wide_of(masters), *wide_of(firsts), *wide_of(seconds)],
         wide_shapes * 4 + [struct((1, LANES))],
         "lamb_wide",
     )

time: 235 us -> 233 us (level)
  waiting for transfers between devices: 58.5 us -> 39.7 us
  starting transfers between devices: 43.6 us -> 52.7 us
  Pallas kernels: 94.9 us -> 101 us
  other arithmetic: 18.4 us -> 21.7 us
    ppermute x30, waiting for transfers between devices: 57.3 us -> 38.4 us  [exchange(): return lax.ppermute(values, axis, [(at, at ^ mask) for at in range(count)])]
    pallas_call x0 -> x1, Pallas kernels: none -> 11.5 us  [local(): pl.pallas_call(functools.partial(early_kernel, tensor_count, own_count //...]
    pallas_call x1, Pallas kernels: 45.9 us -> 40.1 us  [local(): pl.pallas_call(functools.partial(backward_kernel, width, masks, tensor_co...]
    all_to_all x0 -> x1, starting transfers between devices: none -> 3.74 us  [local(): early = lax.all_to_all(early, 'dp', 0, 0)]
    ppermute x30, starting transfers between devices: 33.1 us -> 36.6 us  [exchange(): return lax.ppermute(values, axis, [(at, at ^ mask) for at in range(count)])]
    unnamed x72 -> x62, local copies, waits for them, and re-layouts: 8.61 us -> 7.39 us
  transfers between devices with their start and end apart: 33 -> 34, of which waited for: 13 -> 13; matrix products, arithmetic and copies ran while one was open for 10% -> 12% of each run, Pallas kernels for 35% -> 33%
where the time goes in v5:
time: 233 us; the launch traced here: 232 us
  Pallas kernels  101 us (43%)
  starting transfers between devices  52.7 us (23%)
  waiting for transfers between devices  39.7 us (17%)
  other arithmetic  21.7 us (9%)
  local copies, waits for them, and re-layouts  15.2 us (7%)
    pallas_call x1, Pallas kernels, local(): pl.pallas_call(functools.partial(backward_kernel, width, masks, tensor_co...  40.1 us
    ppermute x30, waiting for transfers between devices, exchange(): return lax.ppermute(values, axis, [(at, at ^ mask) for at in range(count)])  38.4 us
    ppermute x30, starting transfers between devices, exchange(): return lax.ppermute(values, axis, [(at, at ^ mask) for at in range(count)])  36.6 us
    pallas_call x1, Pallas kernels, local(): pl.pallas_call(functools.partial(forward_kernel, width, len(in_pieces), p...  26.2 us
    pallas_call x4, Pallas kernels, whole_call(): pl.pallas_call(kernel, grid_spec=pltpu.PrefetchScalarGridSpec(num_scalar_...  13 us
    pallas_call x1, Pallas kernels, local(): pl.pallas_call(functools.partial(early_kernel, tensor_count, own_count //...  11.5 us
    pallas_call x1, Pallas kernels, local(): pl.pallas_call(functools.partial(middle_kernel, tensor_count, len(out_pie...  9.76 us
    unnamed x62, local copies, waits for them, and re-layouts  7.39 us
  transfers between devices with their start and end apart: 34, of which 13 were waited for; matrix products, arithmetic and copies ran while one was open for 12% of the time, Pallas kernels for 33%

profile of v5, /device:TPU:0, one launch (start us, length us, event | category | flops | bytes accessed | tf_op | source)
XLA Modules:
  0.0 231.7 jit_solution(100717599512695207)
XLA Ops:
  0.7 3.0 %collective-permute-start = (bf16[512,768]{1,0:T(8,128)(2,1)}, bf16[512,768]{1,0:T(8,128)(2,1)S(1)}, u32[]{:S(2)}, u32[]{:S(2)}) collective-permute-start(bf16[512,768]{1,0:T(8,128)(2,1)} %refs_0_.5), channel_id=1, source_target_pairs={{0,2},{1,3},{2,0},{3,1},{4,6},{5,7},{6,4},{7,5},{8,10},{9,11},{10,... | collective-permute-start | bytes 2359304 | tf_op jit(solution)/shard_map/ppermute | solution.py:45
  7.2 2.6 %collective-permute-start.2 = (bf16[96,896]{1,0:T(8,128)(2,1)S(1)}, bf16[96,896]{1,0:T(8,128)(2,1)S(1)}, u32[]{:S(2)}, u32[]{:S(2)}) collective-permute-start(bf16[96,896]{1,0:T(8,128)(2,1)S(1)} %fusion.12.refs_4_), channel_id=1, source_target_pairs={{0,16},{4,20},{8,24},{12,28},{16,0},{20,4},{24,8},{28,12},{1,17},{... | collective-permute-start | bytes 516104 | tf_op jit(solution)/shard_map/ppermute | solution.py:45
  14.0 8.9 %collective-permute-done.2.refs_7_ = bf16[96,896]{1,0:T(8,128)(2,1)S(1)} collective-permute-done((bf16[96,896]{1,0:T(8,128)(2,1)S(1)}, bf16[96,896]{1,0:T(8,128)(2,1)S(1)}, u32[]{:S(2)}, u32[]{:S(2)}) %collective-permute-start.2) | collective-permute-done | bytes 172064 | tf_op jit(solution)/shard_map/ppermute | solution.py:45
  25.3 4.9 %all-to-all-start = ((bf16[32,25,256]{2,1,0:T(8,128)(2,1)}), bf16[32,25,256]{2,1,0:T(8,128)(2,1)}, u32[]{:S(2)}, u32[]{:S(2)}) async-start(bf16[32,25,256]{2,1,0:T(8,128)(2,1)} %broadcast_in_dim.52), calls=%async_computation | async-start | bytes 1048576 | tf_op jit(solution)/shard_map/all_to_all | solution.py:910
  35.1 3.3 %collective-permute-start.10 = (bf16[96,384]{1,0:T(8,128)(2,1)}, bf16[96,384]{1,0:T(8,128)(2,1)S(1)}, u32[]{:S(2)}, u32[]{:S(2)}) collective-permute-start(bf16[96,384]{1,0:T(8,128)(2,1)} %convert_element_type.144.refs_4_), channel_id=1, source_target_pairs={{0,24},{4,28},{8,16},{12,20},{16,8},{20,12},{24,0},{28,4},{1,25},{... | collective-permute-start | bytes 221192 | tf_op jit(solution)/shard_map/ppermute | solution.py:45
  40.1 5.2 %collective-permute-done.10.refs_7_ = bf16[96,384]{1,0:T(8,128)(2,1)S(1)} collective-permute-done((bf16[96,384]{1,0:T(8,128)(2,1)}, bf16[96,384]{1,0:T(8,128)(2,1)S(1)}, u32[]{:S(2)}, u32[]{:S(2)}) %collective-permute-start.10) | collective-permute-done | bytes 73760 | tf_op jit(solution)/shard_map/ppermute | solution.py:45
  45.4 6.0 %collective-permute-done.9.refs_6_ = bf16[96,384]{1,0:T(8,128)(2,1)S(1)} collective-permute-done((bf16[96,384]{1,0:T(8,128)(2,1)}, bf16[96,384]{1,0:T(8,128)(2,1)S(1)}, u32[]{:S(2)}, u32[]{:S(2)}) %collective-permute-start.9) | collective-permute-done | bytes 73760 | tf_op jit(solution)/shard_map/ppermute | solution.py:45
  61.5 26.2 %ssd_forward.1 = (bf16[2048,768]{1,0:T(8,128)(2,1)}, f32[2048,384]{1,0:T(8,128)}, f32[2048,640]{1,0:T(8,128)}, f32[2048,640]{1,0:T(8,128)}, bf16[2048,640]{1,0:T...) custom-call(s32[2]{0:T(128)} %pad_add_fusion.ids, ...), custom_call_target="tpu_custom_call" | custom-call | tf_op jit(solution)/shard_map/ssd_forward/pallas_call | solution.py:1016
  91.2 9.8 %gate_middle.1 = (f32[2048,384]{1,0:T(8,128)}, bf16[2,512,768]{2,1,0:T(8,128)(2,1)}, bf16[2,512,768]{2,1,0:T(8,128)(2,1)}, f32[2,2048]{1,0:T(2,128)}) custom-call(s32[2]{0:T(128)} %pad_add_fusion.ids, s32[1]{0:T(128)} %copy.80.lengths, bf16[512,768]{1,0:T(8,128)(2,1)} %refs_0_.6, bf16[512,768]{1,0:T(8,128)(2,1)} %copy-done.7, ...), custom_call_target="tpu_custom_call" | custom-call | tf_op jit(solution)/shard_map/gate_middle/pallas_call | solution.py:1074
  107.0 11.5 %early_grads.1 = bf16[8,96,768]{2,1,0:T(8,128)(2,1)} custom-call(s32[2]{0:T(128)} %pad_add_fusion.ids, s32[1]{0:T(128)} %copy.80.lengths, bf16[512,768]{1,0:T(8,128)(2,1)} %refs_0_.6, bf16[512,768]{1,0:T(8,128)(2,1)} %copy-done.7, bf16[512,768]{1,0:T(8,128)(2,1)} %collective-permute-done.12.refs_2_, bf16[512,768]{1,0:T(8,128)(2,1)} %copy-done.8, ...), custom_call_target="tpu_custom_call" | custom-call | tf_op jit(solution)/shard_map/early_grads/pallas_call | solution.py:1114
  118.5 3.7 %all-to-all-start.1 = ((bf16[8,96,768]{2,1,0:T(8,128)(2,1)}), bf16[8,96,768]{2,1,0:T(8,128)(2,1)S(1)}, u32[]{:S(2)}, u32[]{:S(2)}) async-start(bf16[8,96,768]{2,1,0:T(8,128)(2,1)} %early_grads.1), calls=%async_computation.1 | async-start | bytes 2359296 | tf_op jit(solution)/shard_map/all_to_all | solution.py:1139
  122.3 40.1 %ssd_backward.1 = (bf16[2,512,768]{2,1,0:T(8,128)(2,1)}, bf16[2,512,768]{2,1,0:T(8,128)(2,1)}, bf16[4,112,640]{2,1,0:T(8,128)(2,1)}, bf16[4,112,640]{2,1,0:T(8,1...) custom-call(s32[2]{0:T(128)} %pad_add_fusion.ids, ...), custom_call_target="tpu_custom_call" | custom-call | tf_op jit(solution)/shard_map/ssd_backward/pallas_call | solution.py:1145
  165.9 2.4 %collective-permute-start.22 = (bf16[2,96,128]{2,1,0:T(8,128)(2,1)}, bf16[2,96,128]{2,1,0:T(8,128)(2,1)S(1)}, u32[]{:S(2)}, u32[]{:S(2)}) collective-permute-start(bf16[2,96,128]{2,1,0:T(8,128)(2,1)} %get-tuple-element.189), channel_id=1, source_target_pairs={{0,16},{4,20},{8,24},{12,28},{16,0},{20,4},{24,8},{28,12},{1,17},{... | collective-permute-start | bytes 147464 | tf_op jit(solution)/shard_map/ppermute | solution.py:45
  168.8 2.2 fusion.9
  174.4 3.8 %collective-permute-done.20 = bf16[4,112,640]{2,1,0:T(8,128)(2,1)} collective-permute-done((bf16[4,112,640]{2,1,0:T(8,128)(2,1)}, bf16[4,112,640]{2,1,0:T(8,128)(2,1)}, u32[]{:S(2)}, u32[]{:S(2)}) %collective-permute-start.20) | collective-permute-done | bytes 573472 | tf_op jit(solution)/shard_map/ppermute | solution.py:45
  188.4 2.4 %collective-permute-start.25 = (bf16[112,640]{1,0:T(8,128)(2,1)S(1)}, bf16[112,640]{1,0:T(8,128)(2,1)S(1)}, u32[]{:S(2)}, u32[]{:S(2)}) collective-permute-start(bf16[112,640]{1,0:T(8,128)(2,1)S(1)} %get-tuple-element.260), channel_id=1, source_target_pairs={{0,16},{4,20},{8,24},{12,28},{16,0},{20,4},{24,8},{28,12},{1,17},{... | collective-permute-start | bytes 430088 | tf_op jit(solution)/shard_map/ppermute | solution.py:45
  193.7 7.7 %collective-permute-done.25.refs_1_.refs_2_ = bf16[112,640]{1,0:T(8,128)(2,1)S(1)} collective-permute-done((bf16[112,640]{1,0:T(8,128)(2,1)S(1)}, bf16[112,640]{1,0:T(8,128)(2,1)S(1)}, u32[]{:S(2)}, u32[]{:S(2)}) %collective-permute-start.25) | collective-permute-done | bytes 143392 | tf_op jit(solution)/shard_map/ppermute | solution.py:45
  202.8 2.5 %pack_maps.1 = f32[4,32,256]{2,1,0:T(8,128)} custom-call(s32[2]{0:T(128)} %pad_add_fusion.ids, f32[112,640]{1,0:T(8,128)} %slice_bitcast_fusion.1.kept_ref.refs_0_, bf16[112,640]{1,0:T(8,128)(2,1)} %copy-done.17, bf16[112,640]{1,0:T(8,128)(2,1)} %copy-done.18, bf16[112,640]{1,0:T(8,128)(2,1)} %copy-done.19), custom_call_target="tpu_custom_call" | custom-call | tf_op jit(solution)/shard_map/pack_maps/pallas_call | solution.py:1288
  205.3 3.3 %all-to-all-start.2 = ((f32[4,32,256]{2,1,0:T(8,128)}), f32[4,32,256]{2,1,0:T(8,128)S(1)}, u32[]{:S(2)}, u32[]{:S(2)}) async-start(f32[4,32,256]{2,1,0:T(8,128)} %pack_maps.1), calls=%async_computation.2 | async-start | bytes 262144 | tf_op jit(solution)/shard_map/all_to_all | solution.py:1307
  208.7 5.3 %lamb_wide.1 = (f32[96,2,384]{2,1,0:T(2,128)}, f32[6,96]{1,0:T(8,128)}, f32[96,384]{1,0:T(8,128)}, f32[6,384]{1,0:T(8,128)}, f32[3,6]{1,0:T(4,128)}, /*index=5*/...) custom-call(s32[2]{0:T(128)} %pad_add_fusion.ids, ...), custom_call_target="tpu_custom_call" | custom-call | tf_op jit(solution)/shard_map/lamb_wide/pallas_call | solution.py:1288
  214.6 2.5 %lamb_maps.1 = (f32[24,256]{1,0:T(8,128)}, f32[8,5]{1,0:T(8,128)}, f32[1,24]{1,0:T(1,128)}, f32[24,256]{1,0:T(8,128)}, f32[8,5]{1,0:T(8,128)}, /*index=5*/f32[1,...) custom-call(s32[2]{0:T(128)} %pad_add_fusion.ids, ...), custom_call_target="tpu_custom_call" | custom-call | tf_op jit(solution)/shard_map/lamb_maps/pallas_call | solution.py:1288
  217.1 4.1 %all-to-all-start.3 = ((f32[32,1,128]{2,1,0:T(1,128)}), f32[32,1,128]{2,1,0:T(1,128)S(1)}, u32[]{:S(2)}, u32[]{:S(2)}) async-start(f32[32,1,128]{2,1,0:T(1,128)} %get-tuple-element.204), calls=%async_computation.3 | async-start | bytes 32768 | tf_op jit(solution)/shard_map/all_to_all | solution.py:1337
  223.6 3.5 %fusion.4 = (bf16[512,768]{1,0:T(8,128)(2,1)}, f32[512,768]{1,0:T(8,128)}) fusion(bf16[512,768]{1,0:T(8,128)(2,1)S(1)} %copy-done, bf16[512,768]{1,0:T(8,128)(2,1)} %collective-permute-done.29, f32[512]{0:T(512)S(1)} %bitcast.85, bf16[2,512,768]{2,1,0:T(8,128)(2,1)} %collective-permute-done.15, bf16[2,512,768]{2,1,0:T(8,128)(2,1)S(1)} %copy-done.10, ...), kind=kLoop, calls=%fused_computation.9 | loop fusion | flops 7471104 | bytes 8662528 | tf_op jit(solution)/shard_map/convert_element_type | solution.py:1271
  228.9 2.7 %lamb_update.1 = (f32[96,2,384]{2,1,0:T(2,128)}, f32[6,96]{1,0:T(8,128)}, f32[96,384]{1,0:T(8,128)}, f32[6,384]{1,0:T(8,128)}, f32[3,6]{1,0:T(4,128)}, /*index=5...) custom-call(s32[2]{0:T(128)} %pad_add_fusion.ids, f32[32,1,128]{2,1,0:T(1,128)} %copy-done.25, ...), custom_call_target="tpu_custom_call" | custom-call | tf_op jit(solution)/shard_map/lamb_update/pallas_call | solution.py:1288
  (168 shorter events, 62.2 us)
Async XLA Ops:
  0.7 22.2 %collective-permute-start = (bf16[512,768]{1,0:T(8,128)(2,1)}, bf16[512,768]{1,0:T(8,128)(2,1)S(1)}, u32[]{:S(2)}, u32[]{:S(2)}) collective-permute-start(bf16[512,768]{1,0:T(8,128)(2,1)} %refs_0_.5), channel_id=1, source_target_pairs={{0,2},{1,3},{2,0},{3,1},{4,6},{5,7},{6,4},{7,5},{8,10},{9,11},{10,... | collective-permute-start | bytes 2359304 | tf_op jit(solution)/shard_map/ppermute | solution.py:45
  5.6 8.4 %collective-permute-start.1 = (bf16[96,896]{1,0:T(8,128)(2,1)S(1)}, bf16[96,896]{1,0:T(8,128)(2,1)S(1)}, u32[]{:S(2)}, u32[]{:S(2)}) collective-permute-start(bf16[96,896]{1,0:T(8,128)(2,1)S(1)} %fusion.12.refs_4_), channel_id=1, source_target_pairs={{0,8},{4,12},{8,0},{12,4},{16,24},{20,28},{24,16},{28,20},{1,9},{5... | collective-permute-start | bytes 516104 | tf_op jit(solution)/shard_map/ppermute | solution.py:45
  7.2 15.6 %collective-permute-start.2 = (bf16[96,896]{1,0:T(8,128)(2,1)S(1)}, bf16[96,896]{1,0:T(8,128)(2,1)S(1)}, u32[]{:S(2)}, u32[]{:S(2)}) collective-permute-start(bf16[96,896]{1,0:T(8,128)(2,1)S(1)} %fusion.12.refs_4_), channel_id=1, source_target_pairs={{0,16},{4,20},{8,24},{12,28},{16,0},{20,4},{24,8},{28,12},{1,17},{... | collective-permute-start | bytes 516104 | tf_op jit(solution)/shard_map/ppermute | solution.py:45
  9.8 13.0 %collective-permute-start.3 = (bf16[96,896]{1,0:T(8,128)(2,1)S(1)}, bf16[96,896]{1,0:T(8,128)(2,1)S(1)}, u32[]{:S(2)}, u32[]{:S(2)}) collective-permute-start(bf16[96,896]{1,0:T(8,128)(2,1)S(1)} %fusion.12.refs_4_), channel_id=1, source_target_pairs={{0,24},{4,28},{8,16},{12,20},{16,8},{20,12},{24,0},{28,4},{1,25},{... | collective-permute-start | bytes 516104 | tf_op jit(solution)/shard_map/ppermute | solution.py:45
  10.0 12.8 %collective-permute-start.4 = (bf16[96,896]{1,0:T(8,128)(2,1)S(1)}, bf16[96,896]{1,0:T(8,128)(2,1)S(1)}, u32[]{:S(2)}, u32[]{:S(2)}) collective-permute-start(bf16[96,896]{1,0:T(8,128)(2,1)S(1)} %fusion.12.refs_4_), channel_id=1, source_target_pairs={{0,4},{4,0},{8,12},{12,8},{16,20},{20,16},{24,28},{28,24},{1,5},{5... | collective-permute-start | bytes 516104 | tf_op jit(solution)/shard_map/ppermute | solution.py:45
  14.0 24.4 %collective-permute-start.5 = (bf16[512,768]{1,0:T(8,128)(2,1)}, bf16[512,768]{1,0:T(8,128)(2,1)S(1)}, u32[]{:S(2)}, u32[]{:S(2)}) collective-permute-start(bf16[512,768]{1,0:T(8,128)(2,1)} %refs_0_.5), channel_id=1, source_target_pairs={{0,1},{1,0},{2,3},{3,2},{4,5},{5,4},{6,7},{7,6},{8,9},{9,8},{10,11... | collective-permute-start | bytes 2359304 | tf_op jit(solution)/shard_map/ppermute | solution.py:45
  25.3 26.8 %all-to-all-start = ((bf16[32,25,256]{2,1,0:T(8,128)(2,1)}), bf16[32,25,256]{2,1,0:T(8,128)(2,1)}, u32[]{:S(2)}, u32[]{:S(2)}) async-start(bf16[32,25,256]{2,1,0:T(8,128)(2,1)} %broadcast_in_dim.52), calls=%async_computation | async-start | bytes 1048576 | tf_op jit(solution)/shard_map/all_to_all | solution.py:910
  30.2 21.8 %collective-permute-start.6 = (bf16[512,768]{1,0:T(8,128)(2,1)S(1)}, bf16[512,768]{1,0:T(8,128)(2,1)S(1)}, u32[]{:S(2)}, u32[]{:S(2)}) collective-permute-start(bf16[512,768]{1,0:T(8,128)(2,1)S(1)} %collective-permute-done.refs_2_), channel_id=1, source_target_pairs={{0,1},{1,0},{2,3},{3,2},{4,5},{5,4},{6,7},{7,6},{8,9},{9,8},{10,11... | collective-permute-start | bytes 2359304 | tf_op jit(solution)/shard_map/ppermute | solution.py:45
  32.0 19.4 %collective-permute-start.7 = (bf16[3,96,896]{2,1,0:T(8,128)(2,1)}, bf16[3,96,896]{2,1,0:T(8,128)(2,1)}, u32[]{:S(2)}, u32[]{:S(2)}) collective-permute-start(bf16[3,96,896]{2,1,0:T(8,128)(2,1)} %pad_maximum_fusion.1), channel_id=1, source_target_pairs={{0,4},{4,0},{8,12},{12,8},{16,20},{20,16},{24,28},{28,24},{1,5},{5... | collective-permute-start | bytes 1548296 | tf_op jit(solution)/shard_map/ppermute | solution.py:45
  35.1 10.2 %collective-permute-start.10 = (bf16[96,384]{1,0:T(8,128)(2,1)}, bf16[96,384]{1,0:T(8,128)(2,1)S(1)}, u32[]{:S(2)}, u32[]{:S(2)}) collective-permute-start(bf16[96,384]{1,0:T(8,128)(2,1)} %convert_element_type.144.refs_4_), channel_id=1, source_target_pairs={{0,24},{4,28},{8,16},{12,20},{16,8},{20,12},{24,0},{28,4},{1,25},{... | collective-permute-start | bytes 221192 | tf_op jit(solution)/shard_map/ppermute | solution.py:45
  38.4 7.0 %collective-permute-start.8 = (bf16[96,384]{1,0:T(8,128)(2,1)}, bf16[96,384]{1,0:T(8,128)(2,1)S(1)}, u32[]{:S(2)}, u32[]{:S(2)}) collective-permute-start(bf16[96,384]{1,0:T(8,128)(2,1)} %convert_element_type.144.refs_4_), channel_id=1, source_target_pairs={{0,8},{4,12},{8,0},{12,4},{16,24},{20,28},{24,16},{28,20},{1,9},{5... | collective-permute-start | bytes 221192 | tf_op jit(solution)/shard_map/ppermute | solution.py:45
  38.4 13.0 %collective-permute-start.9 = (bf16[96,384]{1,0:T(8,128)(2,1)}, bf16[96,384]{1,0:T(8,128)(2,1)S(1)}, u32[]{:S(2)}, u32[]{:S(2)}) collective-permute-start(bf16[96,384]{1,0:T(8,128)(2,1)} %convert_element_type.144.refs_4_), channel_id=1, source_target_pairs={{0,16},{4,20},{8,24},{12,28},{16,0},{20,4},{24,8},{28,12},{1,17},{... | collective-permute-start | bytes 221192 | tf_op jit(solution)/shard_map/ppermute | solution.py:45
  54.1 33.6 %collective-permute-start.12 = (bf16[512,768]{1,0:T(8,128)(2,1)S(1)}, bf16[512,768]{1,0:T(8,128)(2,1)}, u32[]{:S(2)}, u32[]{:S(2)}) collective-permute-start(bf16[512,768]{1,0:T(8,128)(2,1)S(1)} %copy-done.1), channel_id=1, source_target_pairs={{0,2},{1,3},{2,0},{3,1},{4,6},{5,7},{6,4},{7,5},{8,10},{9,11},{10,... | collective-permute-start | bytes 2359304 | tf_op jit(solution)/shard_map/ppermute | solution.py:45
  55.7 33.2 %collective-permute-start.11 = (bf16[512,768]{1,0:T(8,128)(2,1)S(1)}, bf16[512,768]{1,0:T(8,128)(2,1)S(1)}, u32[]{:S(2)}, u32[]{:S(2)}) collective-permute-start(bf16[512,768]{1,0:T(8,128)(2,1)S(1)} %copy-done.1), channel_id=1, source_target_pairs={{0,1},{1,0},{2,3},{3,2},{4,5},{5,4},{6,7},{7,6},{8,9},{9,8},{10,11... | collective-permute-start | bytes 2359304 | tf_op jit(solution)/shard_map/ppermute | solution.py:45
  58.6 29.1 %collective-permute-start.13 = (bf16[4,96,384]{2,1,0:T(8,128)(2,1)}, bf16[4,96,384]{2,1,0:T(8,128)(2,1)}, u32[]{:S(2)}, u32[]{:S(2)}) collective-permute-start(bf16[4,96,384]{2,1,0:T(8,128)(2,1)} %pad_maximum_fusion.2), channel_id=1, source_target_pairs={{0,4},{4,0},{8,12},{12,8},{16,20},{20,16},{24,28},{28,24},{1,5},{5... | collective-permute-start | bytes 884744 | tf_op jit(solution)/shard_map/ppermute | solution.py:45
  118.5 44.1 %all-to-all-start.1 = ((bf16[8,96,768]{2,1,0:T(8,128)(2,1)}), bf16[8,96,768]{2,1,0:T(8,128)(2,1)S(1)}, u32[]{:S(2)}, u32[]{:S(2)}) async-start(bf16[8,96,768]{2,1,0:T(8,128)(2,1)} %early_grads.1), calls=%async_computation.1 | async-start | bytes 2359296 | tf_op jit(solution)/shard_map/all_to_all | solution.py:1139
  162.4 12.0 %collective-permute-start.19 = (bf16[2,512,768]{2,1,0:T(8,128)(2,1)}, bf16[2,512,768]{2,1,0:T(8,128)(2,1)}, u32[]{:S(2)}, u32[]{:S(2)}) collective-permute-start(bf16[2,512,768]{2,1,0:T(8,128)(2,1)} %get-tuple-element.186), channel_id=1, source_target_pairs={{0,1},{1,0},{2,3},{3,2},{4,5},{5,4},{6,7},{7,6},{8,9},{9,8},{10,11... | collective-permute-start | bytes 4718600 | tf_op jit(solution)/shard_map/ppermute | solution.py:45
  162.6 15.6 %collective-permute-start.20 = (bf16[4,112,640]{2,1,0:T(8,128)(2,1)}, bf16[4,112,640]{2,1,0:T(8,128)(2,1)}, u32[]{:S(2)}, u32[]{:S(2)}) collective-permute-start(bf16[4,112,640]{2,1,0:T(8,128)(2,1)} %get-tuple-element.187), channel_id=1, source_target_pairs={{0,4},{4,0},{8,12},{12,8},{16,20},{20,16},{24,28},{28,24},{1,5},{5... | collective-permute-start | bytes 1720328 | tf_op jit(solution)/shard_map/ppermute | solution.py:45
  171.0 52.3 %collective-permute-start.29 = (bf16[512,768]{1,0:T(8,128)(2,1)}, bf16[512,768]{1,0:T(8,128)(2,1)}, u32[]{:S(2)}, u32[]{:S(2)}) collective-permute-start(bf16[512,768]{1,0:T(8,128)(2,1)} %fusion.9), channel_id=1, source_target_pairs={{0,2},{1,3},{2,0},{3,1},{4,6},{5,7},{6,4},{7,5},{8,10},{9,11},{10,... | collective-permute-start | bytes 2359304 | tf_op jit(solution)/shard_map/ppermute | solution.py:45
  183.6 37.7 %collective-permute-start.28 = (bf16[512,768]{1,0:T(8,128)(2,1)}, bf16[512,768]{1,0:T(8,128)(2,1)}, u32[]{:S(2)}, u32[]{:S(2)}) collective-permute-start(bf16[512,768]{1,0:T(8,128)(2,1)} %fusion.10), channel_id=1, source_target_pairs={{0,2},{1,3},{2,0},{3,1},{4,6},{5,7},{6,4},{7,5},{8,10},{9,11},{10,... | collective-permute-start | bytes 2359304 | tf_op jit(solution)/shard_map/ppermute | solution.py:45
  188.4 13.1 %collective-permute-start.25 = (bf16[112,640]{1,0:T(8,128)(2,1)S(1)}, bf16[112,640]{1,0:T(8,128)(2,1)S(1)}, u32[]{:S(2)}, u32[]{:S(2)}) collective-permute-start(bf16[112,640]{1,0:T(8,128)(2,1)S(1)} %get-tuple-element.260), channel_id=1, source_target_pairs={{0,16},{4,20},{8,24},{12,28},{16,0},{20,4},{24,8},{28,12},{1,17},{... | collective-permute-start | bytes 430088 | tf_op jit(solution)/shard_map/ppermute | solution.py:45
  191.6 9.9 %collective-permute-start.26 = (bf16[112,640]{1,0:T(8,128)(2,1)S(1)}, bf16[112,640]{1,0:T(8,128)(2,1)S(1)}, u32[]{:S(2)}, u32[]{:S(2)}) collective-permute-start(bf16[112,640]{1,0:T(8,128)(2,1)S(1)} %get-tuple-element.259), channel_id=1, source_target_pairs={{0,24},{4,28},{8,16},{12,20},{16,8},{20,12},{24,0},{28,4},{1,25},{... | collective-permute-start | bytes 430088 | tf_op jit(solution)/shard_map/ppermute | solution.py:45
  205.3 8.6 %all-to-all-start.2 = ((f32[4,32,256]{2,1,0:T(8,128)}), f32[4,32,256]{2,1,0:T(8,128)S(1)}, u32[]{:S(2)}, u32[]{:S(2)}) async-start(f32[4,32,256]{2,1,0:T(8,128)} %pack_maps.1), calls=%async_computation.2 | async-start | bytes 262144 | tf_op jit(solution)/shard_map/all_to_all | solution.py:1307
  217.1 11.2 %all-to-all-start.3 = ((f32[32,1,128]{2,1,0:T(1,128)}), f32[32,1,128]{2,1,0:T(1,128)S(1)}, u32[]{:S(2)}, u32[]{:S(2)}) async-start(f32[32,1,128]{2,1,0:T(1,128)} %get-tuple-element.204), calls=%async_computation.3 | async-start | bytes 32768 | tf_op jit(solution)/shard_map/all_to_all | solution.py:1337
  (41 other events, 445.9 us)
